TPU v7x, 256 devices: a whole 4x4x8 slice. The times are simulated.
256 devices in a mesh: req: 32 (over z, x), tp: 8 (over y, core).
Axes of the slice: x: 4, y: 4, z: 8, core: 2. Of those that a mesh axis runs over, the one named last changes fastest.
Arguments:
- hidden_in: bfloat16 [32768, 2048], P('req'), may hold values from -6 to 6
- qkv_weight: bfloat16 [2048, 3, 2048], P(None, None, 'tp'), may hold values from -0.125 to 0.125
- out_weight: bfloat16 [2048, 2048], P('tp'), may hold values from -1.5 to 1.5
- kv_pool: bfloat16 [512, 2, 128, 2048], P('req', None, None, 'tp'), may hold values from -48 to 48
- cached_len: int32 [32], replicated, may hold values from 3585 to 4096, as said below
- page_slot: int32 [32, 32], replicated, may hold values from 0 to 15
- page_holder: int32 [32, 32, 1], replicated, may hold values from 0 to 31; in each aligned block of 32 rows (0 to 31, 32 to 63, ..., all dimensions but the last counted through in order) at most 2 rows name the same one
- cont_flag: int32 [32], replicated, may hold values 0 or 1
Outputs:
- attn_out: bfloat16 [32768, 2048], P(('req', 'tp'))
Inputs may be any that keep to these rules, and one draw needn't show every extreme that they name: `page_holder`: within the table entries of the requests of one index of req (aligned blocks of 1 request), no holder is named more than 2 times. `cached_len`: A cached length of 4096 occurs in every draw. `page_slot`: page slot k of holder h is row h * 16 + k of kv_pool.
All inputs are finite; a program needn't handle non-finite values.
Results may differ from a plain program's by a relative error of at most 0.02.
Values may be sent and summed in bfloat16 or wider, within the bound.
A program may use at most 128 MiB of HBM per device.

v0:
```python
import jax
import jax.numpy as jnp
from jax import lax
from jax.sharding import PartitionSpec as P

HD = 128
NEW = 1024
PAGE = 128
MAXP = 32


def rotate(feature, position):
    half_width = feature.shape[-1] // 2
    indices = jnp.arange(half_width).astype(jnp.float32)
    inverse = jnp.exp(indices * (-2.0 / feature.shape[-1]) * jnp.log(jnp.float32(10000.0)))
    angles = position[:, None, None] * inverse[None, None, :]
    cosine = jnp.cos(angles)
    sine_part = jnp.sin(angles)
    first_half = feature[..., :half_width]
    second_half = feature[..., half_width:]
    return jnp.concatenate(
        [
            first_half * cosine - second_half * sine_part,
            second_half * cosine + first_half * sine_part,
        ],
        axis=-1,
    )


def attend_block(query_part, keys_part, values_part, allowed):
    scores = jnp.einsum(
        "qd,kd->qk", query_part, keys_part, preferred_element_type=jnp.float32
    ) * HD ** (-0.5)
    scores = jnp.where(allowed, scores, -1e30)
    row_top = jnp.max(scores, axis=-1)
    weights = jnp.where(allowed, jnp.exp(scores - row_top[:, None]), 0.0)
    row_total = jnp.sum(weights, axis=-1)
    summed = jnp.einsum(
        "qk,kd->qd", weights.astype(jnp.bfloat16), values_part, preferred_element_type=jnp.float32
    )
    return (summed, row_top, row_total)


def body(hidden_in, qkv_weight, out_weight, kv_pool, cached_len, page_slot, page_holder, cont_flag):
    req_count = lax.axis_size("req")
    tp_count = lax.axis_size("tp")
    req_index = lax.axis_index("req")
    local_reqs = hidden_in.shape[0] // NEW
    local_width = qkv_weight.shape[2]
    local_heads = local_width // HD
    table_block = local_reqs * MAXP
    capacity = max(2, 2 * table_block // req_count)
    cache_span = MAXP * PAGE
    holder_rows = page_holder[:, :, 0]
    held_here = holder_rows == req_index
    ranking = jnp.cumsum(held_here.astype(jnp.int32), axis=1) - 1
    picked = held_here[:, :, None] & (ranking[:, :, None] == jnp.arange(capacity)[None, None, :])
    send_slots = jnp.sum(jnp.where(picked, page_slot[:, :, None], 0), axis=1)
    outgoing = kv_pool[send_slots]
    lengths = lax.dynamic_slice_in_dim(cached_len, req_index * local_reqs, local_reqs)
    flags = lax.dynamic_slice_in_dim(cont_flag, req_index * local_reqs, local_reqs)
    live_len = lengths * flags
    token_rows = hidden_in.astype(jnp.float32)
    centre = jnp.mean(token_rows, axis=-1, keepdims=True)
    centred = token_rows - centre
    spread = jnp.mean(centred * centred, axis=-1, keepdims=True)
    normed = (centred * lax.rsqrt(spread + 1e-05)).astype(jnp.bfloat16)
    united_qkv = jnp.einsum("td,dcf->tcf", normed, qkv_weight, preferred_element_type=jnp.float32)
    positions = (live_len[:, None] + jnp.arange(NEW)[None, :]).astype(jnp.float32).reshape(-1)
    query_rot = rotate(united_qkv[:, 0].reshape(-1, local_heads, HD), positions).astype(
        jnp.bfloat16
    )
    new_key = rotate(united_qkv[:, 1].reshape(-1, local_heads, HD), positions).astype(jnp.bfloat16)
    new_value = united_qkv[:, 2].reshape(-1, local_heads, HD).astype(jnp.bfloat16)
    row_count = local_reqs * NEW
    block_rows = min(512, NEW)
    req_blocks = NEW // block_rows
    row_blocks = row_count // block_rows
    work_items = local_heads * row_blocks
    query_heads = query_rot.transpose(1, 0, 2)
    new_places = jnp.arange(NEW)[None, :]

    def block_place(index):
        head = index // row_blocks
        block = index % row_blocks
        owner = block // req_blocks
        query_pos = block % req_blocks * block_rows + jnp.arange(block_rows)
        query_part = lax.dynamic_slice(
            query_heads, (head, block * block_rows, 0), (1, block_rows, HD)
        )[0]
        return (head, owner, query_pos, query_part)

    incoming = lax.all_to_all(outgoing, "req", split_axis=0, concat_axis=0, tiled=True)
    own_holders = lax.dynamic_index_in_dim(holder_rows, req_index, 0, keepdims=False)
    same_holder = own_holders[:, None] == own_holders[None, :]
    earlier = jnp.arange(table_block)[None, :] < jnp.arange(table_block)[:, None]
    own_rank = jnp.sum((same_holder & earlier).astype(jnp.int32), axis=1)
    fetched = incoming.reshape(req_count * capacity, 2, PAGE, local_width)[
        own_holders * capacity + own_rank
    ]
    fetched = fetched.reshape(local_reqs, MAXP, 2, PAGE, local_width)
    cache_key = fetched[:, :, 0].reshape(local_reqs, cache_span, local_heads, HD)
    cache_value = fetched[:, :, 1].reshape(local_reqs, cache_span, local_heads, HD)
    keys_all = jnp.concatenate(
        [cache_key, new_key.reshape(local_reqs, NEW, local_heads, HD)], axis=1
    )
    values_all = jnp.concatenate(
        [cache_value, new_value.reshape(local_reqs, NEW, local_heads, HD)], axis=1
    )

    def joined_block(index):
        head, owner, query_pos, query_part = block_place(index)
        keys_part = lax.dynamic_slice(
            keys_all, (owner, 0, head, 0), (1, cache_span + NEW, 1, HD)
        ).reshape(cache_span + NEW, HD)
        values_part = lax.dynamic_slice(
            values_all, (owner, 0, head, 0), (1, cache_span + NEW, 1, HD)
        ).reshape(cache_span + NEW, HD)
        live_one = lax.dynamic_index_in_dim(live_len, owner, 0, keepdims=False)
        cache_ok = jnp.broadcast_to(
            jnp.arange(cache_span)[None, :] < live_one, (block_rows, cache_span)
        )
        allowed = jnp.concatenate([cache_ok, new_places <= query_pos[:, None]], axis=1)
        summed, row_top, row_total = attend_block(query_part, keys_part, values_part, allowed)
        return (summed / row_total[:, None]).astype(jnp.bfloat16)

    blocks_out = lax.map(joined_block, jnp.arange(work_items))
    attended = (
        blocks_out.reshape(local_heads, row_count, HD)
        .transpose(1, 0, 2)
        .reshape(row_count, local_width)
    )
    share_rows = row_count // tp_count
    head_term = jnp.dot(attended, out_weight, preferred_element_type=jnp.float32)
    summed_rows = lax.psum(head_term.astype(jnp.bfloat16), "tp")
    result = lax.dynamic_slice_in_dim(summed_rows, lax.axis_index("tp") * share_rows, share_rows, 0)
    return result


def solution(mesh):
    in_specs = (
        P("req", None),
        P(None, None, "tp"),
        P("tp", None),
        P("req", None, None, "tp"),
        P(),
        P(),
        P(),
        P(),
    )
    out_specs = P(("req", "tp"), None)
    return jax.shard_map(body, mesh=mesh, in_specs=in_specs, out_specs=out_specs, check_vma=False)
```

profile of v0, /device:TPU:2, one launch (start us, length us, event | category | flops | bytes accessed | tf_op | source)
XLA Modules:
  0.0 384.3 jit_solution(15847027432307803292)
XLA Ops:
  8.7 7.0 %gather_fusion = bf16[64,2,128,256]{3,2,1,0:T(8,128)(2,1)} fusion(bf16[16,2,128,256]{3,2,1,0:T(8,128)(2,1)} %param.13, s32[1024]{0:T(1024)S(1)} %pad_clamp_fusion.1), kind=kCustom, calls=%fused_computation | custom fusion | bytes 16777472 | tf_op jit(solution)/shard_map/gather | solution.py:59
  15.7 11.8 %all-to-all-start = ((bf16[32,2,2,128,256]{4,3,2,1,0:T(8,128)(2,1)}), bf16[32,2,2,128,256]{4,3,2,1,0:T(8,128)(2,1)}, u32[]{:S(2)}, u32[]{:S(2)}) async-start(bf16[32,2,2,128,256]{4,3,2,1,0:T(8,128)(2,1)} %bitcast.83), calls=%async_computation | async-start | bytes 16777216 | tf_op jit(solution)/shard_map/all_to_all | solution.py:93
  28.9 2.8 convert_reduce_fusion
  32.9 4.0 %fusion.42 = f32[1024,3,256]{0,2,1:T(8,128)S(1)} fusion(bf16[2048,3,256]{2,0,1:T(8,128)(2,1)S(1)} %copy-done, bf16[1024,2048]{1,0:T(8,128)(2,1)S(1)} %copy-done.2, f32[1024]{0:T(1024)S(1)} %add_rsqrt_fusion, f32[1024]{0:T(1024)S(1)} %broadcast_multiply_fusion), kind=kOutput, calls=%fused_computation.34 | convolution fusion | flops 3229614080 | bytes 10493952 | tf_op jit(solution)/shard_map/td,dcf->tcf/dot_general | solution.py:68
  37.0 1.6 copy-done.5
  39.7 1.8 fusion.55
  45.4 2.4 copy.48
  50.6 1.9 multiply_cosine_fusion
  52.5 2.8 fusion.46
  56.4 160.8 %all-to-all-done = bf16[32,2,2,128,256]{4,3,2,1,0:T(8,128)(2,1)} async-done(((bf16[32,2,2,128,256]{4,3,2,1,0:T(8,128)(2,1)}), bf16[32,2,2,128,256]{4,3,2,1,0:T(8,128)(2,1)}, u32[]{:S(2)}, u32[]{:S(2)}) %all-to-all-start) | async-done | bytes 8388640 | tf_op jit(solution)/shard_map/all_to_all | solution.py:93
  217.2 6.1 %gather_fusion.1 = bf16[32,2,128,256]{3,2,1,0:T(8,128)(2,1)} fusion(bf16[64,2,128,256]{3,2,1,0:T(8,128)(2,1)} %bitcast.6, s32[1024]{0:T(1024)S(1)} %pad_clamp_fusion), kind=kCustom, calls=%fused_computation.1 | custom fusion | bytes 8388736 | tf_op jit(solution)/shard_map/gather | solution.py:98
  223.4 4.7 %fusion.54 = (bf16[1,32,1,128,256]{4,3,2,1,0:T(8,128)(2,1)}, bf16[1,32,1,128,256]{4,3,2,1,0:T(8,128)(2,1)}) fusion(bf16[1,32,2,128,256]{4,3,2,1,0:T(8,128)(2,1)} %bitcast.84), kind=kLoop, calls=%fused_computation.74 | loop fusion | bytes 8388608 | tf_op jit(solution)/shard_map/slice | solution.py:103
  228.0 2.5 reshape_squeeze.16
  232.2 2.5 reshape_squeeze.14
  236.7 2.3 maximum_maximum_fusion
  239.0 46.8 %while.13 = (s32[]{:T(128)}, bf16[4,512,128]{2,1,0:T(8,128)(2,1)}, s32[1]{0:T(128)}, s32[4]{0:T(128)S(1)}, bf16[2,1024,128]{2,1,0:T(8,128)(2,1)}, /*index=5*/bf1...) while((s32[]{:T(128)}, bf16[4,512,128]{2,1,0:T(8,128)(2,1)}, ...), condition=%wide.region_8.9_spmd.clone, body=%wide.region_5.8_spmd.clone.sunk | while | flops 1374293504 | bytes 46968904 | solution.py:127
  242.9 2.9 fusion.68
  245.8 2.5 fusion.69
  248.3 2.4 fusion.70
  254.6 2.9 fusion.68
  257.5 2.5 fusion.69
  260.0 2.4 fusion.70
  266.3 2.9 fusion.68
  269.2 2.5 fusion.69
  271.7 2.4 fusion.70
  278.0 2.9 fusion.68
  280.9 2.5 fusion.69
  283.4 2.4 fusion.70
  285.8 2.0 copy.45
  287.8 4.8 %convolution_convert_fusion = bf16[1024,2048]{1,0:T(8,128)(2,1)} fusion(bf16[1024,256]{0,1:T(8,128)(2,1)} %bitcast.87, bf16[256,2048]{1,0:T(8,128)(2,1)} %param.12), kind=kOutput, calls=%fused_computation.37 | convolution fusion | flops 1075838976 | bytes 5767168 | tf_op jit(solution)/shard_map/dot_general | solution.py:134
  292.6 83.0 %all-reduce.2.cloned.1.call-done = bf16[1024,2048]{1,0:T(8,128)(2,1)} async-done(((bf16[1024,2048]{1,0:T(8,128)(2,1)}), bf16[1024,2048]{1,0:T(8,128)(2,1)}) %all-reduce.2.cloned.1.call-update) | async-done | bytes 4194320 | tf_op jit(solution)/shard_map/psum | solution.py:135
  375.6 1.9 constant_dynamic-slice_fusion.1
  (81 shorter events, 20.0 us)
Async XLA Ops:
  6.5 26.4 %copy-start = (bf16[2048,3,256]{2,0,1:T(8,128)(2,1)S(1)}, bf16[2048,3,256]{2,0,1:T(8,128)(2,1)}, u32[]{:S(2)}) copy-start(bf16[2048,3,256]{2,0,1:T(8,128)(2,1)} %param.11) | copy-start | bytes 9437188
  15.7 11.9 %copy-start.9 = (s32[32]{0:T(128)S(1)}, s32[32]{0:T(128)}, u32[]{:S(2)}) copy-start(s32[32]{0:T(128)} %param.17) | copy-start | bytes 388
  15.7 12.6 %copy-start.10 = (s32[32]{0:T(128)S(1)}, s32[32]{0:T(128)}, u32[]{:S(2)}) copy-start(s32[32]{0:T(128)} %param.14) | copy-start | bytes 388
  15.7 201.5 %all-to-all-start = ((bf16[32,2,2,128,256]{4,3,2,1,0:T(8,128)(2,1)}), bf16[32,2,2,128,256]{4,3,2,1,0:T(8,128)(2,1)}, u32[]{:S(2)}, u32[]{:S(2)}) async-start(bf16[32,2,2,128,256]{4,3,2,1,0:T(8,128)(2,1)} %bitcast.83), calls=%async_computation | async-start | bytes 16777216 | tf_op jit(solution)/shard_map/all_to_all | solution.py:93
  27.5 348.1 %all-reduce.2.cloned.1.call-start = ((), (), s32[]{:S(2)}) async-start(), calls=%async_computation.1 | async-start | bytes 8388608 | tf_op jit(solution)/shard_map/psum | solution.py:135
  27.5 4.1 %copy-start.2 = (bf16[1024,2048]{1,0:T(8,128)(2,1)S(1)}, bf16[1024,2048]{1,0:T(8,128)(2,1)}, u32[]{:S(2)}) copy-start(bf16[1024,2048]{1,0:T(8,128)(2,1)} %param.10) | copy-start | bytes 12582916
  37.0 1.7 copy-start.5
  234.7 1.6 copy-start.3
  234.7 1.7 copy-start.6
  234.7 1.8 copy-start.7
  234.8 2.0 copy-start.8
  245.8 2.5 copy-start.4
  257.5 2.5 copy-start.4
  269.2 2.5 copy-start.4
  280.9 2.5 copy-start.4
  287.8 89.6 %copy-start.1 = (bf16[2048,3,256]{2,0,1:T(8,128)(2,1)S(1)}, bf16[2048,3,256]{2,0,1:T(8,128)(2,1)}, u32[]{:S(2)}) copy-start(bf16[2048,3,256]{2,0,1:T(8,128)(2,1)} %param.11) | copy-start | bytes 9437188
Sparse Core Ops, SparseCore 0:
  292.7 82.8 all-reduce.1
where the time goes:
time: 385 us; the launch traced here: 384 us
  waiting for transfers between devices  244 us (63%)
  local copies, waits for them, and re-layouts  45.9 us (12%)
  matrix products  30 us (8%)
  other arithmetic  26.4 us (7%)
  between operations  14.9 us (4%)
  starting transfers between devices  11.8 us (3%)
  loops' own time  11.4 us (3%)
    all_to_all x1, waiting for transfers between devices, body(): lax.all_to_all(outgoing, 'req', split_axis=0, concat_axis=0, tiled=True)  161 us
    psum x1, waiting for transfers between devices, body(): summed_rows = lax.psum(head_term.astype(jnp.bfloat16), 'tp')  83 us
    all_to_all x1, starting transfers between devices, body(): lax.all_to_all(outgoing, 'req', split_axis=0, concat_axis=0, tiled=True)  11.8 us
    dot_general x4, matrix products, attend_block(): jnp.einsum('qd,kd->qk', query_part, keys_part, preferred_element_type=jnp...  11.5 us
    another operation x1, loops' own time, body(): blocks_out = lax.map(joined_block, jnp.arange(work_items))  11.4 us
    reduce_sum x4, other arithmetic, attend_block(): row_total = jnp.sum(weights, axis=-1)  9.99 us
    dot_general x4, matrix products, attend_block(): jnp.einsum('qk,kd->qd', weights.astype(jnp.bfloat16), values_part, prefer...  9.69 us
    unnamed x24, local copies, waits for them, and re-layouts  7.73 us
  transfers between devices with their start and end apart: 2, of which 2 were waited for; matrix products, arithmetic and copies ran while one was open for 7% of the time, Pallas kernels for 0%

commit v1 on v0

--- a/solution.py
+++ b/solution.py
@@ -48,15 +48,21 @@
     local_reqs = hidden_in.shape[0] // NEW
     local_width = qkv_weight.shape[2]
     local_heads = local_width // HD
-    table_block = local_reqs * MAXP
-    capacity = max(2, 2 * table_block // req_count)
     cache_span = MAXP * PAGE
     holder_rows = page_holder[:, :, 0]
-    held_here = holder_rows == req_index
-    ranking = jnp.cumsum(held_here.astype(jnp.int32), axis=1) - 1
-    picked = held_here[:, :, None] & (ranking[:, :, None] == jnp.arange(capacity)[None, None, :])
-    send_slots = jnp.sum(jnp.where(picked, page_slot[:, :, None], 0), axis=1)
+    all_rows = holder_rows.shape[0]
+    same_holder_all = holder_rows[:, :, None] == holder_rows[:, None, :]
+    entry_ids = jnp.arange(holder_rows.shape[1])
+    earlier_all = entry_ids[None, None, :] < entry_ids[None, :, None]
+    rank_all = jnp.sum((same_holder_all & earlier_all).astype(jnp.int32), axis=2)
+    first_hit = (holder_rows == req_index) & (rank_all == 0)
+    send_slots = jnp.sum(jnp.where(first_hit, page_slot, 0), axis=1)
     outgoing = kv_pool[send_slots]
+    spill_flat = (rank_all > 0).reshape(-1)
+    spill_pos = jnp.cumsum(spill_flat.astype(jnp.int32)) - 1
+    spill_count = jnp.sum(spill_flat.astype(jnp.int32))
+    holders_flat = holder_rows.reshape(-1)
+    slots_flat = page_slot.reshape(-1)
     lengths = lax.dynamic_slice_in_dim(cached_len, req_index * local_reqs, local_reqs)
     flags = lax.dynamic_slice_in_dim(cont_flag, req_index * local_reqs, local_reqs)
     live_len = lengths * flags
@@ -91,13 +97,38 @@
         return (head, owner, query_pos, query_part)
 
     incoming = lax.all_to_all(outgoing, "req", split_axis=0, concat_axis=0, tiled=True)
+    spill_chunk = 8
+
+    def spill_pages(chunk):
+        wanted = chunk * spill_chunk + jnp.arange(spill_chunk)
+        match = spill_flat[None, :] & (spill_pos[None, :] == wanted[:, None])
+        owner = jnp.sum(jnp.where(match, holders_flat[None, :], 0), axis=1)
+        slot = jnp.sum(jnp.where(match, slots_flat[None, :], 0), axis=1)
+        mine = jnp.any(match, axis=1) & (owner == req_index)
+        contrib = jnp.where(mine[:, None, None, None], kv_pool[slot], jnp.zeros((), kv_pool.dtype))
+        return lax.psum(contrib, "req")
+
     own_holders = lax.dynamic_index_in_dim(holder_rows, req_index, 0, keepdims=False)
-    same_holder = own_holders[:, None] == own_holders[None, :]
-    earlier = jnp.arange(table_block)[None, :] < jnp.arange(table_block)[:, None]
-    own_rank = jnp.sum((same_holder & earlier).astype(jnp.int32), axis=1)
-    fetched = incoming.reshape(req_count * capacity, 2, PAGE, local_width)[
-        own_holders * capacity + own_rank
-    ]
+    own_rank = lax.dynamic_index_in_dim(rank_all, req_index, 0, keepdims=False)
+    own_pos = lax.dynamic_index_in_dim(spill_pos.reshape(all_rows, -1), req_index, 0, keepdims=False)
+    first_spill = spill_pages(0)
+    source = jnp.concatenate([incoming, first_spill], axis=0)
+    pick = jnp.where(own_rank == 0, own_holders, req_count + jnp.clip(own_pos, 0, spill_chunk - 1))
+    fetched = source[pick]
+
+    def more_cond(carry):
+        chunk, _ = carry
+        return chunk * spill_chunk < spill_count
+
+    def more_body(carry):
+        chunk, pages = carry
+        got = spill_pages(chunk)
+        local = own_pos - chunk * spill_chunk
+        hit = (own_rank > 0) & (local >= 0) & (local < spill_chunk)
+        pages = jnp.where(hit[:, None, None, None], got[jnp.clip(local, 0, spill_chunk - 1)], pages)
+        return (chunk + 1, pages)
+
+    _, fetched = lax.while_loop(more_cond, more_body, (jnp.int32(1), fetched))
     fetched = fetched.reshape(local_reqs, MAXP, 2, PAGE, local_width)
     cache_key = fetched[:, :, 0].reshape(local_reqs, cache_span, local_heads, HD)
     cache_value = fetched[:, :, 1].reshape(local_reqs, cache_span, local_heads, HD)
@@ -130,11 +161,8 @@
         .transpose(1, 0, 2)
         .reshape(row_count, local_width)
     )
-    share_rows = row_count // tp_count
     head_term = jnp.dot(attended, out_weight, preferred_element_type=jnp.float32)
-    summed_rows = lax.psum(head_term.astype(jnp.bfloat16), "tp")
-    result = lax.dynamic_slice_in_dim(summed_rows, lax.axis_index("tp") * share_rows, share_rows, 0)
-    return result
+    return lax.psum_scatter(head_term.astype(jnp.bfloat16), "tp", scatter_dimension=0, tiled=True)
 
 
 def solution(mesh):

time: 385 us -> 354 us (0.919)
  waiting for transfers between devices: 244 us -> 199 us
  other arithmetic: 26.4 us -> 36.8 us
  matrix products: 30 us -> 36.5 us
    all_to_all x1, waiting for transfers between devices: 161 us -> 0.01 us  [body(): lax.all_to_all(outgoing, 'req', split_axis=0, concat_axis=0, tiled=True)]
    psum x1, waiting for transfers between devices: 83 us -> 160 us  [spill_pages(): return lax.psum(contrib, 'req')]
    reduce_scatter x0 -> x1, waiting for transfers between devices: none -> 39.2 us  [body(): lax.psum_scatter(head_term.astype(jnp.bfloat16), 'tp', scatter_dimension=...]
    concatenate x0 -> x2, other arithmetic: none -> 8.58 us  [the longest x1 5.28 us: body(): source = jnp.concatenate([incoming, first_spill], axis=0)]
    unnamed x24 -> x23, local copies, waits for them, and re-layouts: 7.73 us -> 0.56 us
    dot_general x4, matrix products: 11.5 us -> 17.7 us  [attend_block(): jnp.einsum('qd,kd->qk', query_part, keys_part, preferred_element_type=jnp...]
    another operation x2, local copies, waits for them, and re-layouts: 4.12 us -> 10.3 us  [body(): fetched[:, :, 1].reshape(local_reqs, cache_span, local_heads, HD)]
    another operation x2, local copies, waits for them, and re-layouts: 2.82 us -> 6.76 us  [body(): fetched[:, :, 0].reshape(local_reqs, cache_span, local_heads, HD)]
  transfers between devices with their start and end apart: 2 -> 3, of which waited for: 2 -> 2; matrix products, arithmetic and copies ran while one was open for 7% -> 7% of each run, Pallas kernels for 0% -> 0%
where the time goes in v1:
time: 354 us; the launch traced here: 353 us
  waiting for transfers between devices  199 us (56%)
  local copies, waits for them, and re-layouts  43 us (12%)
  other arithmetic  36.8 us (10%)
  matrix products  36.5 us (10%)
  between operations  14.8 us (4%)
  starting transfers between devices  12.1 us (3%)
  loops' own time  11.3 us (3%)
    psum x1, waiting for transfers between devices, spill_pages(): return lax.psum(contrib, 'req')  160 us
    reduce_scatter x1, waiting for transfers between devices, body(): lax.psum_scatter(head_term.astype(jnp.bfloat16), 'tp', scatter_dimension=...  39.2 us
    dot_general x4, matrix products, attend_block(): jnp.einsum('qd,kd->qk', query_part, keys_part, preferred_element_type=jnp...  17.7 us
    all_to_all x1, starting transfers between devices, body(): lax.all_to_all(outgoing, 'req', split_axis=0, concat_axis=0, tiled=True)  11.8 us
    another operation x1, loops' own time, body(): blocks_out = lax.map(joined_block, jnp.arange(work_items))  10.7 us
    another operation x2, local copies, waits for them, and re-layouts, body(): fetched[:, :, 1].reshape(local_reqs, cache_span, local_heads, HD)  10.3 us
    dot_general x4, matrix products, attend_block(): jnp.einsum('qk,kd->qd', weights.astype(jnp.bfloat16), values_part, prefer...  9.99 us
    reduce_sum x4, other arithmetic, attend_block(): row_total = jnp.sum(weights, axis=-1)  9.99 us
  transfers between devices with their start and end apart: 3, of which 2 were waited for; matrix products, arithmetic and copies ran while one was open for 7% of the time, Pallas kernels for 0%

profile of v1, /device:TPU:2, one launch (start us, length us, event | category | flops | bytes accessed | tf_op | source)
XLA Modules:
  0.0 353.3 jit_solution(13241626098705244110)
XLA Ops:
  9.6 4.3 %gather_fusion.2 = bf16[32,2,128,256]{3,2,1,0:T(8,128)(2,1)} fusion(bf16[16,2,128,256]{3,2,1,0:T(8,128)(2,1)} %param.15, s32[1024]{0:T(1024)S(1)} %pad_clamp_fusion.4), kind=kCustom, calls=%fused_computation.2 | custom fusion | bytes 8388736 | tf_op jit(solution)/shard_map/gather | solution.py:60
  13.9 11.8 %all-to-all-start = ((bf16[32,2,128,256]{3,2,1,0:T(8,128)(2,1)}), bf16[32,2,128,256]{3,2,1,0:T(8,128)(2,1)}, u32[]{:S(2)}, u32[]{:S(2)}) async-start(bf16[32,2,128,256]{3,2,1,0:T(8,128)(2,1)} %gather_fusion.2), calls=%async_computation | async-start | bytes 8388608 | tf_op jit(solution)/shard_map/all_to_all | solution.py:99
  28.1 3.2 gather_fusion.3
  31.4 2.3 broadcast_select_fusion.2
  36.0 2.8 convert_reduce_fusion
  40.1 4.0 %fusion.45 = f32[1024,3,256]{0,2,1:T(8,128)S(1)} fusion(bf16[2048,3,256]{2,0,1:T(8,128)(2,1)S(1)} %copy-done, bf16[1024,2048]{1,0:T(8,128)(2,1)S(1)} %copy-done.3, f32[1024]{0:T(1024)S(1)} %add_rsqrt_fusion, f32[1024]{0:T(1024)S(1)} %broadcast_multiply_fusion), kind=kOutput, calls=%fused_computation.53 | convolution fusion | flops 3229614080 | bytes 10493952 | tf_op jit(solution)/shard_map/td,dcf->tcf/dot_general | solution.py:74
  50.7 159.5 %all-reduce.3.cloned.1.call-done = bf16[8,2,128,256]{3,2,1,0:T(8,128)(2,1)} async-done(((bf16[8,2,128,256]{3,2,1,0:T(8,128)(2,1)}), bf16[8,2,128,256]{3,2,1,0:T(8,128)(2,1)}) %all-reduce.3.cloned.1.call-update) | async-done | bytes 1048592 | tf_op jit(solution)/shard_map/psum | solution.py:109
  210.3 5.3 %pad_maximum_fusion = bf16[40,2,128,256]{3,2,1,0:T(8,128)(2,1)} fusion(bf16[8,2,128,256]{3,2,1,0:T(8,128)(2,1)} %all-reduce.3.cloned.1.call-done, bf16[32,2,128,256]{3,2,1,0:T(8,128)(2,1)} %all-to-all-done), kind=kLoop, calls=%fused_computation.51 | loop fusion | flops 2621440 | bytes 10485760 | tf_op jit(solution)/shard_map/concatenate | solution.py:115
  215.6 5.5 %gather_fusion.4 = bf16[32,2,128,256]{3,2,1,0:T(8,128)(2,1)} fusion(bf16[40,2,128,256]{3,2,1,0:T(8,128)(2,1)} %pad_maximum_fusion, s32[1024]{0:T(1024)S(1)} %pad_clamp_fusion.2), kind=kCustom, calls=%fused_computation.4 | custom fusion | bytes 8388736 | tf_op jit(solution)/shard_map/gather | solution.py:117
  221.8 4.1 %fusion.62 = (bf16[1,32,1,128,256]{4,3,2,1,0:T(8,128)(2,1)}, bf16[1,32,1,128,256]{4,3,2,1,0:T(8,128)(2,1)S(1)}) fusion(bf16[1,32,2,128,256]{4,3,2,1,0:T(8,128)(2,1)} %bitcast.120), kind=kLoop, calls=%fused_computation.106 | loop fusion | bytes 8388608 | tf_op jit(solution)/shard_map/slice | solution.py:134
  225.9 2.0 reshape.422
  228.0 4.7 %copy.37 = bf16[1,4096,2,128]{1,3,2,0:T(8,128)(2,1)S(1)} copy(bf16[1,4096,2,128]{3,2,1,0:T(2,128)(2,1)} %reshape.422) | data formatting | bytes 4194304 | tf_op jit(solution)/shard_map/reshape;squeeze | solution.py:133
  232.7 4.1 %reshape.423 = bf16[1,4096,2,128]{3,2,1,0:T(2,128)(2,1)} reshape(bf16[1,32,1,128,256]{4,3,2,1,0:T(8,128)(2,1)} %get-tuple-element.250) | data formatting | bytes 4194304 | tf_op jit(solution)/shard_map/reshape;squeeze | solution.py:134
  236.8 6.2 %copy.38 = bf16[1,4096,2,128]{1,3,2,0:T(8,128)(2,1)} copy(bf16[1,4096,2,128]{3,2,1,0:T(2,128)(2,1)} %reshape.423) | data formatting | bytes 4194304 | tf_op jit(solution)/shard_map/reshape;squeeze | solution.py:134
  243.0 3.3 pad_maximum_fusion.1
  246.3 1.7 maximum_maximum_fusion
  248.0 52.4 %while.24 = (s32[]{:T(128)}, bf16[4,512,128]{2,1,0:T(8,128)(2,1)}, s32[1]{0:T(128)}, s32[4]{0:T(128)S(1)}, bf16[2,1024,128]{1,2,0:T(8,128)(2,1)}, /*index=5*/bf1...) while((s32[]{:T(128)}, bf16[4,512,128]{2,1,0:T(8,128)(2,1)}, ...), condition=%wide.region_20.21_spmd.clone, body=%wide.region_17.20_spmd.clone.sunk | while | flops 1374293504 | bytes 46969404 | solution.py:158
  251.7 4.4 %fusion.80 = (f32[512]{0:T(512)S(1)}, f32[512,5120]{1,0:T(8,128)S(1)}) fusion(bf16[1,5120,2,128]{1,3,2,0:T(8,128)(2,1)} %get-tuple-element.523, s32[]{:T(128)S(6)} %select_n.234, bf16[2,1024,128]{1,2,0:T(8,128)(2,1)} %get-tuple-element.522, s32[]{:T(128)S(6)} %select_n.236, pred[512,1024]{1,0:T(32,128)(4,1)S(1)} %iota_compare_fusion.6, ...), kind=kOutput, calls=%fused_computation.105.clone.1 | convolution fusion | flops 681573888 | bytes 12460544 | tf_op jit(solution)/shard_map/while/body/eval_jaxpr/qd,kd->qk/dot_general | solution.py:31
  256.1 2.5 fusion.81
  258.6 2.5 fusion.82
  264.8 4.4 %fusion.80 = (f32[512]{0:T(512)S(1)}, f32[512,5120]{1,0:T(8,128)S(1)}) fusion(bf16[1,5120,2,128]{1,3,2,0:T(8,128)(2,1)} %get-tuple-element.523, s32[]{:T(128)S(6)} %select_n.234, bf16[2,1024,128]{1,2,0:T(8,128)(2,1)} %get-tuple-element.522, s32[]{:T(128)S(6)} %select_n.236, pred[512,1024]{1,0:T(32,128)(4,1)S(1)} %iota_compare_fusion.6, ...), kind=kOutput, calls=%fused_computation.105.clone.1 | convolution fusion | flops 681573888 | bytes 12460544 | tf_op jit(solution)/shard_map/while/body/eval_jaxpr/qd,kd->qk/dot_general | solution.py:31
  269.2 2.5 fusion.81
  271.7 2.5 fusion.82
  277.8 4.4 %fusion.80 = (f32[512]{0:T(512)S(1)}, f32[512,5120]{1,0:T(8,128)S(1)}) fusion(bf16[1,5120,2,128]{1,3,2,0:T(8,128)(2,1)} %get-tuple-element.523, s32[]{:T(128)S(6)} %select_n.234, bf16[2,1024,128]{1,2,0:T(8,128)(2,1)} %get-tuple-element.522, s32[]{:T(128)S(6)} %select_n.236, pred[512,1024]{1,0:T(32,128)(4,1)S(1)} %iota_compare_fusion.6, ...), kind=kOutput, calls=%fused_computation.105.clone.1 | convolution fusion | flops 681573888 | bytes 12460544 | tf_op jit(solution)/shard_map/while/body/eval_jaxpr/qd,kd->qk/dot_general | solution.py:31
  282.3 2.5 fusion.81
  284.8 2.5 fusion.82
  290.9 4.4 %fusion.80 = (f32[512]{0:T(512)S(1)}, f32[512,5120]{1,0:T(8,128)S(1)}) fusion(bf16[1,5120,2,128]{1,3,2,0:T(8,128)(2,1)} %get-tuple-element.523, s32[]{:T(128)S(6)} %select_n.234, bf16[2,1024,128]{1,2,0:T(8,128)(2,1)} %get-tuple-element.522, s32[]{:T(128)S(6)} %select_n.236, pred[512,1024]{1,0:T(32,128)(4,1)S(1)} %iota_compare_fusion.6, ...), kind=kOutput, calls=%fused_computation.105.clone.1 | convolution fusion | flops 681573888 | bytes 12460544 | tf_op jit(solution)/shard_map/while/body/eval_jaxpr/qd,kd->qk/dot_general | solution.py:31
  295.4 2.5 fusion.81
  297.9 2.5 fusion.82
  300.4 2.0 copy.35
  302.4 4.8 %convolution_convert_fusion = bf16[1024,2048]{1,0:T(8,128)(2,1)} fusion(bf16[1024,256]{0,1:T(8,128)(2,1)} %bitcast.123, bf16[256,2048]{1,0:T(8,128)(2,1)} %param.14), kind=kOutput, calls=%fused_computation.56 | convolution fusion | flops 1075838976 | bytes 5767168 | tf_op jit(solution)/shard_map/dot_general | solution.py:164
  307.2 39.2 %reduce-scatter.2.cloned.1.call-done = bf16[128,2048]{1,0:T(8,128)(2,1)} async-done(((bf16[1024,2048]{1,0:T(8,128)(2,1)}), bf16[128,2048]{1,0:T(8,128)(2,1)}) %reduce-scatter.2.cloned.1.call-update) | async-done | bytes 524304 | tf_op jit(solution)/shard_map/reduce_scatter | solution.py:165
  (101 shorter events, 19.1 us)
Async XLA Ops:
  6.5 33.6 %copy-start = (bf16[2048,3,256]{2,0,1:T(8,128)(2,1)S(1)}, bf16[2048,3,256]{2,0,1:T(8,128)(2,1)}, u32[]{:S(2)}) copy-start(bf16[2048,3,256]{2,0,1:T(8,128)(2,1)} %param.13) | copy-start | bytes 9437188
  9.6 24.3 %copy-start.9 = (pred[32,32]{1,0:T(8,128)(4,1)}, pred[32,32]{1,0:T(8,128)(4,1)S(1)}, u32[]{:S(2)}) copy-start(pred[32,32]{1,0:T(8,128)(4,1)S(1)} %get-tuple-element.447) | copy-start | bytes 3076
  13.9 12.0 %copy-start.8 = (s32[32,32]{1,0:T(8,128)S(1)}, s32[32,32]{1,0:T(8,128)}, u32[]{:S(2)}) copy-start(s32[32,32]{1,0:T(8,128)} %param.17) | copy-start | bytes 12292
  13.9 13.0 %copy-start.6 = (s32[32,32,1]{1,2,0:T(1,128)S(1)}, s32[32,32,1]{1,2,0:T(1,128)}, u32[]{:S(2)}) copy-start(s32[32,32,1]{1,2,0:T(1,128)} %param.18) | copy-start | bytes 12292
  13.9 196.3 %all-to-all-start = ((bf16[32,2,128,256]{3,2,1,0:T(8,128)(2,1)}), bf16[32,2,128,256]{3,2,1,0:T(8,128)(2,1)}, u32[]{:S(2)}, u32[]{:S(2)}) async-start(bf16[32,2,128,256]{3,2,1,0:T(8,128)(2,1)} %gather_fusion.2), calls=%async_computation | async-start | bytes 8388608 | tf_op jit(solution)/shard_map/all_to_all | solution.py:99
  25.8 9.1 %copy-start.10 = (s32[32]{0:T(128)S(1)}, s32[32]{0:T(128)}, u32[]{:S(2)}) copy-start(s32[32]{0:T(128)} %param.16) | copy-start | bytes 388
  25.8 9.6 %copy-start.11 = (s32[32]{0:T(128)S(1)}, s32[32]{0:T(128)}, u32[]{:S(2)}) copy-start(s32[32]{0:T(128)} %param.19) | copy-start | bytes 388
  25.8 184.5 %all-reduce.3.cloned.1.call-start = ((), (), s32[]{:S(2)}) async-start(), calls=%async_computation.2 | async-start | bytes 2097152 | tf_op jit(solution)/shard_map/psum | solution.py:109
  34.2 4.7 %copy-start.3 = (bf16[1024,2048]{1,0:T(8,128)(2,1)S(1)}, bf16[1024,2048]{1,0:T(8,128)(2,1)}, u32[]{:S(2)}) copy-start(bf16[1024,2048]{1,0:T(8,128)(2,1)} %param.12) | copy-start | bytes 12582916
  215.6 5.5 %copy-start.2 = (bf16[16,2,128,256]{3,2,1,0:T(8,128)(2,1)S(1)}, bf16[16,2,128,256]{3,2,1,0:T(8,128)(2,1)}, u32[]{:S(2)}) copy-start(bf16[16,2,128,256]{3,2,1,0:T(8,128)(2,1)} %param.15) | copy-start | bytes 6291460
  221.6 124.8 %reduce-scatter.2.cloned.1.call-start = ((), (), s32[]{:S(2)}) async-start(), calls=%async_computation.3 | async-start | bytes 4718592 | tf_op jit(solution)/shard_map/reduce_scatter | solution.py:165
  232.7 10.3 %copy-start.5 = (bf16[1024,1,256]{0,2,1:T(8,128)(2,1)S(1)}, bf16[1024,1,256]{0,2,1:T(8,128)(2,1)}, u32[]{:S(2)}) copy-start(bf16[1024,1,256]{0,2,1:T(8,128)(2,1)} %slice.84) | copy-start | bytes 1572868
  236.8 9.5 %copy-start.7 = (bf16[1,1024,2,64]{1,3,2,0:T(8,128)(2,1)S(1)}, bf16[1,1024,2,64]{1,3,2,0:T(8,128)(2,1)}, u32[]{:S(2)}) copy-start(bf16[1,1024,2,64]{1,3,2,0:T(8,128)(2,1)} %get-tuple-element.255) | copy-start | bytes 786436
  256.1 2.5 copy-start.4
  269.2 2.5 copy-start.4
  282.3 2.5 copy-start.4
  295.4 2.5 copy-start.4
  302.4 44.0 %copy-start.1 = (bf16[2048,3,256]{2,0,1:T(8,128)(2,1)S(1)}, bf16[2048,3,256]{2,0,1:T(8,128)(2,1)}, u32[]{:S(2)}) copy-start(bf16[2048,3,256]{2,0,1:T(8,128)(2,1)} %param.13) | copy-start | bytes 9437188
Sparse Core Ops, SparseCore 0:
  33.9 176.3 all-reduce.2
  307.3 39.0 reduce-scatter.1

commit v2 on v0

v2 whole, which is shorter than its diff:
```python
import functools

import jax
import jax.numpy as jnp
from jax import lax
from jax.experimental import pallas as pl
from jax.experimental.pallas import tpu as pltpu
from jax.sharding import PartitionSpec as P

HD = 128
NEW = 1024
PAGE = 128
MAXP = 32
BLOCK_Q = 256


def rotate(feature, position):
    half_width = feature.shape[-1] // 2
    indices = jnp.arange(half_width).astype(jnp.float32)
    inverse = jnp.exp(indices * (-2.0 / feature.shape[-1]) * jnp.log(jnp.float32(10000.0)))
    angles = position[:, None, None] * inverse[None, None, :]
    cosine = jnp.cos(angles)
    sine_part = jnp.sin(angles)
    first_half = feature[..., :half_width]
    second_half = feature[..., half_width:]
    return jnp.concatenate(
        [
            first_half * cosine - second_half * sine_part,
            second_half * cosine + first_half * sine_part,
        ],
        axis=-1,
    )


def attend_kernel(live_ref, q_ref, ck_ref, cv_ref, nk_ref, nv_ref, out_ref):
    block = pl.program_id(1)
    live = live_ref[0]
    cache_span = ck_ref.shape[0] * ck_ref.shape[2]
    query = q_ref[...]
    cache_key = ck_ref[...].reshape(cache_span, HD)
    cache_value = cv_ref[...].reshape(cache_span, HD)
    contract = (((1,), (1,)), ((), ()))
    scale = HD ** (-0.5)
    cache_scores = lax.dot_general(
        query, cache_key, contract, preferred_element_type=jnp.float32
    ) * scale
    new_scores = lax.dot_general(
        query, nk_ref[...], contract, preferred_element_type=jnp.float32
    ) * scale
    cache_ok = lax.broadcasted_iota(jnp.int32, cache_scores.shape, 1) < live
    query_pos = block * BLOCK_Q + lax.broadcasted_iota(jnp.int32, new_scores.shape, 0)
    new_ok = lax.broadcasted_iota(jnp.int32, new_scores.shape, 1) <= query_pos
    cache_scores = jnp.where(cache_ok, cache_scores, -1e30)
    new_scores = jnp.where(new_ok, new_scores, -1e30)
    row_top = jnp.maximum(
        jnp.max(cache_scores, axis=1, keepdims=True), jnp.max(new_scores, axis=1, keepdims=True)
    )
    cache_weights = jnp.where(cache_ok, jnp.exp(cache_scores - row_top), 0.0)
    new_weights = jnp.where(new_ok, jnp.exp(new_scores - row_top), 0.0)
    row_total = jnp.sum(cache_weights, axis=1, keepdims=True) + jnp.sum(
        new_weights, axis=1, keepdims=True
    )
    summed = jnp.dot(
        cache_weights.astype(jnp.bfloat16), cache_value, preferred_element_type=jnp.float32
    ) + jnp.dot(new_weights.astype(jnp.bfloat16), nv_ref[...], preferred_element_type=jnp.float32)
    out_ref[...] = (summed / row_total).astype(out_ref.dtype)


def attend(live, query, pages, new_key, new_value):
    rows, width = query.shape
    heads = width // HD
    pages_n = pages.shape[0]
    grid_spec = pltpu.PrefetchScalarGridSpec(
        num_scalar_prefetch=1,
        grid=(heads, rows // BLOCK_Q),
        in_specs=[
            pl.BlockSpec((BLOCK_Q, HD), lambda h, b, live: (b, h)),
            pl.BlockSpec((pages_n, None, PAGE, HD), lambda h, b, live: (0, 0, 0, h)),
            pl.BlockSpec((pages_n, None, PAGE, HD), lambda h, b, live: (0, 1, 0, h)),
            pl.BlockSpec((rows, HD), lambda h, b, live: (0, h)),
            pl.BlockSpec((rows, HD), lambda h, b, live: (0, h)),
        ],
        out_specs=pl.BlockSpec((BLOCK_Q, HD), lambda h, b, live: (b, h)),
    )
    keys_n = pages_n * PAGE + rows
    return pl.pallas_call(
        attend_kernel,
        grid_spec=grid_spec,
        out_shape=jax.ShapeDtypeStruct((rows, width), jnp.bfloat16),
        compiler_params=pltpu.CompilerParams(vmem_limit_bytes=48 * 1024 * 1024),
        cost_estimate=pl.CostEstimate(
            flops=4 * rows * keys_n * width,
            transcendentals=rows * keys_n * heads,
            bytes_accessed=2 * (2 * keys_n * width + 2 * rows * width),
        ),
    )(live, query, pages, pages, new_key, new_value)


def body(hidden_in, qkv_weight, out_weight, kv_pool, cached_len, page_slot, page_holder, cont_flag):
    req_count = lax.axis_size("req")
    req_index = lax.axis_index("req")
    local_reqs = hidden_in.shape[0] // NEW
    local_width = qkv_weight.shape[2]
    local_heads = local_width // HD
    table_block = local_reqs * MAXP
    capacity = max(2, 2 * table_block // req_count)
    holder_rows = page_holder[:, :, 0]
    held_here = holder_rows == req_index
    ranking = jnp.cumsum(held_here.astype(jnp.int32), axis=1) - 1
    picked = held_here[:, :, None] & (ranking[:, :, None] == jnp.arange(capacity)[None, None, :])
    send_slots = jnp.sum(jnp.where(picked, page_slot[:, :, None], 0), axis=1)
    outgoing = kv_pool[send_slots]
    incoming = lax.all_to_all(outgoing, "req", split_axis=0, concat_axis=0, tiled=True)
    lengths = lax.dynamic_slice_in_dim(cached_len, req_index * local_reqs, local_reqs)
    flags = lax.dynamic_slice_in_dim(cont_flag, req_index * local_reqs, local_reqs)
    live_len = lengths * flags
    token_rows = hidden_in.astype(jnp.float32)
    centre = jnp.mean(token_rows, axis=-1, keepdims=True)
    centred = token_rows - centre
    spread = jnp.mean(centred * centred, axis=-1, keepdims=True)
    normed = (centred * lax.rsqrt(spread + 1e-05)).astype(jnp.bfloat16)
    united_qkv = jnp.einsum("td,dcf->tcf", normed, qkv_weight, preferred_element_type=jnp.float32)
    positions = (live_len[:, None] + jnp.arange(NEW)[None, :]).astype(jnp.float32).reshape(-1)
    query_rot = rotate(united_qkv[:, 0].reshape(-1, local_heads, HD), positions).astype(
        jnp.bfloat16
    ).reshape(-1, local_width)
    new_key = rotate(united_qkv[:, 1].reshape(-1, local_heads, HD), positions).astype(
        jnp.bfloat16
    ).reshape(-1, local_width)
    new_value = united_qkv[:, 2].astype(jnp.bfloat16)
    own_holders = lax.dynamic_index_in_dim(holder_rows, req_index, 0, keepdims=False)
    same_holder = own_holders[:, None] == own_holders[None, :]
    earlier = jnp.arange(table_block)[None, :] < jnp.arange(table_block)[:, None]
    own_rank = jnp.sum((same_holder & earlier).astype(jnp.int32), axis=1)
    fetched = incoming.reshape(req_count * capacity, 2, PAGE, local_width)[
        own_holders * capacity + own_rank
    ]
    attended = attend(live_len[:1], query_rot, fetched, new_key, new_value)
    head_term = jnp.dot(attended, out_weight, preferred_element_type=jnp.float32)
    return lax.psum_scatter(head_term.astype(jnp.bfloat16), "tp", scatter_dimension=0, tiled=True)


def solution(mesh):
    in_specs = (
        P("req", None),
        P(None, None, "tp"),
        P("tp", None),
        P("req", None, None, "tp"),
        P(),
        P(),
        P(),
        P(),
    )
    out_specs = P(("req", "tp"), None)
    return jax.shard_map(body, mesh=mesh, in_specs=in_specs, out_specs=out_specs, check_vma=False)
```

time: 385 us -> 309 us (0.80)
  waiting for transfers between devices: 244 us -> 194 us
  Pallas kernels: 0 us -> 25.6 us
  matrix products: 30 us -> 7.25 us
  loops' own time: 11.4 us -> 0 us
  other arithmetic: 26.4 us -> 15.4 us
  local copies, waits for them, and re-layouts: 45.9 us -> 39.5 us
    psum x1 -> x0, waiting for transfers between devices: 83 us -> none  [body(): summed_rows = lax.psum(head_term.astype(jnp.bfloat16), 'tp')]
    reduce_scatter x0 -> x1, waiting for transfers between devices: none -> 45.7 us  [body(): lax.psum_scatter(head_term.astype(jnp.bfloat16), 'tp', scatter_dimension=...]
    pallas_call x0 -> x1, Pallas kernels: none -> 25.6 us  [attend(): pl.pallas_call(attend_kernel, grid_spec=grid_spec, out_shape=jax.ShapeDty...]
    dot_general x8 -> x0, matrix products: 21.2 us -> none  [the longest x4 11.5 us: attend_block(): jnp.einsum('qd,kd->qk', query_part, keys_part, preferred_element_type=jnp...]
    all_to_all x1, waiting for transfers between devices: 161 us -> 148 us  [body(): lax.all_to_all(outgoing, 'req', split_axis=0, concat_axis=0, tiled=True)]
    another operation x1 -> x0, loops' own time: 11.4 us -> none  [body(): blocks_out = lax.map(joined_block, jnp.arange(work_items))]
    reduce_sum x4 -> x0, other arithmetic: 9.99 us -> none  [attend_block(): row_total = jnp.sum(weights, axis=-1)]
    unnamed x24 -> x25, local copies, waits for them, and re-layouts: 7.73 us -> 17.2 us
  transfers between devices with their start and end apart: 2 -> 2, of which waited for: 2 -> 2; matrix products, arithmetic and copies ran while one was open for 7% -> 13% of each run, Pallas kernels for 0% -> 0%
where the time goes in v2:
time: 309 us; the launch traced here: 308 us
  waiting for transfers between devices  194 us (63%)
  local copies, waits for them, and re-layouts  39.5 us (13%)
  Pallas kernels  25.6 us (8%)
  other arithmetic  15.4 us (5%)
  between operations  14.8 us (5%)
  starting transfers between devices  11.8 us (4%)
  matrix products  7.25 us (2%)
    all_to_all x1, waiting for transfers between devices, body(): lax.all_to_all(outgoing, 'req', split_axis=0, concat_axis=0, tiled=True)  148 us
    reduce_scatter x1, waiting for transfers between devices, body(): lax.psum_scatter(head_term.astype(jnp.bfloat16), 'tp', scatter_dimension=...  45.7 us
    pallas_call x1, Pallas kernels, attend(): pl.pallas_call(attend_kernel, grid_spec=grid_spec, out_shape=jax.ShapeDty...  25.6 us
    unnamed x25, local copies, waits for them, and re-layouts  17.2 us
    all_to_all x1, starting transfers between devices, body(): lax.all_to_all(outgoing, 'req', split_axis=0, concat_axis=0, tiled=True)  11.7 us
    gather x1, local copies, waits for them, and re-layouts, body(): outgoing = kv_pool[send_slots]  7.04 us
  transfers between devices with their start and end apart: 2, of which 2 were waited for; matrix products, arithmetic and copies ran while one was open for 13% of the time, Pallas kernels for 0%

profile of v2, /device:TPU:2, one launch (start us, length us, event | category | flops | bytes accessed | tf_op | source)
XLA Modules:
  0.0 307.9 jit_solution(12209609140625854670)
XLA Ops:
  6.5 0.9 broadcast_compare_fusion
  7.6 0.8 select_reduce_fusion
  8.7 7.0 %gather_fusion = bf16[64,2,128,256]{3,2,1,0:T(8,128)(2,1)} fusion(bf16[16,2,128,256]{3,2,1,0:T(8,128)(2,1)} %param.11, s32[1024]{0:T(1024)S(1)} %pad_clamp_fusion.1), kind=kCustom, calls=%fused_computation | custom fusion | bytes 16777472 | tf_op jit(solution)/shard_map/gather | solution.py:112
  15.7 11.7 %all-to-all-start = ((bf16[32,2,2,128,256]{4,3,2,1,0:T(8,128)(2,1)}), bf16[32,2,2,128,256]{4,3,2,1,0:T(8,128)(2,1)}, u32[]{:S(2)}, u32[]{:S(2)}) async-start(bf16[32,2,2,128,256]{4,3,2,1,0:T(8,128)(2,1)} %bitcast.42), calls=%async_computation | async-start | bytes 16777216 | tf_op jit(solution)/shard_map/all_to_all | solution.py:113
  28.8 2.8 convert_reduce_fusion
  31.6 1.2 fusion.2
  32.9 4.0 %fusion.5 = f32[1024,3,256]{0,2,1:T(8,128)S(1)} fusion(bf16[2048,3,256]{2,0,1:T(8,128)(2,1)S(1)} %copy-done, bf16[1024,2048]{1,0:T(8,128)(2,1)S(1)} %copy-done.4, f32[1024]{0:T(1024)S(1)} %add_rsqrt_fusion, f32[1024]{0:T(1024)S(1)} %broadcast_multiply_fusion), kind=kOutput, calls=%fused_computation.9 | convolution fusion | flops 3229614080 | bytes 10493952 | tf_op jit(solution)/shard_map/td,dcf->tcf/dot_general | solution.py:122
  36.9 1.6 copy-done.5
  38.6 0.9 slice.39
  39.4 2.0 copy.36
  41.5 2.7 fusion.14
  44.2 1.1 fusion.15
  45.3 2.2 copy.35
  47.4 2.3 fusion.16
  49.7 2.2 copy.33
  51.9 2.2 copy.34
  54.1 2.2 copy.32
  57.5 1.9 multiply_cosine_fusion
  59.4 3.8 %subtract_convert_fusion = (bf16[1024,2,64]{2,1,0:T(2,128)(2,1)S(1)}, bf16[1024,2,64]{2,1,0:T(2,128)(2,1)S(1)}, bf16[1024,2,64]{2,1,0:T(2,128)(2,1)S(1)}, bf16[1024,2,64]{2,1,0:T(2,128)(2,1)S(1)}) fusion(f32[1024,2,64]{2,1,0:T(2,128)} %copy.35, f32[1024,2,64]{2,1,0:T(2,128)} %copy.34, f32[1024,64]{1,0:T(8,128)S(1)} %get-tuple-element.20, ...), kind=kLoop, calls=%fused_computation.14 | loop fusion | flops 2097152 | bytes 3670016 | tf_op jit(solution)/shard_map/convert.2
  63.2 2.9 pad_maximum_fusion
  66.1 0.9 copy.44
  67.0 0.9 copy.43
  67.8 0.7 fusion.12
  68.7 0.7 fusion.11
  69.4 147.8 %all-to-all-done = bf16[32,2,2,128,256]{4,3,2,1,0:T(8,128)(2,1)} async-done(((bf16[32,2,2,128,256]{4,3,2,1,0:T(8,128)(2,1)}), bf16[32,2,2,128,256]{4,3,2,1,0:T(8,128)(2,1)}, u32[]{:S(2)}, u32[]{:S(2)}) %all-to-all-start) | async-done | bytes 8388640 | tf_op jit(solution)/shard_map/all_to_all | solution.py:113
  217.2 6.1 %gather_fusion.1 = bf16[32,2,128,256]{3,2,1,0:T(8,128)(2,1)} fusion(bf16[64,2,128,256]{3,2,1,0:T(8,128)(2,1)} %bitcast.5, s32[1024]{0:T(1024)S(1)} %pad_clamp_fusion), kind=kCustom, calls=%fused_computation.1 | custom fusion | bytes 8388736 | tf_op jit(solution)/shard_map/gather | solution.py:135
  223.3 1.0 copy-done.1
  224.4 1.0 copy-done.2
  225.4 1.0 copy-done.3
  226.5 25.6 %shard_map.82 = bf16[1024,256]{1,0:T(8,128)(2,1)S(1)} custom-call(s32[1]{0:T(128)} %mul.122.live_ref, bf16[1024,256]{1,0:T(8,128)(2,1)S(1)} %bitcast.40, bf16[32,2,128,256]{3,2,1,0:T(8,128)(2,1)} %gather_fusion.1, bf16[32,2,128,256]{3,2,1,0:T(8,128)(2,1)} %gather_fusion.1, bf16[1024,256]{1,0:T(8,128)(2,1)S(1)} %bitcast.41, bf16[1024,256]{1,0:T(8,128)(2,1)S(1)} %bitcast.39), custom_call_target="tpu_custom_call" | custom-call | flops 5368709120 | bytes 6291456 | tf_op jit(solution)/shard_map/pallas_call | solution.py:86
  252.1 3.2 %convolution_convert_fusion = bf16[1024,2048]{1,0:T(8,128)(2,1)} fusion(bf16[1024,256]{1,0:T(8,128)(2,1)S(1)} %shard_map.82, bf16[256,2048]{1,0:T(8,128)(2,1)S(1)} %copy-done.6), kind=kOutput, calls=%fused_computation.12 | convolution fusion | flops 1075838976 | bytes 5767168 | tf_op jit(solution)/shard_map/dot_general | solution.py:139
  255.3 45.7 %reduce-scatter.2.cloned.1.call-done = bf16[128,2048]{1,0:T(8,128)(2,1)} async-done(((bf16[1024,2048]{1,0:T(8,128)(2,1)}), bf16[128,2048]{1,0:T(8,128)(2,1)}) %reduce-scatter.2.cloned.1.call-update) | async-done | bytes 524304 | tf_op jit(solution)/shard_map/reduce_scatter | solution.py:140
  (31 shorter events, 2.0 us)
Async XLA Ops:
  6.5 26.3 %copy-start = (bf16[2048,3,256]{2,0,1:T(8,128)(2,1)S(1)}, bf16[2048,3,256]{2,0,1:T(8,128)(2,1)}, u32[]{:S(2)}) copy-start(bf16[2048,3,256]{2,0,1:T(8,128)(2,1)} %param.9) | copy-start | bytes 9437188
  15.7 11.8 %copy-start.7 = (s32[32]{0:T(128)S(1)}, s32[32]{0:T(128)}, u32[]{:S(2)}) copy-start(s32[32]{0:T(128)} %param.15) | copy-start | bytes 388
  15.7 12.4 %copy-start.8 = (s32[32]{0:T(128)S(1)}, s32[32]{0:T(128)}, u32[]{:S(2)}) copy-start(s32[32]{0:T(128)} %param.12) | copy-start | bytes 388
  15.7 201.5 %all-to-all-start = ((bf16[32,2,2,128,256]{4,3,2,1,0:T(8,128)(2,1)}), bf16[32,2,2,128,256]{4,3,2,1,0:T(8,128)(2,1)}, u32[]{:S(2)}, u32[]{:S(2)}) async-start(bf16[32,2,2,128,256]{4,3,2,1,0:T(8,128)(2,1)} %bitcast.42), calls=%async_computation | async-start | bytes 16777216 | tf_op jit(solution)/shard_map/all_to_all | solution.py:113
  27.5 273.6 %reduce-scatter.2.cloned.1.call-start = ((), (), s32[]{:S(2)}) async-start(), calls=%async_computation.2 | async-start | bytes 4718592 | tf_op jit(solution)/shard_map/reduce_scatter | solution.py:140
  27.5 4.1 %copy-start.4 = (bf16[1024,2048]{1,0:T(8,128)(2,1)S(1)}, bf16[1024,2048]{1,0:T(8,128)(2,1)}, u32[]{:S(2)}) copy-start(bf16[1024,2048]{1,0:T(8,128)(2,1)} %param.8) | copy-start | bytes 12582916
  36.9 1.6 copy-start.5
  223.3 1.0 copy-start.1
  224.4 1.0 copy-start.2
  225.4 1.0 copy-start.3
  226.5 25.7 %copy-start.6 = (bf16[256,2048]{1,0:T(8,128)(2,1)S(1)}, bf16[256,2048]{1,0:T(8,128)(2,1)}, u32[]{:S(2)}) copy-start(bf16[256,2048]{1,0:T(8,128)(2,1)} %param.10) | copy-start | bytes 3145732
Sparse Core Ops, SparseCore 0:
  255.5 45.5 reduce-scatter.1

commit v3 on v2

--- a/solution.py
+++ b/solution.py
@@ -12,6 +12,8 @@
 PAGE = 128
 MAXP = 32
 BLOCK_Q = 256
+RELAY_A = 8
+RELAY_B = 1
 
 
 def rotate(feature, position):
@@ -96,24 +98,7 @@
     )(live, query, pages, pages, new_key, new_value)
 
 
-def body(hidden_in, qkv_weight, out_weight, kv_pool, cached_len, page_slot, page_holder, cont_flag):
-    req_count = lax.axis_size("req")
-    req_index = lax.axis_index("req")
-    local_reqs = hidden_in.shape[0] // NEW
-    local_width = qkv_weight.shape[2]
-    local_heads = local_width // HD
-    table_block = local_reqs * MAXP
-    capacity = max(2, 2 * table_block // req_count)
-    holder_rows = page_holder[:, :, 0]
-    held_here = holder_rows == req_index
-    ranking = jnp.cumsum(held_here.astype(jnp.int32), axis=1) - 1
-    picked = held_here[:, :, None] & (ranking[:, :, None] == jnp.arange(capacity)[None, None, :])
-    send_slots = jnp.sum(jnp.where(picked, page_slot[:, :, None], 0), axis=1)
-    outgoing = kv_pool[send_slots]
-    incoming = lax.all_to_all(outgoing, "req", split_axis=0, concat_axis=0, tiled=True)
-    lengths = lax.dynamic_slice_in_dim(cached_len, req_index * local_reqs, local_reqs)
-    flags = lax.dynamic_slice_in_dim(cont_flag, req_index * local_reqs, local_reqs)
-    live_len = lengths * flags
+def project(hidden_in, qkv_weight, live_len, local_heads, local_width):
     token_rows = hidden_in.astype(jnp.float32)
     centre = jnp.mean(token_rows, axis=-1, keepdims=True)
     centred = token_rows - centre
@@ -128,14 +113,107 @@
         jnp.bfloat16
     ).reshape(-1, local_width)
     new_value = united_qkv[:, 2].astype(jnp.bfloat16)
-    own_holders = lax.dynamic_index_in_dim(holder_rows, req_index, 0, keepdims=False)
-    same_holder = own_holders[:, None] == own_holders[None, :]
-    earlier = jnp.arange(table_block)[None, :] < jnp.arange(table_block)[:, None]
-    own_rank = jnp.sum((same_holder & earlier).astype(jnp.int32), axis=1)
-    fetched = incoming.reshape(req_count * capacity, 2, PAGE, local_width)[
+    return query_rot, new_key, new_value
+
+
+def exchange_wide(kv_pool, page_slot, holder_rows, rank_all, req_index, req_count):
+    capacity = 2
+    held_here = holder_rows == req_index
+    ranking = jnp.cumsum(held_here.astype(jnp.int32), axis=1) - 1
+    picked = held_here[:, :, None] & (ranking[:, :, None] == jnp.arange(capacity)[None, None, :])
+    send_slots = jnp.sum(jnp.where(picked, page_slot[:, :, None], 0), axis=1)
+    incoming = lax.all_to_all(kv_pool[send_slots], "req", split_axis=0, concat_axis=0, tiled=True)
+    own_holders = holder_rows[req_index]
+    own_rank = rank_all[req_index]
+    return incoming.reshape((req_count * capacity,) + kv_pool.shape[1:])[
         own_holders * capacity + own_rank
     ]
-    attended = attend(live_len[:1], query_rot, fetched, new_key, new_value)
+
+
+def exchange_relay(kv_pool, page_slot, holder_rows, rank_all, req_index, req_count):
+    rows, entries = holder_rows.shape
+    spill = rank_all > 0
+    frag = PAGE // req_count
+    spill_flat = spill.reshape(-1)
+    holders_flat = holder_rows.reshape(-1)
+    slots_flat = page_slot.reshape(-1)
+    by_holder = (holders_flat[:, None] == jnp.arange(req_count)[None, :]) & spill_flat[:, None]
+    by_holder = by_holder.astype(jnp.int32)
+    holder_order = jnp.sum((jnp.cumsum(by_holder, axis=0) - by_holder) * by_holder, axis=1)
+    spill_i = spill.astype(jnp.int32)
+    req_order = jnp.cumsum(spill_i, axis=1) - spill_i
+    wanted = jnp.arange(RELAY_A)
+    match_a = (
+        spill_flat[None, :]
+        & (holders_flat[None, :] == req_index)
+        & (holder_order[None, :] == wanted[:, None])
+    )
+    slot_a = jnp.sum(jnp.where(match_a, slots_flat[None, :], 0), axis=1)
+    pages_a = kv_pool[slot_a]
+    pieces = pages_a.reshape(RELAY_A, 2, req_count, frag, -1).transpose(2, 0, 1, 3, 4)
+    relayed = lax.all_to_all(pieces, "req", split_axis=0, concat_axis=0, tiled=True)
+    relayed = relayed.reshape((req_count * RELAY_A, 2, frag, relayed.shape[-1]))
+    match_b = spill[:, None, :] & (req_order[:, None, :] == jnp.arange(RELAY_B)[None, :, None])
+    src_holder = jnp.sum(jnp.where(match_b, holder_rows[:, None, :], 0), axis=2)
+    src_index = jnp.sum(
+        jnp.where(match_b, holder_order.reshape(rows, entries)[:, None, :], 0), axis=2
+    )
+    extra = relayed[src_holder * RELAY_A + jnp.clip(src_index, 0, RELAY_A - 1)]
+    extra = extra.transpose(0, 2, 1, 3, 4).reshape(rows, 2, RELAY_B * frag, -1)
+    first_hit = (holder_rows == req_index) & (rank_all == 0)
+    send_slots = jnp.sum(jnp.where(first_hit, page_slot, 0), axis=1)
+    outgoing = jnp.concatenate([kv_pool[send_slots], extra], axis=2)
+    incoming = lax.all_to_all(outgoing, "req", split_axis=0, concat_axis=0, tiled=True)
+    first_pages = incoming[:, :, :PAGE]
+    spill_pages = (
+        incoming[:, :, PAGE:]
+        .reshape(req_count, 2, RELAY_B, frag, -1)
+        .transpose(2, 1, 0, 3, 4)
+        .reshape(RELAY_B, 2, PAGE, -1)
+    )
+    source = jnp.concatenate([first_pages, spill_pages], axis=0)
+    own_holders = holder_rows[req_index]
+    pick = jnp.where(
+        rank_all[req_index] == 0,
+        own_holders,
+        req_count + jnp.clip(req_order[req_index], 0, RELAY_B - 1),
+    )
+    return source[pick]
+
+
+def body(hidden_in, qkv_weight, out_weight, kv_pool, cached_len, page_slot, page_holder, cont_flag):
+    req_count = lax.axis_size("req")
+    req_index = lax.axis_index("req")
+    local_width = qkv_weight.shape[2]
+    local_heads = local_width // HD
+    holder_rows = page_holder[:, :, 0]
+    entries = holder_rows.shape[1]
+    same_holder = holder_rows[:, :, None] == holder_rows[:, None, :]
+    earlier = jnp.arange(entries)[None, None, :] < jnp.arange(entries)[None, :, None]
+    rank_all = jnp.sum((same_holder & earlier).astype(jnp.int32), axis=2)
+    spill = (rank_all > 0).astype(jnp.int32)
+    relay_fits = (jnp.max(jnp.sum(spill, axis=1)) <= RELAY_B) & (
+        jnp.max(jnp.sum(spill[:, :, None] * (holder_rows[:, :, None] == jnp.arange(req_count)), axis=(0, 1)))
+        <= RELAY_A
+    )
+    lengths = lax.dynamic_slice_in_dim(cached_len, req_index, 1)
+    flags = lax.dynamic_slice_in_dim(cont_flag, req_index, 1)
+    live_len = lengths * flags
+    operands = (hidden_in, qkv_weight, kv_pool, page_slot, holder_rows, rank_all, live_len)
+
+    def branch(exchange):
+        def run(ops):
+            hidden, weight, pool, slots, holders, ranks, live = ops
+            fetched = exchange(pool, slots, holders, ranks, req_index, req_count)
+            query_rot, new_key, new_value = project(hidden, weight, live, local_heads, local_width)
+            return fetched, query_rot, new_key, new_value
+
+        return run
+
+    fetched, query_rot, new_key, new_value = lax.cond(
+        relay_fits, branch(exchange_relay), branch(exchange_wide), operands
+    )
+    attended = attend(live_len, query_rot, fetched, new_key, new_value)
     head_term = jnp.dot(attended, out_weight, preferred_element_type=jnp.float32)
     return lax.psum_scatter(head_term.astype(jnp.bfloat16), "tp", scatter_dimension=0, tiled=True)
 

time: 309 us -> 281 us (0.909)
  waiting for transfers between devices: 194 us -> 144 us
  other arithmetic: 15.4 us -> 26.4 us
  starting transfers between devices: 11.8 us -> 17.5 us
  local copies, waits for them, and re-layouts: 39.5 us -> 42.7 us
    all_to_all x1 -> x2, waiting for transfers between devices: 148 us -> 104 us  [the longest x1 79.4 us: exchange_relay(): lax.all_to_all(outgoing, 'req', split_axis=0, concat_axis=0, tiled=True)]
    unnamed x25 -> x2, local copies, waits for them, and re-layouts: 17.2 us -> 0.01 us
    concatenate x0 -> x1, local copies, waits for them, and re-layouts: none -> 7.64 us  [exchange_relay(): outgoing = jnp.concatenate([kv_pool[send_slots], extra], axis=2)]
    concatenate x0 -> x2, other arithmetic: none -> 6.96 us  [the longest x1 4.6 us: exchange_relay(): outgoing = jnp.concatenate([kv_pool[send_slots], extra], axis=2)]
    all_to_all x1 -> x2, starting transfers between devices: 11.7 us -> 17.5 us  [the longest x1 11.7 us: exchange_relay(): lax.all_to_all(pieces, 'req', split_axis=0, concat_axis=0, tiled=True)]
    another operation x3 -> x5, other arithmetic: 3.99 us -> 9.7 us
    reduce_scatter x1, waiting for transfers between devices: 45.7 us -> 40.1 us  [body(): lax.psum_scatter(head_term.astype(jnp.bfloat16), 'tp', scatter_dimension=...]
    another operation x0 -> x23, local copies, waits for them, and re-layouts: none -> 5.56 us
  transfers between devices with their start and end apart: 2 -> 3, of which waited for: 2 -> 3; matrix products, arithmetic and copies ran while one was open for 13% -> 6% of each run, Pallas kernels for 0% -> 0%
where the time goes in v3:
time: 281 us; the launch traced here: 280 us
  waiting for transfers between devices  144 us (51%)
  local copies, waits for them, and re-layouts  42.7 us (15%)
  other arithmetic  26.4 us (9%)
  Pallas kernels  25.6 us (9%)
  starting transfers between devices  17.5 us (6%)
  between operations  15.9 us (6%)
  matrix products  7.32 us (3%)
    all_to_all x1, waiting for transfers between devices, exchange_relay(): lax.all_to_all(outgoing, 'req', split_axis=0, concat_axis=0, tiled=True)  79.4 us
    reduce_scatter x1, waiting for transfers between devices, body(): lax.psum_scatter(head_term.astype(jnp.bfloat16), 'tp', scatter_dimension=...  40.1 us
    pallas_call x1, Pallas kernels, attend(): pl.pallas_call(attend_kernel, grid_spec=grid_spec, out_shape=jax.ShapeDty...  25.6 us
    all_to_all x1, waiting for transfers between devices, exchange_relay(): lax.all_to_all(pieces, 'req', split_axis=0, concat_axis=0, tiled=True)  24.8 us
    all_to_all x1, starting transfers between devices, exchange_relay(): lax.all_to_all(pieces, 'req', split_axis=0, concat_axis=0, tiled=True)  11.7 us
    another operation x4, other arithmetic  9.51 us
    concatenate x1, local copies, waits for them, and re-layouts, exchange_relay(): outgoing = jnp.concatenate([kv_pool[send_slots], extra], axis=2)  7.64 us
    all_to_all x1, starting transfers between devices, exchange_relay(): lax.all_to_all(outgoing, 'req', split_axis=0, concat_axis=0, tiled=True)  5.83 us
  transfers between devices with their start and end apart: 3, of which 3 were waited for; matrix products, arithmetic and copies ran while one was open for 6% of the time, Pallas kernels for 0%

profile of v3, /device:TPU:2, one launch (start us, length us, event | category | flops | bytes accessed | tf_op | source)
XLA Modules:
  0.0 280.2 jit_solution(9759243752046524947)
XLA Ops:
  6.5 1.6 convert_reduce_fusion.2
  8.3 1.2 dynamic_slice.21
  9.5 1.2 dynamic_slice.22
  12.0 1.1 select_reduce_fusion.5
  15.5 188.9 %conditional.3 = (bf16[32,2,128,256]{3,2,1,0:T(8,128)(2,1)}, bf16[1024,256]{1,0:T(8,128)(2,1)S(1)}, bf16[1024,256]{1,0:T(8,128)(2,1)S(1)}, bf16[1024,256]{1,0:T(8,128)(2,1)S(1)}) conditional(s32[]{:T(128)} %convert_element_type.124, (s32[]{:T(128)}, s32[32,32]{1,0:T(8,128)}, s32[32,32]{1,0:T(8,128)}, bf16[16,2,128,256]{3,2,1,0:T(8,128)(2,1)}, ...), branch_computations={%region_5.10_spmd, %region_10.21_spmd} | conditional | flops 3261850112 | bytes 175990176
  18.3 9.0 %reduce-window.4 = s32[32,8,128]{2,1,0:T(8,128)S(1)} reduce-window(s32[32,8,128]{2,1,0:T(8,128)S(1)} %fusion.27, s32[]{:T(128)} %constant.40.clone), window={size=1x1x128 pad=0_0x0_0x127_0}, to_apply=%region_12.12 | reduce-window | flops 4161536 | bytes 262148 | tf_op jit(solution)/shard_map/reduce-window
  28.0 3.3 %gather_fusion.3 = bf16[8,2,128,256]{3,2,1,0:T(8,128)(2,1)} fusion(bf16[16,2,128,256]{3,2,1,0:T(8,128)(2,1)} %get-tuple-element.67, s32[1024]{0:T(1024)S(1)} %pad_clamp_fusion.4), kind=kCustom, calls=%fused_computation.3 | custom fusion | bytes 2097184 | tf_op jit(solution)/shard_map/cond/branch_1_fun/gather | solution.py:152
  31.3 1.8 copy.92
  33.1 1.1 copy.93
  34.3 11.7 %all-to-all-start.1 = ((bf16[32,8,2,4,256]{4,1,3,2,0:T(8,128)(2,1)}), bf16[32,8,2,4,256]{4,1,3,2,0:T(8,128)(2,1)}, u32[]{:S(2)}, u32[]{:S(2)}) async-start(bf16[32,8,2,4,256]{4,1,3,2,0:T(8,128)(2,1)} %copy.93), calls=%async_computation.1 | async-start | bytes 2097152 | tf_op jit(solution)/shard_map/cond/branch_1_fun/all_to_all | solution.py:154
  46.4 2.8 gather_fusion.2
  49.3 24.8 %all-to-all-done.1 = bf16[32,8,2,4,256]{4,1,3,2,0:T(8,128)(2,1)} async-done(((bf16[32,8,2,4,256]{4,1,3,2,0:T(8,128)(2,1)}), bf16[32,8,2,4,256]{4,1,3,2,0:T(8,128)(2,1)}, u32[]{:S(2)}, u32[]{:S(2)}) %all-to-all-start.1) | async-done | bytes 1048608 | tf_op jit(solution)/shard_map/cond/branch_1_fun/all_to_all | solution.py:154
  74.1 1.3 copy.117
  76.8 4.6 %pad_maximum_fusion.2 = bf16[32,2,132,256]{3,2,1,0:T(8,128)(2,1)} fusion(bf16[32,2,4,256]{3,2,1,0:T(4,128)(2,1)S(1)} %gather_fusion.4, bf16[32,2,128,256]{3,2,1,0:T(8,128)(2,1)} %gather_fusion.2), kind=kLoop, calls=%fused_computation.46 | loop fusion | flops 8650752 | bytes 8650752 | tf_op jit(solution)/shard_map/cond/branch_1_fun/concatenate | solution.py:165
  81.4 7.6 %copy.96 = bf16[32,2,132,256]{3,1,2,0:T(2,128)(2,1)} copy(bf16[32,2,132,256]{3,2,1,0:T(8,128)(2,1)} %pad_maximum_fusion.2) | data formatting | bytes 8650752 | tf_op jit(solution)/shard_map/cond/branch_1_fun/concatenate | solution.py:165
  89.1 5.8 %all-to-all-start.2 = ((bf16[32,2,132,256]{3,1,2,0:T(2,128)(2,1)}), bf16[32,2,132,256]{3,1,2,0:T(2,128)(2,1)}, u32[]{:S(2)}, u32[]{:S(2)}) async-start(bf16[32,2,132,256]{3,1,2,0:T(2,128)(2,1)} %copy.96), calls=%async_computation.2 | async-start | bytes 8650752 | tf_op jit(solution)/shard_map/cond/branch_1_fun/all_to_all | solution.py:166
  95.0 3.0 %convert_reduce_fusion.1 = f32[1024]{0:T(1024)S(1)} fusion(bf16[1024,2048]{1,0:T(8,128)(2,1)} %get-tuple-element.73), kind=kLoop, calls=%fused_computation.41 | loop fusion | flops 4193280 | bytes 4198400 | tf_op jit(solution)/shard_map/cond/branch_1_fun/reduce_sum | solution.py:103
  98.4 1.2 fusion.14
  99.6 1.0 multiply_cosine_fusion.1
  100.6 4.1 %fusion.17 = f32[1024,3,256]{0,2,1:T(8,128)S(1)} fusion(bf16[2048,3,256]{2,0,1:T(8,128)(2,1)S(1)} %copy-done.11, bf16[1024,2048]{1,0:T(8,128)(2,1)S(1)} %copy-done.3, f32[1024]{0:T(1024)S(1)} %add_rsqrt_fusion.1, f32[1024]{0:T(1024)S(1)} %broadcast_multiply_fusion.1), kind=kOutput, calls=%fused_computation.49 | convolution fusion | flops 3229614080 | bytes 10493952 | tf_op jit(solution)/shard_map/cond/branch_1_fun/td,dcf->tcf/dot_general | solution.py:107
  105.4 1.1 copy-done.5
  106.5 1.0 copy.108
  107.5 1.0 copy.110
  108.5 1.3 fusion.21
  110.1 79.4 %all-to-all-done.2 = bf16[32,2,132,256]{3,1,2,0:T(2,128)(2,1)} async-done(((bf16[32,2,132,256]{3,1,2,0:T(2,128)(2,1)}), bf16[32,2,132,256]{3,1,2,0:T(2,128)(2,1)}, u32[]{:S(2)}, u32[]{:S(2)}) %all-to-all-start.2) | async-done | bytes 4325408 | tf_op jit(solution)/shard_map/cond/branch_1_fun/all_to_all | solution.py:166
  189.5 1.0 slice.78
  190.5 5.6 %slice.77 = bf16[32,2,128,256]{3,1,2,0:T(2,128)(2,1)S(1)} slice(bf16[32,2,132,256]{3,1,2,0:T(2,128)(2,1)} %all-to-all-done.2), slice={[0:32], [0:2], [0:128], [0:256]} | slice | bytes 8388608 | tf_op jit(solution)/shard_map/cond/branch_1_fun/slice | solution.py:167
  196.9 2.4 pad_maximum_fusion.3
  199.3 5.1 %gather_fusion.5 = bf16[32,2,128,256]{3,2,1,0:T(8,128)(2,1)} fusion(bf16[33,2,128,256]{3,2,1,0:T(8,128)(2,1)} %pad_maximum_fusion.3, s32[1024]{0:T(1024)S(1)} %pad_clamp_fusion.2), kind=kCustom, calls=%fused_computation.5 | custom fusion | bytes 8388736 | tf_op jit(solution)/shard_map/cond/branch_1_fun/gather | solution.py:181
  204.4 25.6 %shard_map.82 = bf16[1024,256]{1,0:T(8,128)(2,1)S(1)} custom-call(s32[1]{0:T(128)} %mul.244.live_ref, bf16[1024,256]{1,0:T(8,128)(2,1)S(1)} %get-tuple-element.203.q_ref, bf16[32,2,128,256]{3,2,1,0:T(8,128)(2,1)} %get-tuple-element.81.ck_ref.cv_ref, bf16[32,2,128,256]{3,2,1,0:T(8,128)(2,1)} %get-tuple-element.81.ck_ref.cv_ref, ...), custom_call_target="tpu_custom_call" | custom-call | flops 5368709120 | bytes 6291456 | tf_op jit(solution)/shard_map/pallas_call | solution.py:88
  230.0 3.2 %convolution_convert_fusion = bf16[1024,2048]{1,0:T(8,128)(2,1)} fusion(bf16[1024,256]{1,0:T(8,128)(2,1)S(1)} %shard_map.82, bf16[256,2048]{1,0:T(8,128)(2,1)S(1)} %copy-done), kind=kOutput, calls=%fused_computation.105 | convolution fusion | flops 1075838976 | bytes 5767168 | tf_op jit(solution)/shard_map/dot_general | solution.py:217
  233.2 40.1 %reduce-scatter.2.cloned.1.call-done = bf16[128,2048]{1,0:T(8,128)(2,1)} async-done(((bf16[1024,2048]{1,0:T(8,128)(2,1)}), bf16[128,2048]{1,0:T(8,128)(2,1)}) %reduce-scatter.2.cloned.1.call-update) | async-done | bytes 524304 | tf_op jit(solution)/shard_map/reduce_scatter | solution.py:218
  (64 shorter events, 8.8 us)
Async XLA Ops:
  6.5 223.5 %copy-start = (bf16[256,2048]{1,0:T(8,128)(2,1)S(1)}, bf16[256,2048]{1,0:T(8,128)(2,1)}, u32[]{:S(2)}) copy-start(bf16[256,2048]{1,0:T(8,128)(2,1)} %param.12) | copy-start | bytes 3145732
  6.5 266.8 %reduce-scatter.2.cloned.1.call-start = ((), (), s32[]{:S(2)}) async-start(), calls=%async_computation.4 | async-start | bytes 4718592 | tf_op jit(solution)/shard_map/reduce_scatter | solution.py:218
  27.9 18.3 %copy-start.6 = (s32[32,32,1]{1,2,0:T(1,128)S(1)}, s32[32,32,1]{1,2,0:T(1,128)}, u32[]{:S(2)}) copy-start(s32[32,32,1]{1,2,0:T(1,128)} %get-tuple-element.199) | copy-start | bytes 12292 | tf_op jit(solution)/shard_map/conditional.1
  28.0 18.2 %copy-start.9 = (s32[32,32]{1,0:T(8,128)S(1)}, s32[32,32]{1,0:T(8,128)}, u32[]{:S(2)}) copy-start(s32[32,32]{1,0:T(8,128)} %get-tuple-element.71) | copy-start | bytes 12292 | tf_op jit(solution)/shard_map/conditional.1
  28.0 18.4 %copy-start.1 = (bf16[16,2,128,256]{3,2,1,0:T(8,128)(2,1)S(1)}, bf16[16,2,128,256]{3,2,1,0:T(8,128)(2,1)}, u32[]{:S(2)}) copy-start(bf16[16,2,128,256]{3,2,1,0:T(8,128)(2,1)} %get-tuple-element.67) | copy-start | bytes 6291460 | tf_op jit(solution)/shard_map/conditional.1
  34.3 39.8 %all-to-all-start.1 = ((bf16[32,8,2,4,256]{4,1,3,2,0:T(8,128)(2,1)}), bf16[32,8,2,4,256]{4,1,3,2,0:T(8,128)(2,1)}, u32[]{:S(2)}, u32[]{:S(2)}) async-start(bf16[32,8,2,4,256]{4,1,3,2,0:T(8,128)(2,1)} %copy.93), calls=%async_computation.1 | async-start | bytes 2097152 | tf_op jit(solution)/shard_map/cond/branch_1_fun/all_to_all | solution.py:154
  89.1 100.4 %all-to-all-start.2 = ((bf16[32,2,132,256]{3,1,2,0:T(2,128)(2,1)}), bf16[32,2,132,256]{3,1,2,0:T(2,128)(2,1)}, u32[]{:S(2)}, u32[]{:S(2)}) async-start(bf16[32,2,132,256]{3,1,2,0:T(2,128)(2,1)} %copy.96), calls=%async_computation.2 | async-start | bytes 8650752 | tf_op jit(solution)/shard_map/cond/branch_1_fun/all_to_all | solution.py:166
  94.9 3.5 %copy-start.3 = (bf16[1024,2048]{1,0:T(8,128)(2,1)S(1)}, bf16[1024,2048]{1,0:T(8,128)(2,1)}, u32[]{:S(2)}) copy-start(bf16[1024,2048]{1,0:T(8,128)(2,1)} %get-tuple-element.73) | copy-start | bytes 12582916 | tf_op jit(solution)/shard_map/conditional.1
  95.0 5.7 %copy-start.11 = (bf16[2048,3,256]{2,0,1:T(8,128)(2,1)S(1)}, bf16[2048,3,256]{2,0,1:T(8,128)(2,1)}, u32[]{:S(2)}) copy-start(bf16[2048,3,256]{2,0,1:T(8,128)(2,1)} %get-tuple-element.201) | copy-start | bytes 9437188 | tf_op jit(solution)/shard_map/conditional.1
  104.8 1.7 copy-start.5
  199.3 5.1 %copy-start.7 = (bf16[1024,256]{1,0:T(8,128)(2,1)S(1)}, bf16[1024,256]{1,0:T(8,128)(2,1)}, u32[]{:S(2)}) copy-start(bf16[1024,256]{1,0:T(8,128)(2,1)} %copy.108) | copy-start | bytes 1572868 | tf_op jit(solution)/shard_map/conditional.1
  199.3 5.1 %copy-start.8 = (bf16[1024,256]{1,0:T(8,128)(2,1)S(1)}, bf16[1024,256]{1,0:T(8,128)(2,1)}, u32[]{:S(2)}) copy-start(bf16[1024,256]{1,0:T(8,128)(2,1)} %copy.110) | copy-start | bytes 1572868 | tf_op jit(solution)/shard_map/conditional.1
Sparse Core Ops, SparseCore 0:
  233.3 39.9 reduce-scatter.1

commit v4 on v3

v4 whole, which is shorter than its diff:
```python
import functools

import jax
import jax.numpy as jnp
from jax import lax
from jax.experimental import pallas as pl
from jax.experimental.pallas import tpu as pltpu
from jax.sharding import PartitionSpec as P

HD = 128
NEW = 1024
PAGE = 128
MAXP = 32
BLOCK_Q = 256
RELAY_A = 8
RELAY_B = 1


def rotate(feature, position):
    half_width = feature.shape[-1] // 2
    indices = jnp.arange(half_width).astype(jnp.float32)
    inverse = jnp.exp(indices * (-2.0 / feature.shape[-1]) * jnp.log(jnp.float32(10000.0)))
    angles = position[:, None, None] * inverse[None, None, :]
    cosine = jnp.cos(angles)
    sine_part = jnp.sin(angles)
    first_half = feature[..., :half_width]
    second_half = feature[..., half_width:]
    return jnp.concatenate(
        [
            first_half * cosine - second_half * sine_part,
            second_half * cosine + first_half * sine_part,
        ],
        axis=-1,
    )


def attend_kernel(
    live_ref, kpm_ref, kpe_ref, q_ref, mk_ref, mv_ref, ek_ref, ev_ref, nk_ref, nv_ref, out_ref
):
    block = pl.program_id(1)
    live = live_ref[0]
    main_span = mk_ref.shape[0] * mk_ref.shape[1]
    extra_span = ek_ref.shape[0] * ek_ref.shape[1]
    query = q_ref[...]
    contract = (((1,), (1,)), ((), ()))
    scale = HD ** (-0.5)

    def scores(keys):
        return lax.dot_general(query, keys, contract, preferred_element_type=jnp.float32) * scale

    main_scores = scores(mk_ref[...].reshape(main_span, HD))
    extra_scores = scores(ek_ref[...].reshape(extra_span, HD))
    new_scores = scores(nk_ref[...])
    main_ok = kpm_ref[...] < live
    extra_ok = kpe_ref[...] < live
    query_pos = block * BLOCK_Q + lax.broadcasted_iota(jnp.int32, new_scores.shape, 0)
    new_ok = lax.broadcasted_iota(jnp.int32, new_scores.shape, 1) <= query_pos
    main_scores = jnp.where(main_ok, main_scores, -1e30)
    extra_scores = jnp.where(extra_ok, extra_scores, -1e30)
    new_scores = jnp.where(new_ok, new_scores, -1e30)
    row_top = jnp.maximum(
        jnp.maximum(
            jnp.max(main_scores, axis=1, keepdims=True),
            jnp.max(extra_scores, axis=1, keepdims=True),
        ),
        jnp.max(new_scores, axis=1, keepdims=True),
    )
    main_w = jnp.where(main_ok, jnp.exp(main_scores - row_top), 0.0)
    extra_w = jnp.where(extra_ok, jnp.exp(extra_scores - row_top), 0.0)
    new_w = jnp.where(new_ok, jnp.exp(new_scores - row_top), 0.0)
    row_total = (
        jnp.sum(main_w, axis=1, keepdims=True)
        + jnp.sum(extra_w, axis=1, keepdims=True)
        + jnp.sum(new_w, axis=1, keepdims=True)
    )

    def weighted(weights, values):
        return jnp.dot(weights.astype(jnp.bfloat16), values, preferred_element_type=jnp.float32)

    summed = (
        weighted(main_w, mv_ref[...].reshape(main_span, HD))
        + weighted(extra_w, ev_ref[...].reshape(extra_span, HD))
        + weighted(new_w, nv_ref[...])
    )
    out_ref[...] = (summed / row_total).astype(out_ref.dtype)


def attend(live, query, main_pages, main_pos, extra_pages, extra_pos, new_key, new_value):
    rows, width = query.shape
    heads = width // HD
    main_n = main_pages.shape[0]
    extra_n = extra_pages.shape[0]
    grid_spec = pltpu.PrefetchScalarGridSpec(
        num_scalar_prefetch=1,
        grid=(heads, rows // BLOCK_Q),
        in_specs=[
            pl.BlockSpec((1, main_n * PAGE), lambda h, b, live: (0, 0)),
            pl.BlockSpec((1, extra_n * PAGE), lambda h, b, live: (0, 0)),
            pl.BlockSpec((BLOCK_Q, HD), lambda h, b, live: (b, h)),
            pl.BlockSpec((main_n, None, PAGE, HD), lambda h, b, live: (0, 0, 0, h)),
            pl.BlockSpec((main_n, None, PAGE, HD), lambda h, b, live: (0, 1, 0, h)),
            pl.BlockSpec((extra_n, None, PAGE, HD), lambda h, b, live: (0, 0, 0, h)),
            pl.BlockSpec((extra_n, None, PAGE, HD), lambda h, b, live: (0, 1, 0, h)),
            pl.BlockSpec((rows, HD), lambda h, b, live: (0, h)),
            pl.BlockSpec((rows, HD), lambda h, b, live: (0, h)),
        ],
        out_specs=pl.BlockSpec((BLOCK_Q, HD), lambda h, b, live: (b, h)),
    )
    keys_n = (main_n + extra_n) * PAGE + rows
    return pl.pallas_call(
        attend_kernel,
        grid_spec=grid_spec,
        out_shape=jax.ShapeDtypeStruct((rows, width), jnp.bfloat16),
        compiler_params=pltpu.CompilerParams(vmem_limit_bytes=56 * 1024 * 1024),
        cost_estimate=pl.CostEstimate(
            flops=4 * rows * keys_n * width,
            transcendentals=rows * keys_n * heads,
            bytes_accessed=2 * (2 * keys_n * width + 2 * rows * width),
        ),
    )(
        live,
        main_pos.reshape(1, -1),
        extra_pos.reshape(1, -1),
        query,
        main_pages,
        main_pages,
        extra_pages,
        extra_pages,
        new_key,
        new_value,
    )


def key_positions(entry_of_slot):
    tokens = jnp.arange(PAGE)[None, :]
    return jnp.where(entry_of_slot[:, None] >= 0, entry_of_slot[:, None] * PAGE + tokens, 1 << 30)


def project(hidden_in, qkv_weight, live_len, local_heads, local_width):
    token_rows = hidden_in.astype(jnp.float32)
    centre = jnp.mean(token_rows, axis=-1, keepdims=True)
    centred = token_rows - centre
    spread = jnp.mean(centred * centred, axis=-1, keepdims=True)
    normed = (centred * lax.rsqrt(spread + 1e-05)).astype(jnp.bfloat16)
    united_qkv = jnp.einsum("td,dcf->tcf", normed, qkv_weight, preferred_element_type=jnp.float32)
    positions = (live_len[:, None] + jnp.arange(NEW)[None, :]).astype(jnp.float32).reshape(-1)
    query_rot = rotate(united_qkv[:, 0].reshape(-1, local_heads, HD), positions).astype(
        jnp.bfloat16
    ).reshape(-1, local_width)
    new_key = rotate(united_qkv[:, 1].reshape(-1, local_heads, HD), positions).astype(
        jnp.bfloat16
    ).reshape(-1, local_width)
    new_value = united_qkv[:, 2].astype(jnp.bfloat16)
    return query_rot, new_key, new_value


def exchange_wide(kv_pool, page_slot, holder_rows, rank_all, req_index, req_count):
    capacity = 2
    held_here = holder_rows == req_index
    ranking = jnp.cumsum(held_here.astype(jnp.int32), axis=1) - 1
    picked = held_here[:, :, None] & (ranking[:, :, None] == jnp.arange(capacity)[None, None, :])
    send_slots = jnp.sum(jnp.where(picked, page_slot[:, :, None], 0), axis=1)
    incoming = lax.all_to_all(kv_pool[send_slots], "req", split_axis=0, concat_axis=0, tiled=True)
    incoming = incoming.reshape((req_count * capacity,) + kv_pool.shape[1:])
    own_holders = holder_rows[req_index]
    own_rank = rank_all[req_index]
    slot_of_entry = own_holders * capacity + own_rank
    hit = slot_of_entry[None, :] == jnp.arange(req_count * capacity)[:, None]
    entry_of_slot = jnp.max(jnp.where(hit, jnp.arange(hit.shape[1])[None, :], -1), axis=1)
    main_pos = key_positions(entry_of_slot)
    extra_pages = incoming[:1]
    extra_pos = key_positions(jnp.full((1,), -1, jnp.int32))
    return incoming, main_pos, extra_pages, extra_pos


def exchange_relay(kv_pool, page_slot, holder_rows, rank_all, req_index, req_count):
    rows, entries = holder_rows.shape
    spill = rank_all > 0
    frag = PAGE // req_count
    width = kv_pool.shape[-1]
    spill_flat = spill.reshape(-1)
    holders_flat = holder_rows.reshape(-1)
    slots_flat = page_slot.reshape(-1)
    spill_i = spill.astype(jnp.int32)
    named = (holder_rows[:, :, None] == jnp.arange(req_count)[None, None, :]).astype(jnp.int32)
    row_spills = jnp.sum(spill_i[:, :, None] * named, axis=1)
    before = jnp.cumsum(row_spills, axis=0) - row_spills
    holder_order = jnp.sum(named * before[:, None, :], axis=2).reshape(-1)
    req_order = jnp.cumsum(spill_i, axis=1) - spill_i
    first_hit = (holder_rows == req_index) & (rank_all == 0)
    send_slots = jnp.sum(jnp.where(first_hit, page_slot, 0), axis=1)
    wanted = jnp.arange(RELAY_A)
    match_a = (
        spill_flat[None, :]
        & (holders_flat[None, :] == req_index)
        & (holder_order[None, :] == wanted[:, None])
    )
    slot_a = jnp.sum(jnp.where(match_a, slots_flat[None, :], 0), axis=1)
    pieces = (
        kv_pool[slot_a]
        .reshape(RELAY_A, 2, req_count, frag, width)
        .transpose(2, 1, 0, 3, 4)
        .reshape(req_count, 2, RELAY_A * frag, width)
    )
    outgoing = jnp.concatenate([kv_pool[send_slots], pieces], axis=2)
    incoming = lax.all_to_all(outgoing, "req", split_axis=0, concat_axis=0, tiled=True)
    relayed = (
        incoming[:, :, PAGE:]
        .reshape(req_count, 2, RELAY_A, frag, width)
        .transpose(0, 2, 1, 3, 4)
        .reshape(req_count * RELAY_A, 2, frag, width)
    )
    match_b = spill[:, None, :] & (req_order[:, None, :] == jnp.arange(RELAY_B)[None, :, None])
    src_holder = jnp.sum(jnp.where(match_b, holder_rows[:, None, :], 0), axis=2)
    src_index = jnp.sum(
        jnp.where(match_b, holder_order.reshape(rows, entries)[:, None, :], 0), axis=2
    )
    extra = relayed[src_holder * RELAY_A + jnp.clip(src_index, 0, RELAY_A - 1)]
    extra = extra.transpose(0, 2, 1, 3, 4).reshape(rows, 2, RELAY_B * frag, width)
    returned = lax.all_to_all(extra, "req", split_axis=0, concat_axis=0, tiled=True)
    extra_pages = (
        returned.reshape(req_count, 2, RELAY_B, frag, width)
        .transpose(2, 1, 0, 3, 4)
        .reshape(RELAY_B, 2, PAGE, width)
    )
    own_holders = holder_rows[req_index]
    own_first = rank_all[req_index] == 0
    entry_ids = jnp.arange(entries)
    main_hit = own_first[None, :] & (own_holders[None, :] == jnp.arange(req_count)[:, None])
    main_pos = key_positions(jnp.max(jnp.where(main_hit, entry_ids[None, :], -1), axis=1))
    extra_hit = (~own_first)[None, :] & (
        req_order[req_index][None, :] == jnp.arange(RELAY_B)[:, None]
    )
    extra_pos = key_positions(jnp.max(jnp.where(extra_hit, entry_ids[None, :], -1), axis=1))
    return incoming, main_pos, extra_pages, extra_pos


def body(hidden_in, qkv_weight, out_weight, kv_pool, cached_len, page_slot, page_holder, cont_flag):
    req_count = lax.axis_size("req")
    req_index = lax.axis_index("req")
    local_width = qkv_weight.shape[2]
    local_heads = local_width // HD
    holder_rows = page_holder[:, :, 0]
    entries = holder_rows.shape[1]
    same_holder = holder_rows[:, :, None] == holder_rows[:, None, :]
    earlier = jnp.arange(entries)[None, None, :] < jnp.arange(entries)[None, :, None]
    rank_all = jnp.sum((same_holder & earlier).astype(jnp.int32), axis=2)
    spill = (rank_all > 0).astype(jnp.int32)
    relay_fits = (jnp.max(jnp.sum(spill, axis=1)) <= RELAY_B) & (
        jnp.max(jnp.sum(spill[:, :, None] * (holder_rows[:, :, None] == jnp.arange(req_count)), axis=(0, 1)))
        <= RELAY_A
    )
    lengths = lax.dynamic_slice_in_dim(cached_len, req_index, 1)
    flags = lax.dynamic_slice_in_dim(cont_flag, req_index, 1)
    live_len = lengths * flags
    operands = (hidden_in, qkv_weight, kv_pool, page_slot, holder_rows, rank_all, live_len)

    def branch(exchange):
        def run(ops):
            hidden, weight, pool, slots, holders, ranks, live = ops
            main_pages, main_pos, extra_pages, extra_pos = exchange(
                pool, slots, holders, ranks, req_index, req_count
            )
            query_rot, new_key, new_value = project(hidden, weight, live, local_heads, local_width)
            return attend(
                live, query_rot, main_pages, main_pos, extra_pages, extra_pos, new_key, new_value
            )

        return run

    attended = lax.cond(relay_fits, branch(exchange_relay), branch(exchange_wide), operands)
    head_term = jnp.dot(attended, out_weight, preferred_element_type=jnp.float32)
    return lax.psum_scatter(head_term.astype(jnp.bfloat16), "tp", scatter_dimension=0, tiled=True)


def solution(mesh):
    in_specs = (
        P("req", None),
        P(None, None, "tp"),
        P("tp", None),
        P("req", None, None, "tp"),
        P(),
        P(),
        P(),
        P(),
    )
    out_specs = P(("req", "tp"), None)
    return jax.shard_map(body, mesh=mesh, in_specs=in_specs, out_specs=out_specs, check_vma=False)
```

time: 281 us -> 275 us (0.979)
  waiting for transfers between devices: 144 us -> 131 us
  local copies, waits for them, and re-layouts: 42.7 us -> 36.5 us
  loops' own time: 0.49 us -> 4.88 us
  other arithmetic: 26.4 us -> 29.4 us
    all_to_all x1, waiting for transfers between devices: 24.8 us -> 3.57 us  [exchange_relay(): lax.all_to_all(extra, 'req', split_axis=0, concat_axis=0, tiled=True)]
    cond x0 -> x21, local copies, waits for them, and re-layouts: none -> 11.2 us
    all_to_all x1, waiting for transfers between devices: 79.4 us -> 89.2 us  [exchange_relay(): lax.all_to_all(outgoing, 'req', split_axis=0, concat_axis=0, tiled=True)]
    reshape x3 -> x7, local copies, waits for them, and re-layouts: 0.9 us -> 9.23 us  [the longest x3 7.13 us: exchange_relay(): pieces = kv_pool[slot_a].reshape(RELAY_A, 2, req_count, frag, width).tran...]
    concatenate x1 -> x0, local copies, waits for them, and re-layouts: 7.64 us -> none  [exchange_relay(): outgoing = jnp.concatenate([kv_pool[send_slots], extra], axis=2)]
    gather x4 -> x2, local copies, waits for them, and re-layouts: 13 us -> 6.12 us  [the longest x1 3.39 us: exchange_relay(): kv_pool[slot_a].reshape(RELAY_A, 2, req_count, frag, width)]
    all_to_all x1, starting transfers between devices: 5.83 us -> 12.6 us  [exchange_relay(): lax.all_to_all(outgoing, 'req', split_axis=0, concat_axis=0, tiled=True)]
    another operation x4 -> x2, other arithmetic: 9.51 us -> 3.53 us
  transfers between devices with their start and end apart: 3 -> 3, of which waited for: 3 -> 3; matrix products, arithmetic and copies ran while one was open for 6% -> 12% of each run, Pallas kernels for 0% -> 0%
where the time goes in v4:
time: 275 us; the launch traced here: 272 us
  waiting for transfers between devices  131 us (48%)
  local copies, waits for them, and re-layouts  36.5 us (13%)
  other arithmetic  29.4 us (11%)
  Pallas kernels  26.7 us (10%)
  starting transfers between devices  19.3 us (7%)
  between operations  16.3 us (6%)
  matrix products  7.32 us (3%)
  loops' own time  4.88 us (2%)
    all_to_all x1, waiting for transfers between devices, exchange_relay(): lax.all_to_all(outgoing, 'req', split_axis=0, concat_axis=0, tiled=True)  89.2 us
    reduce_scatter x1, waiting for transfers between devices, body(): lax.psum_scatter(head_term.astype(jnp.bfloat16), 'tp', scatter_dimension=...  38.3 us
    pallas_call x1, Pallas kernels, attend(): pl.pallas_call(attend_kernel, grid_spec=grid_spec, out_shape=jax.ShapeDty...  26.7 us
    all_to_all x1, starting transfers between devices, exchange_relay(): lax.all_to_all(outgoing, 'req', split_axis=0, concat_axis=0, tiled=True)  12.6 us
    cond x21, local copies, waits for them, and re-layouts  11.2 us
    reshape x3, local copies, waits for them, and re-layouts, exchange_relay(): pieces = kv_pool[slot_a].reshape(RELAY_A, 2, req_count, frag, width).tran...  7.13 us
    all_to_all x1, starting transfers between devices, exchange_relay(): lax.all_to_all(extra, 'req', split_axis=0, concat_axis=0, tiled=True)  6.77 us
  transfers between devices with their start and end apart: 3, of which 3 were waited for; matrix products, arithmetic and copies ran while one was open for 12% of the time, Pallas kernels for 0%

profile of v4, /device:TPU:2, one launch (start us, length us, event | category | flops | bytes accessed | tf_op | source)
XLA Modules:
  0.0 271.6 jit_solution(16268028540249337002)
XLA Ops:
  6.6 1.3 dynamic_slice.22
  7.9 1.2 dynamic_slice.21
  10.4 1.6 convert_reduce_fusion.2
  15.9 207.1 %conditional.1 = (bf16[1024,256]{1,0:T(8,128)(2,1)S(1)}) conditional(s32[]{:T(128)} %convert_element_type.98, (s32[]{:T(128)}, s32[32,32]{1,0:T(8,128)}, s32[32,32]{1,0:T(8,128)S(1)}, bf16[1024,2048]{1,0:T(8,128)(2,1)}, bf16[2048,3,256]{2,0,1:T(8,128)(2,1)}, /*index=5*/s32[1]{0:T(128)}, s32[32,32]{1,0:T(8,128)}, ...), branch_computations={%region_5.11_spmd, %region_11.24_spmd} | conditional | flops 13044421632 | bytes 155676160 | solution.py:271
  22.7 1.5 select_reduce_fusion.2
  24.4 3.4 %gather_fusion.2 = bf16[8,2,128,256]{3,2,1,0:T(8,128)(2,1)} fusion(bf16[16,2,128,256]{3,2,1,0:T(8,128)(2,1)} %get-tuple-element.56, s32[1024]{0:T(1024)S(1)} %pad_clamp_fusion.2), kind=kCustom, calls=%fused_computation.2 | custom fusion | bytes 2097184 | tf_op jit(solution)/shard_map/cond/branch_1_fun/gather | solution.py:200
  27.8 2.2 reshape.477
  30.0 2.8 %copy.85 = bf16[8,2,32,4,256]{4,3,0,1,2:T(4,128)(2,1)} copy(bf16[8,2,32,4,256]{4,3,2,1,0:T(4,128)(2,1)} %reshape.477) | data formatting | bytes 2097152 | tf_op jit(solution)/shard_map/cond/branch_1_fun/reshape | solution.py:201
  32.8 2.1 reshape.478
  35.0 2.7 %gather_fusion.1 = bf16[32,2,128,256]{3,2,1,0:T(8,128)(2,1)} fusion(bf16[16,2,128,256]{3,2,1,0:T(8,128)(2,1)S(1)} %copy-done.1, s32[1024]{0:T(1024)S(1)} %pad_clamp_fusion.3), kind=kCustom, calls=%fused_computation.1 | custom fusion | bytes 8388736 | tf_op jit(solution)/shard_map/cond/branch_1_fun/gather | solution.py:205
  37.7 5.4 %pad_maximum_fusion.2 = bf16[32,2,160,256]{3,2,1,0:T(8,128)(2,1)} fusion(bf16[32,2,32,256]{3,2,1,0:T(8,128)(2,1)} %reshape.478, bf16[32,2,128,256]{3,2,1,0:T(8,128)(2,1)} %gather_fusion.1), kind=kLoop, calls=%fused_computation.48 | loop fusion | flops 10485760 | bytes 10485760 | tf_op jit(solution)/shard_map/cond/branch_1_fun/concatenate | solution.py:205
  43.1 12.6 %all-to-all-start.1 = ((bf16[32,2,160,256]{3,2,1,0:T(8,128)(2,1)}), bf16[32,2,160,256]{3,2,1,0:T(8,128)(2,1)}, u32[]{:S(2)}, u32[]{:S(2)}) async-start(bf16[32,2,160,256]{3,2,1,0:T(8,128)(2,1)} %pad_maximum_fusion.2), calls=%async_computation.1 | async-start | bytes 10485760 | tf_op jit(solution)/shard_map/cond/branch_1_fun/all_to_all | solution.py:206
  57.9 3.0 %convert_reduce_fusion.1 = f32[1024]{0:T(1024)S(1)} fusion(bf16[1024,2048]{1,0:T(8,128)(2,1)} %get-tuple-element.54), kind=kLoop, calls=%fused_computation.43 | loop fusion | flops 4193280 | bytes 4198400 | tf_op jit(solution)/shard_map/cond/branch_1_fun/reduce_sum | solution.py:141
  61.3 1.2 fusion.12
  62.6 4.1 %fusion.15 = f32[1024,3,256]{0,2,1:T(8,128)S(1)} fusion(bf16[2048,3,256]{2,0,1:T(8,128)(2,1)S(1)} %copy-done.10, bf16[1024,2048]{1,0:T(8,128)(2,1)S(1)} %copy-done.3, f32[1024]{0:T(1024)S(1)} %add_rsqrt_fusion.1, f32[1024]{0:T(1024)S(1)} %broadcast_multiply_fusion.2), kind=kOutput, calls=%fused_computation.50 | convolution fusion | flops 3229614080 | bytes 10493952 | tf_op jit(solution)/shard_map/cond/branch_1_fun/td,dcf->tcf/dot_general | solution.py:145
  66.9 1.2 fusion.33
  68.8 1.4 copy.69
  71.3 1.4 copy.67
  72.7 2.2 copy.68
  74.9 2.2 copy.66
  77.3 1.9 multiply_cosine_fusion.1
  79.2 3.5 %subtract_convert_fusion.2 = (bf16[1024,2,64]{2,1,0:T(2,128)(2,1)S(1)}, bf16[1024,2,64]{2,1,0:T(2,128)(2,1)S(1)}, bf16[1024,2,64]{2,1,0:T(2,128)(2,1)S(1)}, bf16[1024,2,64]{2,1,0:T(2,128)(2,1)S(1)}) fusion(f32[1024,2,64]{2,1,0:T(2,128)S(1)} %copy.69, f32[1024,2,64]{2,1,0:T(2,128)} %copy.68, f32[1024,64]{1,0:T(8,128)S(1)} %get-tuple-element.145, ...), kind=kLoop, calls=%fused_computation.56 | loop fusion | flops 2097152 | bytes 3670016 | tf_op jit(solution)/shard_map/convert.6
  82.6 3.7 %pad_maximum_fusion.3 = (bf16[1024,2,128]{2,1,0:T(2,128)(2,1)}, bf16[1024,2,128]{2,1,0:T(2,128)(2,1)}) fusion(bf16[1024,2,64]{2,1,0:T(2,128)(2,1)S(1)} %get-tuple-element.138, bf16[1024,2,64]{2,1,0:T(2,128)(2,1)S(1)} %get-tuple-element.139, bf16[1024,2,64]{2,1,0:T(2,128)(2,1)S(1)} %get-tuple-element.133, bf16[1024,2,64]{2,1,0:T(2,128)(2,1)S(1)} %get-tuple-element.132), kind=kLoop, calls=%fused_computation.63 | loop fusion | flops 2097152 | bytes 2097152 | tf_op jit(solution)/shard_map/cond/branch_1_fun/concatenate | solution.py:28
  86.3 89.2 %all-to-all-done.1.mk_ref.mv_ref = bf16[32,2,160,256]{3,2,1,0:T(8,128)(2,1)} async-done(((bf16[32,2,160,256]{3,2,1,0:T(8,128)(2,1)}), bf16[32,2,160,256]{3,2,1,0:T(8,128)(2,1)}, u32[]{:S(2)}, u32[]{:S(2)}) %all-to-all-start.1) | async-done | bytes 5242912 | tf_op jit(solution)/shard_map/cond/branch_1_fun/all_to_all | solution.py:206
  175.6 1.3 slice.69
  178.3 1.3 gather_fusion.3
  179.6 6.8 %all-to-all-start.2 = ((bf16[32,2,4,256]{3,2,1,0:T(4,128)(2,1)}), bf16[32,2,4,256]{3,2,1,0:T(4,128)(2,1)S(1)}, u32[]{:S(2)}, u32[]{:S(2)}) async-start(bf16[32,2,4,256]{3,2,1,0:T(4,128)(2,1)} %gather_fusion.3), calls=%async_computation.2 | async-start | bytes 262144 | tf_op jit(solution)/shard_map/cond/branch_1_fun/all_to_all | solution.py:220
  186.9 1.3 slice.73
  191.7 3.6 %all-to-all-done.2 = bf16[32,2,4,256]{3,2,1,0:T(4,128)(2,1)S(1)} async-done(((bf16[32,2,4,256]{3,2,1,0:T(4,128)(2,1)}), bf16[32,2,4,256]{3,2,1,0:T(4,128)(2,1)S(1)}, u32[]{:S(2)}, u32[]{:S(2)}) %all-to-all-start.2) | async-done | bytes 131104 | tf_op jit(solution)/shard_map/cond/branch_1_fun/all_to_all | solution.py:220
  196.0 26.7 %branch_1_fun.1 = bf16[1024,256]{1,0:T(8,128)(2,1)S(1)} custom-call(s32[1]{0:T(128)} %get-tuple-element.50.live_ref, s32[1,4096]{1,0:T(1,128)} %bitcast.113, s32[1,128]{1,0:T(1,128)} %broadcast_select_fusion.kpe_ref, bf16[1024,256]{1,0:T(8,128)(2,1)} %bitcast.109, bf16[32,2,160,256]{3,2,1,0:T(8,128)(2,1)} %all-to-all-done.1.mk_ref.mv_ref, ...), custom_call_target="tpu_custom_call" | custom-call | flops 5502926848 | bytes 6422528 | tf_op jit(solution)/shard_map/cond/branch_1_fun/pallas_call | solution.py:110
  223.0 3.2 %convolution_convert_fusion = bf16[1024,2048]{1,0:T(8,128)(2,1)} fusion(bf16[1024,256]{1,0:T(8,128)(2,1)S(1)} %get-tuple-element.149, bf16[256,2048]{1,0:T(8,128)(2,1)S(1)} %copy-done), kind=kOutput, calls=%fused_computation.106 | convolution fusion | flops 1075838976 | bytes 5767168 | tf_op jit(solution)/shard_map/dot_general | solution.py:272
  226.2 38.3 %reduce-scatter.2.cloned.1.call-done = bf16[128,2048]{1,0:T(8,128)(2,1)} async-done(((bf16[1024,2048]{1,0:T(8,128)(2,1)}), bf16[128,2048]{1,0:T(8,128)(2,1)}) %reduce-scatter.2.cloned.1.call-update) | async-done | bytes 524304 | tf_op jit(solution)/shard_map/reduce_scatter | solution.py:273
  (66 shorter events, 16.1 us)
Async XLA Ops:
  6.5 216.4 %copy-start = (bf16[256,2048]{1,0:T(8,128)(2,1)S(1)}, bf16[256,2048]{1,0:T(8,128)(2,1)}, u32[]{:S(2)}) copy-start(bf16[256,2048]{1,0:T(8,128)(2,1)} %param.12) | copy-start | bytes 3145732
  6.5 257.9 %reduce-scatter.2.cloned.1.call-start = ((), (), s32[]{:S(2)}) async-start(), calls=%async_computation.4 | async-start | bytes 4718592 | tf_op jit(solution)/shard_map/reduce_scatter | solution.py:273
  24.4 10.5 %copy-start.1 = (bf16[16,2,128,256]{3,2,1,0:T(8,128)(2,1)S(1)}, bf16[16,2,128,256]{3,2,1,0:T(8,128)(2,1)}, u32[]{:S(2)}) copy-start(bf16[16,2,128,256]{3,2,1,0:T(8,128)(2,1)} %get-tuple-element.56) | copy-start | bytes 6291460 | tf_op jit(solution)/shard_map/cond
  43.1 12.8 %copy-start.8 = (s32[32,32,1]{1,2,0:T(1,128)S(1)}, s32[32,32,1]{1,2,0:T(1,128)}, u32[]{:S(2)}) copy-start(s32[32,32,1]{1,2,0:T(1,128)} %get-tuple-element.109) | copy-start | bytes 12292 | tf_op jit(solution)/shard_map/cond
  43.1 132.5 %all-to-all-start.1 = ((bf16[32,2,160,256]{3,2,1,0:T(8,128)(2,1)}), bf16[32,2,160,256]{3,2,1,0:T(8,128)(2,1)}, u32[]{:S(2)}, u32[]{:S(2)}) async-start(bf16[32,2,160,256]{3,2,1,0:T(8,128)(2,1)} %pad_maximum_fusion.2), calls=%async_computation.1 | async-start | bytes 10485760 | tf_op jit(solution)/shard_map/cond/branch_1_fun/all_to_all | solution.py:206
  57.9 3.5 %copy-start.3 = (bf16[1024,2048]{1,0:T(8,128)(2,1)S(1)}, bf16[1024,2048]{1,0:T(8,128)(2,1)}, u32[]{:S(2)}) copy-start(bf16[1024,2048]{1,0:T(8,128)(2,1)} %get-tuple-element.54) | copy-start | bytes 12582916 | tf_op jit(solution)/shard_map/cond
  57.9 4.7 %copy-start.10 = (bf16[2048,3,256]{2,0,1:T(8,128)(2,1)S(1)}, bf16[2048,3,256]{2,0,1:T(8,128)(2,1)}, u32[]{:S(2)}) copy-start(bf16[2048,3,256]{2,0,1:T(8,128)(2,1)} %get-tuple-element.105) | copy-start | bytes 9437188 | tf_op jit(solution)/shard_map/cond
  66.7 2.0 copy-start.4
  177.3 11.9 %copy-start.7 = (bf16[1024,2,128]{2,1,0:T(2,128)(2,1)S(1)}, bf16[1024,2,128]{2,1,0:T(2,128)(2,1)}, u32[]{:S(2)}) copy-start(bf16[1024,2,128]{2,1,0:T(2,128)(2,1)} %get-tuple-element.147) | copy-start | bytes 1572868 | tf_op jit(solution)/shard_map/cond
  177.3 12.8 %copy-start.6 = (bf16[1024,2,128]{2,1,0:T(2,128)(2,1)S(1)}, bf16[1024,2,128]{2,1,0:T(2,128)(2,1)}, u32[]{:S(2)}) copy-start(bf16[1024,2,128]{2,1,0:T(2,128)(2,1)} %get-tuple-element.148) | copy-start | bytes 1572868 | tf_op jit(solution)/shard_map/cond
  179.6 15.6 %all-to-all-start.2 = ((bf16[32,2,4,256]{3,2,1,0:T(4,128)(2,1)}), bf16[32,2,4,256]{3,2,1,0:T(4,128)(2,1)S(1)}, u32[]{:S(2)}, u32[]{:S(2)}) async-start(bf16[32,2,4,256]{3,2,1,0:T(4,128)(2,1)} %gather_fusion.3), calls=%async_computation.2 | async-start | bytes 262144 | tf_op jit(solution)/shard_map/cond/branch_1_fun/all_to_all | solution.py:220
Sparse Core Ops, SparseCore 0:
  226.3 38.1 reduce-scatter.1

commit v5 on v4

--- a/solution.py
+++ b/solution.py
@@ -12,6 +12,7 @@
 PAGE = 128
 MAXP = 32
 BLOCK_Q = 256
+MESH = pl.DeviceIdType.MESH
 RELAY_A = 8
 RELAY_B = 1
 
@@ -65,9 +66,9 @@
         ),
         jnp.max(new_scores, axis=1, keepdims=True),
     )
-    main_w = jnp.where(main_ok, jnp.exp(main_scores - row_top), 0.0)
-    extra_w = jnp.where(extra_ok, jnp.exp(extra_scores - row_top), 0.0)
-    new_w = jnp.where(new_ok, jnp.exp(new_scores - row_top), 0.0)
+    main_w = jnp.exp(main_scores - row_top)
+    extra_w = jnp.exp(extra_scores - row_top)
+    new_w = jnp.exp(new_scores - row_top)
     row_total = (
         jnp.sum(main_w, axis=1, keepdims=True)
         + jnp.sum(extra_w, axis=1, keepdims=True)
@@ -131,6 +132,66 @@
     )
 
 
+def swap_kernel(send_ref, recv_ref, send_sems, recv_sems):
+    count = send_ref.shape[0]
+    me = lax.axis_index("req")
+    tp_me = lax.axis_index("tp")
+    barrier = pltpu.get_barrier_semaphore()
+
+    def others(fn):
+        def step(peer, carry):
+            @pl.when(peer != me)
+            def _():
+                fn(peer)
+
+            return carry
+
+        lax.fori_loop(0, count, step, 0)
+
+    def greet(peer):
+        pl.semaphore_signal(barrier, inc=1, device_id=(peer, tp_me), device_id_type=MESH)
+
+    others(greet)
+    pl.semaphore_wait(barrier, count - 1)
+
+    def outgoing(peer):
+        return pltpu.make_async_remote_copy(
+            src_ref=send_ref.at[peer],
+            dst_ref=recv_ref.at[me],
+            send_sem=send_sems.at[peer],
+            recv_sem=recv_sems.at[me],
+            device_id=(peer, tp_me),
+            device_id_type=MESH,
+        )
+
+    def arriving(peer):
+        return pltpu.make_async_remote_copy(
+            src_ref=send_ref.at[peer],
+            dst_ref=recv_ref.at[peer],
+            send_sem=send_sems.at[peer],
+            recv_sem=recv_sems.at[peer],
+            device_id=(peer, tp_me),
+            device_id_type=MESH,
+        )
+
+    others(lambda peer: outgoing(peer).start())
+    recv_ref[pl.ds(me, 1)] = send_ref[pl.ds(me, 1)]
+    others(lambda peer: outgoing(peer).wait_send())
+    others(lambda peer: arriving(peer).wait_recv())
+
+
+def swap_pieces(pieces):
+    count = pieces.shape[0]
+    return pl.pallas_call(
+        swap_kernel,
+        out_shape=jax.ShapeDtypeStruct(pieces.shape, pieces.dtype),
+        in_specs=[pl.BlockSpec(memory_space=pltpu.VMEM)],
+        out_specs=pl.BlockSpec(memory_space=pltpu.VMEM),
+        scratch_shapes=[pltpu.SemaphoreType.DMA((count,)), pltpu.SemaphoreType.DMA((count,))],
+        compiler_params=pltpu.CompilerParams(collective_id=0, has_side_effects=True),
+    )(pieces)
+
+
 def key_positions(entry_of_slot):
     tokens = jnp.arange(PAGE)[None, :]
     return jnp.where(entry_of_slot[:, None] >= 0, entry_of_slot[:, None] * PAGE + tokens, 1 << 30)
@@ -217,7 +278,7 @@
     )
     extra = relayed[src_holder * RELAY_A + jnp.clip(src_index, 0, RELAY_A - 1)]
     extra = extra.transpose(0, 2, 1, 3, 4).reshape(rows, 2, RELAY_B * frag, width)
-    returned = lax.all_to_all(extra, "req", split_axis=0, concat_axis=0, tiled=True)
+    returned = swap_pieces(extra)
     extra_pages = (
         returned.reshape(req_count, 2, RELAY_B, frag, width)
         .transpose(2, 1, 0, 3, 4)

time: 275 us -> 265 us (0.964)
  Pallas kernels: 26.7 us -> 36.4 us
  waiting for transfers between devices: 131 us -> 123 us
  starting transfers between devices: 19.3 us -> 11.8 us
  loops' own time: 4.88 us -> 2.1 us
    pallas_call x0 -> x1, Pallas kernels: none -> 12.4 us  [swap_pieces(): pl.pallas_call(swap_kernel, out_shape=jax.ShapeDtypeStruct(pieces.shape,...]
    all_to_all x1 -> x0, starting transfers between devices: 6.77 us -> none  [exchange_relay(): lax.all_to_all(extra, 'req', split_axis=0, concat_axis=0, tiled=True)]
    all_to_all x1, waiting for transfers between devices: 89.2 us -> 83.5 us  [exchange_relay(): lax.all_to_all(outgoing, 'req', split_axis=0, concat_axis=0, tiled=True)]
    all_to_all x1 -> x0, waiting for transfers between devices: 3.57 us -> none  [exchange_relay(): lax.all_to_all(extra, 'req', split_axis=0, concat_axis=0, tiled=True)]
    another operation x1, loops' own time: 4.88 us -> 2.1 us  [body(): lax.cond(relay_fits, branch(exchange_relay), branch(exchange_wide), opera...]
    cond x21 -> x17, local copies, waits for them, and re-layouts: 11.2 us -> 12.3 us
  transfers between devices with their start and end apart: 3 -> 2, of which waited for: 3 -> 2; matrix products, arithmetic and copies ran while one was open for 12% -> 12% of each run, Pallas kernels for 0% -> 0%
where the time goes in v5:
time: 265 us; the launch traced here: 264 us
  waiting for transfers between devices  123 us (46%)
  local copies, waits for them, and re-layouts  38.9 us (15%)
  Pallas kernels  36.4 us (14%)
  other arithmetic  28.7 us (11%)
  between operations  16 us (6%)
  starting transfers between devices  11.8 us (4%)
  matrix products  7.32 us (3%)
    all_to_all x1, waiting for transfers between devices, exchange_relay(): lax.all_to_all(outgoing, 'req', split_axis=0, concat_axis=0, tiled=True)  83.5 us
    reduce_scatter x1, waiting for transfers between devices, body(): lax.psum_scatter(head_term.astype(jnp.bfloat16), 'tp', scatter_dimension=...  39.4 us
    pallas_call x1, Pallas kernels, attend(): pl.pallas_call(attend_kernel, grid_spec=grid_spec, out_shape=jax.ShapeDty...  24 us
    pallas_call x1, Pallas kernels, swap_pieces(): pl.pallas_call(swap_kernel, out_shape=jax.ShapeDtypeStruct(pieces.shape,...  12.4 us
    cond x17, local copies, waits for them, and re-layouts  12.3 us
    all_to_all x1, starting transfers between devices, exchange_relay(): lax.all_to_all(outgoing, 'req', split_axis=0, concat_axis=0, tiled=True)  11.8 us
    reshape x3, local copies, waits for them, and re-layouts, exchange_relay(): pieces = kv_pool[slot_a].reshape(RELAY_A, 2, req_count, frag, width).tran...  7.13 us
    concatenate x1, other arithmetic, exchange_relay(): outgoing = jnp.concatenate([kv_pool[send_slots], pieces], axis=2)  5.38 us
  transfers between devices with their start and end apart: 2, of which 2 were waited for; matrix products, arithmetic and copies ran while one was open for 12% of the time, Pallas kernels for 0%

profile of v5, /device:TPU:2, one launch (start us, length us, event | category | flops | bytes accessed | tf_op | source)
XLA Modules:
  0.0 264.2 jit_solution(10520611833686859971)
XLA Ops:
  6.6 1.3 dynamic_slice.22
  7.9 1.2 dynamic_slice.21
  10.4 1.6 convert_reduce_fusion.2
  15.9 198.8 %conditional.1 = (bf16[1024,256]{1,0:T(8,128)(2,1)S(1)}) conditional(s32[]{:T(128)} %convert_element_type.98, (s32[]{:T(128)}, s32[32,32]{1,0:T(8,128)}, s32[32,32]{1,0:T(8,128)S(1)}, bf16[1024,2048]{1,0:T(8,128)(2,1)}, bf16[2048,3,256]{2,0,1:T(8,128)(2,1)}, /*index=5*/s32[1]{0:T(128)}, s32[32,32]{1,0:T(8,128)}, ...), branch_computations={%region_5.11_spmd, %region_11.24_spmd} | conditional | flops 13044421632 | bytes 151088544 | solution.py:332
  19.8 1.5 select_reduce_fusion.2
  21.6 3.4 %gather_fusion.2 = bf16[8,2,128,256]{3,2,1,0:T(8,128)(2,1)} fusion(bf16[16,2,128,256]{3,2,1,0:T(8,128)(2,1)} %get-tuple-element.56, s32[1024]{0:T(1024)S(1)} %pad_clamp_fusion.2), kind=kCustom, calls=%fused_computation.2 | custom fusion | bytes 2097184 | tf_op jit(solution)/shard_map/cond/branch_1_fun/gather | solution.py:261
  24.9 2.2 reshape.477
  27.1 2.8 %copy.103 = bf16[8,2,32,4,256]{4,3,0,1,2:T(4,128)(2,1)} copy(bf16[8,2,32,4,256]{4,3,2,1,0:T(4,128)(2,1)} %reshape.477) | data formatting | bytes 2097152 | tf_op jit(solution)/shard_map/cond/branch_1_fun/reshape | solution.py:262
  29.9 2.1 reshape.478
  32.1 2.7 %gather_fusion.1 = bf16[32,2,128,256]{3,2,1,0:T(8,128)(2,1)} fusion(bf16[16,2,128,256]{3,2,1,0:T(8,128)(2,1)S(1)} %copy-done.1, s32[1024]{0:T(1024)S(1)} %pad_clamp_fusion.3), kind=kCustom, calls=%fused_computation.1 | custom fusion | bytes 8388736 | tf_op jit(solution)/shard_map/cond/branch_1_fun/gather | solution.py:266
  34.8 5.4 %pad_maximum_fusion.2 = bf16[32,2,160,256]{3,2,1,0:T(8,128)(2,1)} fusion(bf16[32,2,32,256]{3,2,1,0:T(8,128)(2,1)} %reshape.478, bf16[32,2,128,256]{3,2,1,0:T(8,128)(2,1)} %gather_fusion.1), kind=kLoop, calls=%fused_computation.48 | loop fusion | flops 10485760 | bytes 10485760 | tf_op jit(solution)/shard_map/cond/branch_1_fun/concatenate | solution.py:266
  40.2 11.8 %all-to-all-start.1 = ((bf16[32,2,160,256]{3,2,1,0:T(8,128)(2,1)}), bf16[32,2,160,256]{3,2,1,0:T(8,128)(2,1)}, u32[]{:S(2)}, u32[]{:S(2)}) async-start(bf16[32,2,160,256]{3,2,1,0:T(8,128)(2,1)} %pad_maximum_fusion.2), calls=%async_computation.1 | async-start | bytes 10485760 | tf_op jit(solution)/shard_map/cond/branch_1_fun/all_to_all | solution.py:267
  54.3 3.0 %convert_reduce_fusion.1 = f32[1024]{0:T(1024)S(1)} fusion(bf16[1024,2048]{1,0:T(8,128)(2,1)} %get-tuple-element.54), kind=kLoop, calls=%fused_computation.43 | loop fusion | flops 4193280 | bytes 4198400 | tf_op jit(solution)/shard_map/cond/branch_1_fun/reduce_sum | solution.py:202
  57.7 1.2 fusion.12
  59.0 4.1 %fusion.15 = f32[1024,3,256]{0,2,1:T(8,128)S(1)} fusion(bf16[2048,3,256]{2,0,1:T(8,128)(2,1)S(1)} %copy-done.8, bf16[1024,2048]{1,0:T(8,128)(2,1)S(1)} %copy-done.3, f32[1024]{0:T(1024)S(1)} %add_rsqrt_fusion.1, f32[1024]{0:T(1024)S(1)} %broadcast_multiply_fusion.2), kind=kOutput, calls=%fused_computation.50 | convolution fusion | flops 3229614080 | bytes 10493952 | tf_op jit(solution)/shard_map/cond/branch_1_fun/td,dcf->tcf/dot_general | solution.py:206
  63.1 1.7 copy-done.5
  65.9 1.7 fusion.32
  67.6 1.1 fusion.33
  68.7 1.4 copy.87
  71.2 1.4 copy.85
  72.7 2.2 copy.86
  74.9 2.2 copy.84
  77.1 1.9 multiply_cosine_fusion.1
  79.0 3.5 %subtract_convert_fusion.2 = (bf16[1024,2,64]{2,1,0:T(2,128)(2,1)S(1)}, bf16[1024,2,64]{2,1,0:T(2,128)(2,1)S(1)}, bf16[1024,2,64]{2,1,0:T(2,128)(2,1)S(1)}, bf16[1024,2,64]{2,1,0:T(2,128)(2,1)S(1)}) fusion(f32[1024,2,64]{2,1,0:T(2,128)S(1)} %copy.87, f32[1024,2,64]{2,1,0:T(2,128)} %copy.86, f32[1024,64]{1,0:T(8,128)S(1)} %get-tuple-element.162, ...), kind=kLoop, calls=%fused_computation.56 | loop fusion | flops 2097152 | bytes 3670016 | tf_op jit(solution)/shard_map/convert.6
  82.4 2.9 %pad_maximum_fusion.3 = (bf16[1024,2,128]{2,1,0:T(2,128)(2,1)S(1)}, bf16[1024,2,128]{2,1,0:T(2,128)(2,1)S(1)}) fusion(bf16[1024,2,64]{2,1,0:T(2,128)(2,1)S(1)} %get-tuple-element.155, bf16[1024,2,64]{2,1,0:T(2,128)(2,1)S(1)} %get-tuple-element.156, bf16[1024,2,64]{2,1,0:T(2,128)(2,1)S(1)} %get-tuple-element.150, bf16[1024,2,64]{2,1,0:T(2,128)(2,1)S(1)} %get-tuple-element.149), kind=kLoop, calls=%fused_computation.63 | loop fusion | flops 2097152 | bytes 2097152 | tf_op jit(solution)/shard_map/cond/branch_1_fun/concatenate | solution.py:29
  88.6 83.5 %all-to-all-done.1.mk_ref.mv_ref = bf16[32,2,160,256]{3,2,1,0:T(8,128)(2,1)} async-done(((bf16[32,2,160,256]{3,2,1,0:T(8,128)(2,1)}), bf16[32,2,160,256]{3,2,1,0:T(8,128)(2,1)}, u32[]{:S(2)}, u32[]{:S(2)}) %all-to-all-start.1) | async-done | bytes 5242912 | tf_op jit(solution)/shard_map/cond/branch_1_fun/all_to_all | solution.py:267
  172.1 1.3 slice.69
  174.9 1.3 gather_fusion.3
  176.3 12.4 %branch_1_fun.2 = bf16[32,2,4,256]{3,2,1,0:T(4,128)(2,1)} custom-call(bf16[32,2,4,256]{3,2,1,0:T(4,128)(2,1)} %gather_fusion.3), custom_call_target="tpu_custom_call" | custom-call | tf_op jit(solution)/shard_map/cond/branch_1_fun/pallas_call | solution.py:185
  190.3 24.0 %branch_1_fun.3 = bf16[1024,256]{1,0:T(8,128)(2,1)S(1)} custom-call(s32[1]{0:T(128)} %get-tuple-element.50.live_ref, s32[1,4096]{1,0:T(1,128)} %bitcast.113, s32[1,128]{1,0:T(1,128)} %broadcast_select_fusion.kpe_ref, bf16[1024,256]{1,0:T(8,128)(2,1)} %bitcast.107, bf16[32,2,160,256]{3,2,1,0:T(8,128)(2,1)} %all-to-all-done.1.mk_ref.mv_ref, ...), custom_call_target="tpu_custom_call" | custom-call | flops 5502926848 | bytes 6422528 | tf_op jit(solution)/shard_map/cond/branch_1_fun/pallas_call | solution.py:111
  214.7 3.2 %convolution_convert_fusion = bf16[1024,2048]{1,0:T(8,128)(2,1)} fusion(bf16[1024,256]{1,0:T(8,128)(2,1)S(1)} %get-tuple-element.166, bf16[256,2048]{1,0:T(8,128)(2,1)S(1)} %copy-done), kind=kOutput, calls=%fused_computation.106 | convolution fusion | flops 1075838976 | bytes 5767168 | tf_op jit(solution)/shard_map/dot_general | solution.py:333
  217.9 39.4 %reduce-scatter.2.cloned.1.call-done = bf16[128,2048]{1,0:T(8,128)(2,1)} async-done(((bf16[1024,2048]{1,0:T(8,128)(2,1)}), bf16[128,2048]{1,0:T(8,128)(2,1)}) %reduce-scatter.2.cloned.1.call-update) | async-done | bytes 524304 | tf_op jit(solution)/shard_map/reduce_scatter | solution.py:334
  (61 shorter events, 16.5 us)
Async XLA Ops:
  6.5 208.2 %copy-start = (bf16[256,2048]{1,0:T(8,128)(2,1)S(1)}, bf16[256,2048]{1,0:T(8,128)(2,1)}, u32[]{:S(2)}) copy-start(bf16[256,2048]{1,0:T(8,128)(2,1)} %param.12) | copy-start | bytes 3145732
  6.5 250.8 %reduce-scatter.2.cloned.1.call-start = ((), (), s32[]{:S(2)}) async-start(), calls=%async_computation.3 | async-start | bytes 4718592 | tf_op jit(solution)/shard_map/reduce_scatter | solution.py:334
  21.5 10.5 %copy-start.1 = (bf16[16,2,128,256]{3,2,1,0:T(8,128)(2,1)S(1)}, bf16[16,2,128,256]{3,2,1,0:T(8,128)(2,1)}, u32[]{:S(2)}) copy-start(bf16[16,2,128,256]{3,2,1,0:T(8,128)(2,1)} %get-tuple-element.56) | copy-start | bytes 6291460 | tf_op jit(solution)/shard_map/cond
  40.2 12.0 %copy-start.6 = (s32[32,32,1]{1,2,0:T(1,128)S(1)}, s32[32,32,1]{1,2,0:T(1,128)}, u32[]{:S(2)}) copy-start(s32[32,32,1]{1,2,0:T(1,128)} %get-tuple-element.126) | copy-start | bytes 12292 | tf_op jit(solution)/shard_map/cond
  40.2 131.9 %all-to-all-start.1 = ((bf16[32,2,160,256]{3,2,1,0:T(8,128)(2,1)}), bf16[32,2,160,256]{3,2,1,0:T(8,128)(2,1)}, u32[]{:S(2)}, u32[]{:S(2)}) async-start(bf16[32,2,160,256]{3,2,1,0:T(8,128)(2,1)} %pad_maximum_fusion.2), calls=%async_computation.1 | async-start | bytes 10485760 | tf_op jit(solution)/shard_map/cond/branch_1_fun/all_to_all | solution.py:267
  54.3 3.5 %copy-start.3 = (bf16[1024,2048]{1,0:T(8,128)(2,1)S(1)}, bf16[1024,2048]{1,0:T(8,128)(2,1)}, u32[]{:S(2)}) copy-start(bf16[1024,2048]{1,0:T(8,128)(2,1)} %get-tuple-element.54) | copy-start | bytes 12582916 | tf_op jit(solution)/shard_map/cond
  54.3 4.7 %copy-start.8 = (bf16[2048,3,256]{2,0,1:T(8,128)(2,1)S(1)}, bf16[2048,3,256]{2,0,1:T(8,128)(2,1)}, u32[]{:S(2)}) copy-start(bf16[2048,3,256]{2,0,1:T(8,128)(2,1)} %get-tuple-element.122) | copy-start | bytes 9437188 | tf_op jit(solution)/shard_map/cond
  63.1 1.8 copy-start.5
Sparse Core Ops, SparseCore 0:
  218.0 39.2 reduce-scatter.1

commit v6 on v5

--- a/solution.py
+++ b/solution.py
@@ -257,13 +257,14 @@
         & (holder_order[None, :] == wanted[:, None])
     )
     slot_a = jnp.sum(jnp.where(match_a, slots_flat[None, :], 0), axis=1)
-    pieces = (
-        kv_pool[slot_a]
-        .reshape(RELAY_A, 2, req_count, frag, width)
-        .transpose(2, 1, 0, 3, 4)
-        .reshape(req_count, 2, RELAY_A * frag, width)
-    )
-    outgoing = jnp.concatenate([kv_pool[send_slots], pieces], axis=2)
+    tokens = jnp.arange(PAGE + RELAY_A * frag)
+    relay_part = tokens[None, :] >= PAGE
+    piece = jnp.clip(tokens - PAGE, 0, None)
+    page_idx = jnp.where(relay_part, slot_a[piece // frag][None, :], send_slots[:, None])
+    tok_idx = jnp.where(
+        relay_part, jnp.arange(req_count)[:, None] * frag + piece[None, :] % frag, tokens[None, :]
+    )
+    outgoing = kv_pool[page_idx[:, None, :], jnp.arange(2)[None, :, None], tok_idx[:, None, :]]
     incoming = lax.all_to_all(outgoing, "req", split_axis=0, concat_axis=0, tiled=True)
     relayed = (
         incoming[:, :, PAGE:]

time: 265 us -> 450 us (1.70)
  local copies, waits for them, and re-layouts: 38.9 us -> 222 us
    gather x2, local copies, waits for them, and re-layouts: 6.12 us -> 196 us  [the longest x1 196 us: exchange_relay(): kv_pool[page_idx[:, None, :], jnp.arange(2)[None, :, None], tok_idx[:, No...]
    reshape x3 -> x0, local copies, waits for them, and re-layouts: 7.13 us -> none  [exchange_relay(): pieces = kv_pool[slot_a].reshape(RELAY_A, 2, req_count, frag, width).tran...]
    concatenate x1 -> x2, other arithmetic: 5.38 us -> 0.13 us  [exchange_relay(): kv_pool[page_idx[:, None, :], jnp.arange(2)[None, :, None], tok_idx[:, No...]
    cond x17 -> x15, local copies, waits for them, and re-layouts: 12.3 us -> 12.3 us
  transfers between devices with their start and end apart: 2 -> 2, of which waited for: 2 -> 2; matrix products, arithmetic and copies ran while one was open for 12% -> 7% of each run, Pallas kernels for 0% -> 0%
where the time goes in v6:
time: 450 us; the launch traced here: 447 us
  local copies, waits for them, and re-layouts  222 us (49%)
  waiting for transfers between devices  123 us (27%)
  Pallas kernels  36.4 us (8%)
  other arithmetic  28.4 us (6%)
  between operations  16 us (4%)
  starting transfers between devices  11.7 us (3%)
  matrix products  7.32 us (2%)
    gather x1, local copies, waits for them, and re-layouts, exchange_relay(): kv_pool[page_idx[:, None, :], jnp.arange(2)[None, :, None], tok_idx[:, No...  196 us
    all_to_all x1, waiting for transfers between devices, exchange_relay(): lax.all_to_all(outgoing, 'req', split_axis=0, concat_axis=0, tiled=True)  83.5 us
    reduce_scatter x1, waiting for transfers between devices, body(): lax.psum_scatter(head_term.astype(jnp.bfloat16), 'tp', scatter_dimension=...  39.4 us
    pallas_call x1, Pallas kernels, attend(): pl.pallas_call(attend_kernel, grid_spec=grid_spec, out_shape=jax.ShapeDty...  24 us
    pallas_call x1, Pallas kernels, swap_pieces(): pl.pallas_call(swap_kernel, out_shape=jax.ShapeDtypeStruct(pieces.shape,...  12.4 us
    cond x15, local copies, waits for them, and re-layouts  12.3 us
    all_to_all x1, starting transfers between devices, exchange_relay(): lax.all_to_all(outgoing, 'req', split_axis=0, concat_axis=0, tiled=True)  11.7 us
  transfers between devices with their start and end apart: 2, of which 2 were waited for; matrix products, arithmetic and copies ran while one was open for 7% of the time, Pallas kernels for 0%

profile of v6, /device:TPU:2, one launch (start us, length us, event | category | flops | bytes accessed | tf_op | source)
XLA Modules:
  0.0 446.9 jit_solution(15099276996610731543)
XLA Ops:
  6.6 1.3 dynamic_slice.22
  7.9 1.2 dynamic_slice.21
  10.4 1.6 convert_reduce_fusion.2
  12.1 1.1 select_reduce_fusion.9
  15.9 381.6 %conditional.1 = (bf16[1024,256]{1,0:T(8,128)(2,1)S(1)}) conditional(s32[]{:T(128)} %convert_element_type.98, (s32[]{:T(128)}, s32[32,32]{1,0:T(8,128)}, s32[32,32]{1,0:T(8,128)S(1)}, bf16[1024,2048]{1,0:T(8,128)(2,1)}, bf16[2048,3,256]{2,0,1:T(8,128)(2,1)}, /*index=5*/s32[1]{0:T(128)}, s32[32,32]{1,0:T(8,128)}, ...), branch_computations={%region_5.11_spmd, %region_11.24_spmd} | conditional | flops 13044421632 | bytes 136830240 | solution.py:333
  18.7 1.1 select_reduce_fusion.3
  19.9 1.5 select_reduce_fusion.2
  22.2 4.3 compare_select_fusion.4
  27.5 195.6 %gather_fusion.1 = bf16[10240,256]{1,0:T(8,128)(2,1)} fusion(bf16[16,2,128,256]{3,2,1,0:T(8,128)(2,1)} %get-tuple-element.56, s32[10240]{0:T(1024)S(1)} %reshape.608), kind=kCustom, calls=%fused_computation.1 | custom fusion | bytes 10608640 | tf_op jit(solution)/shard_map/cond/branch_1_fun/gather | solution.py:267
  223.1 11.7 %all-to-all-start.1 = ((bf16[32,2,160,256]{3,2,1,0:T(8,128)(2,1)}), bf16[32,2,160,256]{3,2,1,0:T(8,128)(2,1)}, u32[]{:S(2)}, u32[]{:S(2)}) async-start(bf16[32,2,160,256]{3,2,1,0:T(8,128)(2,1)} %bitcast.84), calls=%async_computation.1 | async-start | bytes 10485760 | tf_op jit(solution)/shard_map/cond/branch_1_fun/all_to_all | solution.py:268
  237.0 3.0 convert_reduce_fusion.1
  240.4 1.2 fusion.12
  241.7 4.1 fusion.15
  245.8 1.7 copy-done.4
  247.7 1.0 copy.85
  248.7 1.7 fusion.34
  250.3 1.1 fusion.35
  251.4 1.4 copy.83
  252.9 1.1 fusion.36
  254.0 1.4 copy.81
  255.4 2.2 copy.82
  257.6 2.2 copy.80
  259.8 1.9 multiply_cosine_fusion.1
  261.7 3.5 subtract_convert_fusion.2
  265.2 2.9 pad_maximum_fusion.2
  271.3 83.5 %all-to-all-done.1.mk_ref.mv_ref = bf16[32,2,160,256]{3,2,1,0:T(8,128)(2,1)} async-done(((bf16[32,2,160,256]{3,2,1,0:T(8,128)(2,1)}), bf16[32,2,160,256]{3,2,1,0:T(8,128)(2,1)}, u32[]{:S(2)}, u32[]{:S(2)}) %all-to-all-start.1) | async-done | bytes 5242912 | tf_op jit(solution)/shard_map/cond/branch_1_fun/all_to_all | solution.py:268
  354.8 1.3 slice.77
  357.7 1.3 gather_fusion.2
  359.0 12.4 %branch_1_fun.2 = bf16[32,2,4,256]{3,2,1,0:T(4,128)(2,1)} custom-call(bf16[32,2,4,256]{3,2,1,0:T(4,128)(2,1)} %gather_fusion.2), custom_call_target="tpu_custom_call" | custom-call | tf_op jit(solution)/shard_map/cond/branch_1_fun/pallas_call | solution.py:185
  373.1 24.0 %branch_1_fun.3 = bf16[1024,256]{1,0:T(8,128)(2,1)S(1)} custom-call(s32[1]{0:T(128)} %get-tuple-element.50.live_ref, s32[1,4096]{1,0:T(1,128)} %bitcast.112, s32[1,128]{1,0:T(1,128)} %broadcast_select_fusion.kpe_ref, bf16[1024,256]{1,0:T(8,128)(2,1)} %bitcast.106, bf16[32,2,160,256]{3,2,1,0:T(8,128)(2,1)} %all-to-all-done.1.mk_ref.mv_ref, ...), custom_call_target="tpu_custom_call" | custom-call | flops 5502926848 | bytes 6422528 | tf_op jit(solution)/shard_map/cond/branch_1_fun/pallas_call | solution.py:111
  397.4 3.2 convolution_convert_fusion
  400.7 39.4 %reduce-scatter.2.cloned.1.call-done = bf16[128,2048]{1,0:T(8,128)(2,1)} async-done(((bf16[1024,2048]{1,0:T(8,128)(2,1)}), bf16[128,2048]{1,0:T(8,128)(2,1)}) %reduce-scatter.2.cloned.1.call-update) | async-done | bytes 524304 | tf_op jit(solution)/shard_map/reduce_scatter | solution.py:335
  (59 shorter events, 13.9 us)
Async XLA Ops:
  6.5 390.9 %copy-start = (bf16[256,2048]{1,0:T(8,128)(2,1)S(1)}, bf16[256,2048]{1,0:T(8,128)(2,1)}, u32[]{:S(2)}) copy-start(bf16[256,2048]{1,0:T(8,128)(2,1)} %param.12) | copy-start | bytes 3145732
  6.5 433.6 %reduce-scatter.2.cloned.1.call-start = ((), (), s32[]{:S(2)}) async-start(), calls=%async_computation.3 | async-start | bytes 4718592 | tf_op jit(solution)/shard_map/reduce_scatter | solution.py:335
  223.1 11.9 %copy-start.5 = (s32[32,32,1]{1,2,0:T(1,128)S(1)}, s32[32,32,1]{1,2,0:T(1,128)}, u32[]{:S(2)}) copy-start(s32[32,32,1]{1,2,0:T(1,128)} %get-tuple-element.124) | copy-start | bytes 12292 | tf_op jit(solution)/shard_map/cond
  223.1 131.7 %all-to-all-start.1 = ((bf16[32,2,160,256]{3,2,1,0:T(8,128)(2,1)}), bf16[32,2,160,256]{3,2,1,0:T(8,128)(2,1)}, u32[]{:S(2)}, u32[]{:S(2)}) async-start(bf16[32,2,160,256]{3,2,1,0:T(8,128)(2,1)} %bitcast.84), calls=%async_computation.1 | async-start | bytes 10485760 | tf_op jit(solution)/shard_map/cond/branch_1_fun/all_to_all | solution.py:268
  237.0 3.5 copy-start.2
  237.0 4.7 %copy-start.7 = (bf16[2048,3,256]{2,0,1:T(8,128)(2,1)S(1)}, bf16[2048,3,256]{2,0,1:T(8,128)(2,1)}, u32[]{:S(2)}) copy-start(bf16[2048,3,256]{2,0,1:T(8,128)(2,1)} %get-tuple-element.122) | copy-start | bytes 9437188 | tf_op jit(solution)/shard_map/cond
  245.8 1.8 copy-start.4
Sparse Core Ops, SparseCore 0:
  400.8 39.2 reduce-scatter.1

commit v7 on v5

--- a/solution.py
+++ b/solution.py
@@ -260,17 +260,10 @@
     pieces = (
         kv_pool[slot_a]
         .reshape(RELAY_A, 2, req_count, frag, width)
-        .transpose(2, 1, 0, 3, 4)
-        .reshape(req_count, 2, RELAY_A * frag, width)
-    )
-    outgoing = jnp.concatenate([kv_pool[send_slots], pieces], axis=2)
-    incoming = lax.all_to_all(outgoing, "req", split_axis=0, concat_axis=0, tiled=True)
-    relayed = (
-        incoming[:, :, PAGE:]
-        .reshape(req_count, 2, RELAY_A, frag, width)
-        .transpose(0, 2, 1, 3, 4)
-        .reshape(req_count * RELAY_A, 2, frag, width)
-    )
+        .transpose(2, 0, 1, 3, 4)
+        .reshape(req_count, RELAY_A * 2 * frag, width)
+    )
+    relayed = swap_pieces(pieces).reshape(req_count * RELAY_A, 2, frag, width)
     match_b = spill[:, None, :] & (req_order[:, None, :] == jnp.arange(RELAY_B)[None, :, None])
     src_holder = jnp.sum(jnp.where(match_b, holder_rows[:, None, :], 0), axis=2)
     src_index = jnp.sum(
@@ -278,9 +271,11 @@
     )
     extra = relayed[src_holder * RELAY_A + jnp.clip(src_index, 0, RELAY_A - 1)]
     extra = extra.transpose(0, 2, 1, 3, 4).reshape(rows, 2, RELAY_B * frag, width)
-    returned = swap_pieces(extra)
+    outgoing = jnp.concatenate([kv_pool[send_slots], extra], axis=2)
+    incoming = lax.all_to_all(outgoing, "req", split_axis=0, concat_axis=0, tiled=True)
     extra_pages = (
-        returned.reshape(req_count, 2, RELAY_B, frag, width)
+        incoming[:, :, PAGE:]
+        .reshape(req_count, 2, RELAY_B, frag, width)
         .transpose(2, 1, 0, 3, 4)
         .reshape(RELAY_B, 2, PAGE, width)
     )

time: 265 us -> 281 us (1.060); the launches traced: 264 us -> 277 us
  waiting for transfers between devices: 123 us -> 97.7 us
  Pallas kernels: 36.4 us -> 52.3 us
  local copies, waits for them, and re-layouts: 38.9 us -> 49.9 us
  loops' own time: 2.1 us -> 7.81 us
  starting transfers between devices: 11.8 us -> 17 us
    all_to_all x1, waiting for transfers between devices: 83.5 us -> 58.1 us  [exchange_relay(): lax.all_to_all(outgoing, 'req', split_axis=0, concat_axis=0, tiled=True)]
    pallas_call x1, Pallas kernels: 12.4 us -> 28.3 us  [swap_pieces(): pl.pallas_call(swap_kernel, out_shape=jax.ShapeDtypeStruct(pieces.shape,...]
    concatenate x0 -> x1, local copies, waits for them, and re-layouts: none -> 7.63 us  [exchange_relay(): outgoing = jnp.concatenate([kv_pool[send_slots], extra], axis=2)]
    another operation x1, loops' own time: 2.1 us -> 7.81 us  [body(): lax.cond(relay_fits, branch(exchange_relay), branch(exchange_wide), opera...]
    all_to_all x1, starting transfers between devices: 11.8 us -> 17 us  [exchange_relay(): lax.all_to_all(outgoing, 'req', split_axis=0, concat_axis=0, tiled=True)]
    all_to_all x0 -> x1, local copies, waits for them, and re-layouts: none -> 4.88 us  [exchange_relay(): lax.all_to_all(outgoing, 'req', split_axis=0, concat_axis=0, tiled=True)]
    cond x17 -> x15, local copies, waits for them, and re-layouts: 12.3 us -> 12.2 us
where the time goes in v7:
time: 281 us; the launch traced here: 277 us
  waiting for transfers between devices  97.7 us (35%)
  Pallas kernels  52.3 us (19%)
  local copies, waits for them, and re-layouts  49.9 us (18%)
  other arithmetic  28.8 us (10%)
  starting transfers between devices  17 us (6%)
  between operations  16.3 us (6%)
  loops' own time  7.81 us (3%)
  matrix products  7.32 us (3%)
    all_to_all x1, waiting for transfers between devices, exchange_relay(): lax.all_to_all(outgoing, 'req', split_axis=0, concat_axis=0, tiled=True)  58.1 us
    reduce_scatter x1, waiting for transfers between devices, body(): lax.psum_scatter(head_term.astype(jnp.bfloat16), 'tp', scatter_dimension=...  39.6 us
    pallas_call x1, Pallas kernels, swap_pieces(): pl.pallas_call(swap_kernel, out_shape=jax.ShapeDtypeStruct(pieces.shape,...  28.3 us
    pallas_call x1, Pallas kernels, attend(): pl.pallas_call(attend_kernel, grid_spec=grid_spec, out_shape=jax.ShapeDty...  24 us
    all_to_all x1, starting transfers between devices, exchange_relay(): lax.all_to_all(outgoing, 'req', split_axis=0, concat_axis=0, tiled=True)  17 us
    cond x15, local copies, waits for them, and re-layouts  12.2 us
    another operation x1, loops' own time, body(): lax.cond(relay_fits, branch(exchange_relay), branch(exchange_wide), opera...  7.81 us
    concatenate x1, local copies, waits for them, and re-layouts, exchange_relay(): outgoing = jnp.concatenate([kv_pool[send_slots], extra], axis=2)  7.63 us
  transfers between devices with their start and end apart: 2, of which 2 were waited for; matrix products, arithmetic and copies ran while one was open for 12% of the time, Pallas kernels for 0%

profile of v7, /device:TPU:2, one launch (start us, length us, event | category | flops | bytes accessed | tf_op | source)
XLA Modules:
  0.0 277.2 jit_solution(5120160635121720895)
XLA Ops:
  6.6 1.3 dynamic_slice.22
  7.9 1.2 dynamic_slice.21
  10.4 1.6 convert_reduce_fusion.2
  15.9 211.4 %conditional.1 = (bf16[1024,256]{1,0:T(8,128)(2,1)S(1)}) conditional(s32[]{:T(128)} %convert_element_type.98, (s32[]{:T(128)}, s32[32,32]{1,0:T(8,128)}, s32[32,32]{1,0:T(8,128)S(1)}, bf16[1024,2048]{1,0:T(8,128)(2,1)}, bf16[2048,3,256]{2,0,1:T(8,128)(2,1)}, /*index=5*/s32[1]{0:T(128)}, s32[32,32]{1,0:T(8,128)}, ...), branch_computations={%region_5.11_spmd, %region_11.24_spmd} | conditional | flops 13044421632 | bytes 157494688 | solution.py:327
  25.8 1.5 select_reduce_fusion.2
  28.4 2.2 gather_fusion.2
  31.8 2.9 %copy.121 = bf16[8,2,32,4,256]{4,3,1,0,2:T(4,128)(2,1)} copy(bf16[8,2,32,4,256]{4,3,2,1,0:T(4,128)(2,1)} %reshape.475) | data formatting | bytes 2097152 | tf_op jit(solution)/shard_map/cond/branch_1_fun/reshape | solution.py:262
  34.7 2.2 reshape.476.send_ref
  36.9 28.3 %branch_1_fun.2 = bf16[32,64,256]{2,1,0:T(8,128)(2,1)} custom-call(bf16[32,64,256]{2,1,0:T(8,128)(2,1)} %reshape.476.send_ref), custom_call_target="tpu_custom_call" | custom-call | tf_op jit(solution)/shard_map/cond/branch_1_fun/pallas_call | solution.py:185
  65.2 2.2 reshape.477
  67.4 2.8 %gather_fusion.1 = bf16[32,2,128,256]{3,2,1,0:T(8,128)(2,1)} fusion(bf16[16,2,128,256]{3,2,1,0:T(8,128)(2,1)S(1)} %copy-done.1, s32[1024]{0:T(1024)S(1)} %pad_clamp_fusion.3), kind=kCustom, calls=%fused_computation.1 | custom fusion | bytes 8388736 | tf_op jit(solution)/shard_map/cond/branch_1_fun/gather | solution.py:274
  70.2 1.9 gather_fusion.3
  72.1 4.6 %pad_maximum_fusion.2 = bf16[32,2,132,256]{3,2,1,0:T(8,128)(2,1)} fusion(bf16[32,2,4,256]{3,2,1,0:T(4,128)(2,1)S(1)} %gather_fusion.3, bf16[32,2,128,256]{3,2,1,0:T(8,128)(2,1)} %gather_fusion.1), kind=kLoop, calls=%fused_computation.48 | loop fusion | flops 8650752 | bytes 8650752 | tf_op jit(solution)/shard_map/cond/branch_1_fun/concatenate | solution.py:274
  76.7 7.6 %copy.87 = bf16[32,2,132,256]{3,1,2,0:T(2,128)(2,1)} copy(bf16[32,2,132,256]{3,2,1,0:T(8,128)(2,1)} %pad_maximum_fusion.2) | data formatting | bytes 8650752 | tf_op jit(solution)/shard_map/cond/branch_1_fun/concatenate | solution.py:274
  84.3 17.0 %all-to-all-start.1 = ((bf16[32,2,132,256]{3,1,2,0:T(2,128)(2,1)}), bf16[32,2,132,256]{3,1,2,0:T(2,128)(2,1)}, u32[]{:S(2)}, u32[]{:S(2)}) async-start(bf16[32,2,132,256]{3,1,2,0:T(2,128)(2,1)} %copy.87), calls=%async_computation.1 | async-start | bytes 8650752 | tf_op jit(solution)/shard_map/cond/branch_1_fun/all_to_all | solution.py:275
  103.3 3.0 %convert_reduce_fusion.1 = f32[1024]{0:T(1024)S(1)} fusion(bf16[1024,2048]{1,0:T(8,128)(2,1)} %get-tuple-element.54), kind=kLoop, calls=%fused_computation.43 | loop fusion | flops 4193280 | bytes 4198400 | tf_op jit(solution)/shard_map/cond/branch_1_fun/reduce_sum | solution.py:202
  106.7 1.2 fusion.12
  108.0 4.1 %fusion.15 = f32[1024,3,256]{0,2,1:T(8,128)S(1)} fusion(bf16[2048,3,256]{2,0,1:T(8,128)(2,1)S(1)} %copy-done.7, bf16[1024,2048]{1,0:T(8,128)(2,1)S(1)} %copy-done.3, f32[1024]{0:T(1024)S(1)} %add_rsqrt_fusion.1, f32[1024]{0:T(1024)S(1)} %broadcast_multiply_fusion.2), kind=kOutput, calls=%fused_computation.50 | convolution fusion | flops 3229614080 | bytes 10493952 | tf_op jit(solution)/shard_map/cond/branch_1_fun/td,dcf->tcf/dot_general | solution.py:206
  112.1 1.7 copy-done.5
  114.9 1.7 fusion.32
  117.6 1.4 copy.107
  120.1 1.4 copy.105
  121.6 2.2 copy.106
  123.8 2.2 copy.104
  126.0 1.9 multiply_cosine_fusion.1
  127.9 3.5 %subtract_convert_fusion.2 = (bf16[1024,2,64]{2,1,0:T(2,128)(2,1)S(1)}, bf16[1024,2,64]{2,1,0:T(2,128)(2,1)S(1)}, bf16[1024,2,64]{2,1,0:T(2,128)(2,1)S(1)}, bf16[1024,2,64]{2,1,0:T(2,128)(2,1)S(1)}) fusion(f32[1024,2,64]{2,1,0:T(2,128)S(1)} %copy.107, f32[1024,2,64]{2,1,0:T(2,128)} %copy.106, f32[1024,64]{1,0:T(8,128)S(1)} %get-tuple-element.179, ...), kind=kLoop, calls=%fused_computation.55 | loop fusion | flops 2097152 | bytes 3670016 | tf_op jit(solution)/shard_map/convert.6
  131.4 3.1 %pad_maximum_fusion.3 = (bf16[1024,2,128]{2,1,0:T(2,128)(2,1)S(1)}, bf16[1024,2,128]{2,1,0:T(2,128)(2,1)S(1)}) fusion(bf16[1024,2,64]{2,1,0:T(2,128)(2,1)S(1)} %get-tuple-element.172, bf16[1024,2,64]{2,1,0:T(2,128)(2,1)S(1)} %get-tuple-element.173, bf16[1024,2,64]{2,1,0:T(2,128)(2,1)S(1)} %get-tuple-element.167, bf16[1024,2,64]{2,1,0:T(2,128)(2,1)S(1)} %get-tuple-element.166), kind=kLoop, calls=%fused_computation.62 | loop fusion | flops 2097152 | bytes 2097152 | tf_op jit(solution)/shard_map/cond/branch_1_fun/concatenate | solution.py:29
  138.3 58.1 %all-to-all-done.1 = bf16[32,2,132,256]{3,1,2,0:T(2,128)(2,1)} async-done(((bf16[32,2,132,256]{3,1,2,0:T(2,128)(2,1)}), bf16[32,2,132,256]{3,1,2,0:T(2,128)(2,1)}, u32[]{:S(2)}, u32[]{:S(2)}) %all-to-all-start.1) | async-done | bytes 4325408 | tf_op jit(solution)/shard_map/cond/branch_1_fun/all_to_all | solution.py:275
  198.1 4.9 %copy.92.mk_ref.mv_ref = bf16[32,2,132,256]{3,2,1,0:T(8,128)(2,1)} copy(bf16[32,2,132,256]{3,1,2,0:T(2,128)(2,1)} %all-to-all-done.1) | data formatting | bytes 8650752 | tf_op jit(solution)/shard_map/cond/branch_1_fun/all_to_all | solution.py:275
  203.0 24.0 %branch_1_fun.3 = bf16[1024,256]{1,0:T(8,128)(2,1)S(1)} custom-call(s32[1]{0:T(128)} %get-tuple-element.50.live_ref, s32[1,4096]{1,0:T(1,128)} %bitcast.107, s32[1,128]{1,0:T(1,128)} %broadcast_select_fusion.kpe_ref, bf16[1024,256]{1,0:T(8,128)(2,1)} %bitcast.101, bf16[32,2,132,256]{3,2,1,0:T(8,128)(2,1)} %copy.92.mk_ref.mv_ref, ...), custom_call_target="tpu_custom_call" | custom-call | flops 5502926848 | bytes 6422528 | tf_op jit(solution)/shard_map/cond/branch_1_fun/pallas_call | solution.py:111
  227.3 3.2 %convolution_convert_fusion = bf16[1024,2048]{1,0:T(8,128)(2,1)} fusion(bf16[1024,256]{1,0:T(8,128)(2,1)S(1)} %get-tuple-element.183, bf16[256,2048]{1,0:T(8,128)(2,1)S(1)} %copy-done), kind=kOutput, calls=%fused_computation.105 | convolution fusion | flops 1075838976 | bytes 5767168 | tf_op jit(solution)/shard_map/dot_general | solution.py:328
  230.5 39.6 %reduce-scatter.2.cloned.1.call-done = bf16[128,2048]{1,0:T(8,128)(2,1)} async-done(((bf16[1024,2048]{1,0:T(8,128)(2,1)}), bf16[128,2048]{1,0:T(8,128)(2,1)}) %reduce-scatter.2.cloned.1.call-update) | async-done | bytes 524304 | tf_op jit(solution)/shard_map/reduce_scatter | solution.py:329
  (58 shorter events, 18.5 us)
Async XLA Ops:
  6.5 220.7 %copy-start = (bf16[256,2048]{1,0:T(8,128)(2,1)S(1)}, bf16[256,2048]{1,0:T(8,128)(2,1)}, u32[]{:S(2)}) copy-start(bf16[256,2048]{1,0:T(8,128)(2,1)} %param.12) | copy-start | bytes 3145732
  6.5 263.5 %reduce-scatter.2.cloned.1.call-start = ((), (), s32[]{:S(2)}) async-start(), calls=%async_computation.3 | async-start | bytes 4718592 | tf_op jit(solution)/shard_map/reduce_scatter | solution.py:329
  31.8 35.6 %copy-start.1 = (bf16[16,2,128,256]{3,2,1,0:T(8,128)(2,1)S(1)}, bf16[16,2,128,256]{3,2,1,0:T(8,128)(2,1)}, u32[]{:S(2)}) copy-start(bf16[16,2,128,256]{3,2,1,0:T(8,128)(2,1)} %get-tuple-element.56) | copy-start | bytes 6291460 | tf_op jit(solution)/shard_map/cond
  84.3 112.1 %all-to-all-start.1 = ((bf16[32,2,132,256]{3,1,2,0:T(2,128)(2,1)}), bf16[32,2,132,256]{3,1,2,0:T(2,128)(2,1)}, u32[]{:S(2)}, u32[]{:S(2)}) async-start(bf16[32,2,132,256]{3,1,2,0:T(2,128)(2,1)} %copy.87), calls=%async_computation.1 | async-start | bytes 8650752 | tf_op jit(solution)/shard_map/cond/branch_1_fun/all_to_all | solution.py:275
  103.3 3.5 %copy-start.3 = (bf16[1024,2048]{1,0:T(8,128)(2,1)S(1)}, bf16[1024,2048]{1,0:T(8,128)(2,1)}, u32[]{:S(2)}) copy-start(bf16[1024,2048]{1,0:T(8,128)(2,1)} %get-tuple-element.54) | copy-start | bytes 12582916 | tf_op jit(solution)/shard_map/cond
  103.3 4.7 %copy-start.7 = (bf16[2048,3,256]{2,0,1:T(8,128)(2,1)S(1)}, bf16[2048,3,256]{2,0,1:T(8,128)(2,1)}, u32[]{:S(2)}) copy-start(bf16[2048,3,256]{2,0,1:T(8,128)(2,1)} %get-tuple-element.139) | copy-start | bytes 9437188 | tf_op jit(solution)/shard_map/cond
  112.1 1.7 copy-start.5
Sparse Core Ops, SparseCore 0:
  230.6 39.4 reduce-scatter.1

commit v8 on v5

--- a/solution.py
+++ b/solution.py
@@ -314,22 +314,28 @@
     lengths = lax.dynamic_slice_in_dim(cached_len, req_index, 1)
     flags = lax.dynamic_slice_in_dim(cont_flag, req_index, 1)
     live_len = lengths * flags
-    operands = (hidden_in, qkv_weight, kv_pool, page_slot, holder_rows, rank_all, live_len)
-
-    def branch(exchange):
-        def run(ops):
-            hidden, weight, pool, slots, holders, ranks, live = ops
-            main_pages, main_pos, extra_pages, extra_pos = exchange(
-                pool, slots, holders, ranks, req_index, req_count
-            )
-            query_rot, new_key, new_value = project(hidden, weight, live, local_heads, local_width)
-            return attend(
-                live, query_rot, main_pages, main_pos, extra_pages, extra_pos, new_key, new_value
-            )
-
-        return run
-
-    attended = lax.cond(relay_fits, branch(exchange_relay), branch(exchange_wide), operands)
+    main_pages, main_pos, extra_pages, extra_pos = exchange_relay(
+        kv_pool, page_slot, holder_rows, rank_all, req_index, req_count
+    )
+    query_rot, new_key, new_value = project(hidden_in, qkv_weight, live_len, local_heads, local_width)
+    attended = attend(
+        live_len, query_rot, main_pages, main_pos, extra_pages, extra_pos, new_key, new_value
+    )
+
+    def keep(ops):
+        return ops[0]
+
+    def redo(ops):
+        _, query, key, value, pool, slots, holders, ranks, live = ops
+        pages, pos, extra, extra_at = exchange_wide(pool, slots, holders, ranks, req_index, req_count)
+        return attend(live, query, pages, pos, extra, extra_at, key, value)
+
+    attended = lax.cond(
+        relay_fits,
+        keep,
+        redo,
+        (attended, query_rot, new_key, new_value, kv_pool, page_slot, holder_rows, rank_all, live_len),
+    )
     head_term = jnp.dot(attended, out_weight, preferred_element_type=jnp.float32)
     return lax.psum_scatter(head_term.astype(jnp.bfloat16), "tp", scatter_dimension=0, tiled=True)
 

time: 265 us -> 262 us (0.989)
    cond x17 -> x0, local copies, waits for them, and re-layouts: 12.3 us -> none
    unnamed x2 -> x25, local copies, waits for them, and re-layouts: 0.01 us -> 8.44 us
  transfers between devices with their start and end apart: 2 -> 2, of which waited for: 2 -> 2; matrix products, arithmetic and copies ran while one was open for 12% -> 13% of each run, Pallas kernels for 0% -> 0%
where the time goes in v8:
time: 262 us; the launch traced here: 261 us
  waiting for transfers between devices  122 us (47%)
  Pallas kernels  37 us (14%)
  local copies, waits for them, and re-layouts  36.4 us (14%)
  other arithmetic  28 us (11%)
  between operations  17.5 us (7%)
  starting transfers between devices  11.8 us (5%)
  matrix products  8.76 us (3%)
    all_to_all x1, waiting for transfers between devices, exchange_relay(): lax.all_to_all(outgoing, 'req', split_axis=0, concat_axis=0, tiled=True)  82.5 us
    reduce_scatter x1, waiting for transfers between devices, body(): lax.psum_scatter(head_term.astype(jnp.bfloat16), 'tp', scatter_dimension=...  39.4 us
    pallas_call x1, Pallas kernels, attend(): pl.pallas_call(attend_kernel, grid_spec=grid_spec, out_shape=jax.ShapeDty...  24.6 us
    pallas_call x1, Pallas kernels, swap_pieces(): pl.pallas_call(swap_kernel, out_shape=jax.ShapeDtypeStruct(pieces.shape,...  12.4 us
    all_to_all x1, starting transfers between devices, exchange_relay(): lax.all_to_all(outgoing, 'req', split_axis=0, concat_axis=0, tiled=True)  11.8 us
    unnamed x25, local copies, waits for them, and re-layouts  8.44 us
    reshape x3, local copies, waits for them, and re-layouts, exchange_relay(): pieces = kv_pool[slot_a].reshape(RELAY_A, 2, req_count, frag, width).tran...  7.13 us
    concatenate x1, other arithmetic, exchange_relay(): outgoing = jnp.concatenate([kv_pool[send_slots], pieces], axis=2)  5.38 us
  transfers between devices with their start and end apart: 2, of which 2 were waited for; matrix products, arithmetic and copies ran while one was open for 13% of the time, Pallas kernels for 0%

profile of v8, /device:TPU:2, one launch (start us, length us, event | category | flops | bytes accessed | tf_op | source)
XLA Modules:
  0.0 261.5 jit_solution(2204549483790056178)
XLA Ops:
  6.5 1.7 convert_reduce_fusion.1
  10.6 1.1 select_reduce_fusion.2
  11.8 1.5 select_reduce_fusion.4
  13.7 3.2 %gather_fusion.2 = bf16[8,2,128,256]{3,2,1,0:T(8,128)(2,1)} fusion(bf16[16,2,128,256]{3,2,1,0:T(8,128)(2,1)} %param.13, s32[1024]{0:T(1024)S(1)} %pad_clamp_fusion.2), kind=kCustom, calls=%fused_computation.2 | custom fusion | bytes 2097184 | tf_op jit(solution)/shard_map/gather | solution.py:261
  16.9 2.2 reshape.422
  19.1 2.8 %copy.63 = bf16[8,2,32,4,256]{4,3,0,1,2:T(4,128)(2,1)} copy(bf16[8,2,32,4,256]{4,3,2,1,0:T(4,128)(2,1)} %reshape.422) | data formatting | bytes 2097152 | tf_op jit(solution)/shard_map/reshape | solution.py:262
  21.9 2.1 reshape.423
  24.1 4.3 %gather_fusion.1 = bf16[32,2,128,256]{3,2,1,0:T(8,128)(2,1)} fusion(bf16[16,2,128,256]{3,2,1,0:T(8,128)(2,1)} %param.13, s32[1024]{0:T(1024)S(1)} %pad_clamp_fusion.3), kind=kCustom, calls=%fused_computation.1 | custom fusion | bytes 8388736 | tf_op jit(solution)/shard_map/gather | solution.py:266
  28.4 5.4 %pad_maximum_fusion = bf16[32,2,160,256]{3,2,1,0:T(8,128)(2,1)} fusion(bf16[32,2,32,256]{3,2,1,0:T(8,128)(2,1)} %reshape.423, bf16[32,2,128,256]{3,2,1,0:T(8,128)(2,1)} %gather_fusion.1), kind=kLoop, calls=%fused_computation.23 | loop fusion | flops 10485760 | bytes 10485760 | tf_op jit(solution)/shard_map/concatenate | solution.py:266
  33.8 11.8 %all-to-all-start.1 = ((bf16[32,2,160,256]{3,2,1,0:T(8,128)(2,1)}), bf16[32,2,160,256]{3,2,1,0:T(8,128)(2,1)}, u32[]{:S(2)}, u32[]{:S(2)}) async-start(bf16[32,2,160,256]{3,2,1,0:T(8,128)(2,1)} %pad_maximum_fusion), calls=%async_computation.1 | async-start | bytes 10485760 | tf_op jit(solution)/shard_map/all_to_all | solution.py:267
  47.2 2.8 %convert_reduce_fusion = f32[1024]{0:T(1024)S(1)} fusion(bf16[1024,2048]{1,0:T(8,128)(2,1)} %param.10), kind=kLoop, calls=%fused_computation.18 | loop fusion | flops 4193280 | bytes 4198400 | tf_op jit(solution)/shard_map/reduce_sum | solution.py:202
  50.0 1.2 fusion.3
  51.2 4.0 %fusion.6 = f32[1024,3,256]{0,2,1:T(8,128)S(1)} fusion(bf16[2048,3,256]{2,0,1:T(8,128)(2,1)S(1)} %copy-done, bf16[1024,2048]{1,0:T(8,128)(2,1)S(1)} %copy-done.3, f32[1024]{0:T(1024)S(1)} %add_rsqrt_fusion, f32[1024]{0:T(1024)S(1)} %broadcast_multiply_fusion.1), kind=kOutput, calls=%fused_computation.25 | convolution fusion | flops 3229614080 | bytes 10493952 | tf_op jit(solution)/shard_map/td,dcf->tcf/dot_general | solution.py:206
  56.4 0.9 fusion.23
  57.9 1.5 copy.52
  59.3 1.1 fusion.22
  60.4 1.4 copy.53
  61.9 2.2 copy.54
  65.5 1.9 multiply_cosine_fusion
  67.4 3.9 %subtract_convert_fusion = (bf16[1024,2,64]{2,1,0:T(2,128)(2,1)S(1)}, bf16[1024,2,64]{2,1,0:T(2,128)(2,1)S(1)}, bf16[1024,2,64]{2,1,0:T(2,128)(2,1)S(1)}, bf16[1024,2,64]{2,1,0:T(2,128)(2,1)S(1)}) fusion(f32[1024,2,64]{2,1,0:T(2,128)} %copy.54, f32[1024,2,64]{2,1,0:T(2,128)S(1)} %copy.53, f32[1024,64]{1,0:T(8,128)S(1)} %get-tuple-element.58, ...), kind=kLoop, calls=%fused_computation.32 | loop fusion | flops 2097152 | bytes 3670016 | tf_op jit(solution)/shard_map/convert.1
  71.3 2.9 %pad_maximum_fusion.1 = (bf16[1024,2,128]{2,1,0:T(2,128)(2,1)S(1)}, bf16[1024,2,128]{2,1,0:T(2,128)(2,1)S(1)}) fusion(bf16[1024,2,64]{2,1,0:T(2,128)(2,1)S(1)} %get-tuple-element.50, bf16[1024,2,64]{2,1,0:T(2,128)(2,1)S(1)} %get-tuple-element.51, bf16[1024,2,64]{2,1,0:T(2,128)(2,1)S(1)} %get-tuple-element.45, bf16[1024,2,64]{2,1,0:T(2,128)(2,1)S(1)} %get-tuple-element.44), kind=kLoop, calls=%fused_computation.41 | loop fusion | flops 2097152 | bytes 2097152 | tf_op jit(solution)/shard_map/concatenate | solution.py:29
  75.1 0.9 copy.65
  78.1 1.0 copy.55
  83.2 82.5 %all-to-all-done.1.mk_ref.mv_ref = bf16[32,2,160,256]{3,2,1,0:T(8,128)(2,1)} async-done(((bf16[32,2,160,256]{3,2,1,0:T(8,128)(2,1)}), bf16[32,2,160,256]{3,2,1,0:T(8,128)(2,1)}, u32[]{:S(2)}, u32[]{:S(2)}) %all-to-all-start.1) | async-done | bytes 5242912 | tf_op jit(solution)/shard_map/all_to_all | solution.py:267
  165.7 2.4 slice.52
  168.0 1.5 reshape.424
  170.5 1.3 gather_fusion.3
  171.8 12.4 %shard_map.82 = bf16[32,2,4,256]{3,2,1,0:T(4,128)(2,1)} custom-call(bf16[32,2,4,256]{3,2,1,0:T(4,128)(2,1)} %gather_fusion.3), custom_call_target="tpu_custom_call" | custom-call | tf_op jit(solution)/shard_map/pallas_call | solution.py:185
  184.2 1.0 copy.49
  185.8 24.6 %shard_map.83 = bf16[1024,256]{1,0:T(8,128)(2,1)} custom-call(s32[1]{0:T(128)} %mul.171.live_ref, s32[1,4096]{1,0:T(1,128)} %bitcast.94, s32[1,128]{1,0:T(1,128)} %broadcast_select_fusion.kpe_ref, bf16[1024,256]{1,0:T(8,128)(2,1)} %bitcast.88, bf16[32,2,160,256]{3,2,1,0:T(8,128)(2,1)} %all-to-all-done.1.mk_ref.mv_ref, ...), custom_call_target="tpu_custom_call" | custom-call | flops 5502926848 | bytes 6422528 | tf_op jit(solution)/shard_map/pallas_call | solution.py:111
  210.5 4.7 %convolution_convert_fusion = bf16[1024,2048]{1,0:T(8,128)(2,1)} fusion(bf16[1024,256]{1,0:T(8,128)(2,1)} %get-tuple-element.61, bf16[256,2048]{1,0:T(8,128)(2,1)} %param.12), kind=kOutput, calls=%fused_computation.28 | convolution fusion | flops 1075838976 | bytes 5767168 | tf_op jit(solution)/shard_map/dot_general | solution.py:339
  215.2 39.4 %reduce-scatter.2.cloned.1.call-done = bf16[128,2048]{1,0:T(8,128)(2,1)} async-done(((bf16[1024,2048]{1,0:T(8,128)(2,1)}), bf16[128,2048]{1,0:T(8,128)(2,1)}) %reduce-scatter.2.cloned.1.call-update) | async-done | bytes 524304 | tf_op jit(solution)/shard_map/reduce_scatter | solution.py:340
  (65 shorter events, 12.3 us)
Async XLA Ops:
  6.5 44.7 %copy-start = (bf16[2048,3,256]{2,0,1:T(8,128)(2,1)S(1)}, bf16[2048,3,256]{2,0,1:T(8,128)(2,1)}, u32[]{:S(2)}) copy-start(bf16[2048,3,256]{2,0,1:T(8,128)(2,1)} %param.11) | copy-start | bytes 9437188
  33.8 12.0 %copy-start.10 = (s32[32]{0:T(128)S(1)}, s32[32]{0:T(128)}, u32[]{:S(2)}) copy-start(s32[32]{0:T(128)} %param.14) | copy-start | bytes 388
  33.8 12.7 %copy-start.11 = (s32[32]{0:T(128)S(1)}, s32[32]{0:T(128)}, u32[]{:S(2)}) copy-start(s32[32]{0:T(128)} %param.17) | copy-start | bytes 388
  33.8 131.9 %all-to-all-start.1 = ((bf16[32,2,160,256]{3,2,1,0:T(8,128)(2,1)}), bf16[32,2,160,256]{3,2,1,0:T(8,128)(2,1)}, u32[]{:S(2)}, u32[]{:S(2)}) async-start(bf16[32,2,160,256]{3,2,1,0:T(8,128)(2,1)} %pad_maximum_fusion), calls=%async_computation.1 | async-start | bytes 10485760 | tf_op jit(solution)/shard_map/all_to_all | solution.py:267
  45.6 209.1 %reduce-scatter.2.cloned.1.call-start = ((), (), s32[]{:S(2)}) async-start(), calls=%async_computation.3 | async-start | bytes 4718592 | tf_op jit(solution)/shard_map/reduce_scatter | solution.py:340
  45.8 4.1 %copy-start.3 = (bf16[1024,2048]{1,0:T(8,128)(2,1)S(1)}, bf16[1024,2048]{1,0:T(8,128)(2,1)}, u32[]{:S(2)}) copy-start(bf16[1024,2048]{1,0:T(8,128)(2,1)} %param.10) | copy-start | bytes 12582916
  71.3 6.7 %copy-start.4 = (bf16[1024,1,256]{0,2,1:T(8,128)(2,1)S(1)}, bf16[1024,1,256]{0,2,1:T(8,128)(2,1)}, u32[]{:S(2)}) copy-start(bf16[1024,1,256]{0,2,1:T(8,128)(2,1)} %slice.51) | copy-start | bytes 1572868
  71.3 10.3 %copy-start.5 = (s32[32,32,1]{1,2,0:T(1,128)S(1)}, s32[32,32,1]{1,2,0:T(1,128)}, u32[]{:S(2)}) copy-start(s32[32,32,1]{1,2,0:T(1,128)} %param.16) | copy-start | bytes 12292
  168.0 17.8 %copy-start.2 = (bf16[16,2,128,256]{3,2,1,0:T(8,128)(2,1)S(1)}, bf16[16,2,128,256]{3,2,1,0:T(8,128)(2,1)}, u32[]{:S(2)}) copy-start(bf16[16,2,128,256]{3,2,1,0:T(8,128)(2,1)} %param.13) | copy-start | bytes 6291460
  168.0 17.8 %copy-start.9 = (s32[32,32]{1,0:T(8,128)S(1)}, s32[32,32]{1,0:T(8,128)}, u32[]{:S(2)}) copy-start(s32[32,32]{1,0:T(8,128)} %param.15) | copy-start | bytes 12292
  210.5 44.2 %copy-start.1 = (bf16[2048,3,256]{2,0,1:T(8,128)(2,1)S(1)}, bf16[2048,3,256]{2,0,1:T(8,128)(2,1)}, u32[]{:S(2)}) copy-start(bf16[2048,3,256]{2,0,1:T(8,128)(2,1)} %param.11) | copy-start | bytes 9437188
Sparse Core Ops, SparseCore 0:
  215.3 39.2 reduce-scatter.1

commit v9 on v8

--- a/solution.py
+++ b/solution.py
@@ -36,9 +36,11 @@
 
 
 def attend_kernel(
-    live_ref, kpm_ref, kpe_ref, q_ref, mk_ref, mv_ref, ek_ref, ev_ref, nk_ref, nv_ref, out_ref
+    live_ref, kpm_ref, kpe_ref, q_ref, mk_ref, mv_ref, ek_ref, ev_ref, nk_ref, nv_ref, w_ref,
+    out_ref, acc_ref
 ):
-    block = pl.program_id(1)
+    block = pl.program_id(0)
+    head = pl.program_id(1)
     live = live_ref[0]
     main_span = mk_ref.shape[0] * mk_ref.shape[1]
     extra_span = ek_ref.shape[0] * ek_ref.shape[1]
@@ -83,38 +85,54 @@
         + weighted(extra_w, ev_ref[...].reshape(extra_span, HD))
         + weighted(new_w, nv_ref[...])
     )
-    out_ref[...] = (summed / row_total).astype(out_ref.dtype)
-
-
-def attend(live, query, main_pages, main_pos, extra_pages, extra_pos, new_key, new_value):
+    attended = (summed / row_total).astype(jnp.bfloat16)
+    part = jnp.dot(attended, w_ref[...], preferred_element_type=jnp.float32)
+
+    @pl.when(head == 0)
+    def _():
+        acc_ref[...] = part
+
+    @pl.when(head != 0)
+    def _():
+        acc_ref[...] += part
+
+    @pl.when(head == pl.num_programs(1) - 1)
+    def _():
+        out_ref[...] = acc_ref[...].astype(out_ref.dtype)
+
+
+def attend(live, query, main_pages, main_pos, extra_pages, extra_pos, new_key, new_value, out_weight):
     rows, width = query.shape
     heads = width // HD
     main_n = main_pages.shape[0]
     extra_n = extra_pages.shape[0]
+    model_width = out_weight.shape[1]
     grid_spec = pltpu.PrefetchScalarGridSpec(
         num_scalar_prefetch=1,
-        grid=(heads, rows // BLOCK_Q),
+        grid=(rows // BLOCK_Q, heads),
         in_specs=[
-            pl.BlockSpec((1, main_n * PAGE), lambda h, b, live: (0, 0)),
-            pl.BlockSpec((1, extra_n * PAGE), lambda h, b, live: (0, 0)),
-            pl.BlockSpec((BLOCK_Q, HD), lambda h, b, live: (b, h)),
-            pl.BlockSpec((main_n, None, PAGE, HD), lambda h, b, live: (0, 0, 0, h)),
-            pl.BlockSpec((main_n, None, PAGE, HD), lambda h, b, live: (0, 1, 0, h)),
-            pl.BlockSpec((extra_n, None, PAGE, HD), lambda h, b, live: (0, 0, 0, h)),
-            pl.BlockSpec((extra_n, None, PAGE, HD), lambda h, b, live: (0, 1, 0, h)),
-            pl.BlockSpec((rows, HD), lambda h, b, live: (0, h)),
-            pl.BlockSpec((rows, HD), lambda h, b, live: (0, h)),
+            pl.BlockSpec((1, main_n * PAGE), lambda b, h, live: (0, 0)),
+            pl.BlockSpec((1, extra_n * PAGE), lambda b, h, live: (0, 0)),
+            pl.BlockSpec((BLOCK_Q, HD), lambda b, h, live: (b, h)),
+            pl.BlockSpec((main_n, None, PAGE, HD), lambda b, h, live: (0, 0, 0, h)),
+            pl.BlockSpec((main_n, None, PAGE, HD), lambda b, h, live: (0, 1, 0, h)),
+            pl.BlockSpec((extra_n, None, PAGE, HD), lambda b, h, live: (0, 0, 0, h)),
+            pl.BlockSpec((extra_n, None, PAGE, HD), lambda b, h, live: (0, 1, 0, h)),
+            pl.BlockSpec((rows, HD), lambda b, h, live: (0, h)),
+            pl.BlockSpec((rows, HD), lambda b, h, live: (0, h)),
+            pl.BlockSpec((HD, model_width), lambda b, h, live: (h, 0)),
         ],
-        out_specs=pl.BlockSpec((BLOCK_Q, HD), lambda h, b, live: (b, h)),
+        out_specs=pl.BlockSpec((BLOCK_Q, model_width), lambda b, h, live: (b, 0)),
+        scratch_shapes=[pltpu.VMEM((BLOCK_Q, model_width), jnp.float32)],
     )
     keys_n = (main_n + extra_n) * PAGE + rows
     return pl.pallas_call(
         attend_kernel,
         grid_spec=grid_spec,
-        out_shape=jax.ShapeDtypeStruct((rows, width), jnp.bfloat16),
+        out_shape=jax.ShapeDtypeStruct((rows, model_width), jnp.bfloat16),
         compiler_params=pltpu.CompilerParams(vmem_limit_bytes=56 * 1024 * 1024),
         cost_estimate=pl.CostEstimate(
-            flops=4 * rows * keys_n * width,
+            flops=4 * rows * keys_n * width + 2 * rows * width * model_width,
             transcendentals=rows * keys_n * heads,
             bytes_accessed=2 * (2 * keys_n * width + 2 * rows * width),
         ),
@@ -129,6 +147,7 @@
         extra_pages,
         new_key,
         new_value,
+        out_weight,
     )
 
 
@@ -278,7 +297,7 @@
     )
     extra = relayed[src_holder * RELAY_A + jnp.clip(src_index, 0, RELAY_A - 1)]
     extra = extra.transpose(0, 2, 1, 3, 4).reshape(rows, 2, RELAY_B * frag, width)
-    returned = swap_pieces(extra)
+    returned = swap_pieces(extra.reshape(rows, -1, width)).reshape(extra.shape)
     extra_pages = (
         returned.reshape(req_count, 2, RELAY_B, frag, width)
         .transpose(2, 1, 0, 3, 4)
@@ -318,26 +337,44 @@
         kv_pool, page_slot, holder_rows, rank_all, req_index, req_count
     )
     query_rot, new_key, new_value = project(hidden_in, qkv_weight, live_len, local_heads, local_width)
-    attended = attend(
-        live_len, query_rot, main_pages, main_pos, extra_pages, extra_pos, new_key, new_value
+    head_term = attend(
+        live_len,
+        query_rot,
+        main_pages,
+        main_pos,
+        extra_pages,
+        extra_pos,
+        new_key,
+        new_value,
+        out_weight,
     )
 
     def keep(ops):
         return ops[0]
 
     def redo(ops):
-        _, query, key, value, pool, slots, holders, ranks, live = ops
+        _, query, key, value, pool, slots, holders, ranks, live, weight_out = ops
         pages, pos, extra, extra_at = exchange_wide(pool, slots, holders, ranks, req_index, req_count)
-        return attend(live, query, pages, pos, extra, extra_at, key, value)
-
-    attended = lax.cond(
+        return attend(live, query, pages, pos, extra, extra_at, key, value, weight_out)
+
+    head_term = lax.cond(
         relay_fits,
         keep,
         redo,
-        (attended, query_rot, new_key, new_value, kv_pool, page_slot, holder_rows, rank_all, live_len),
-    )
-    head_term = jnp.dot(attended, out_weight, preferred_element_type=jnp.float32)
-    return lax.psum_scatter(head_term.astype(jnp.bfloat16), "tp", scatter_dimension=0, tiled=True)
+        (
+            head_term,
+            query_rot,
+            new_key,
+            new_value,
+            kv_pool,
+            page_slot,
+            holder_rows,
+            rank_all,
+            live_len,
+            out_weight,
+        ),
+    )
+    return lax.psum_scatter(head_term, "tp", scatter_dimension=0, tiled=True)
 
 
 def solution(mesh):

time: 262 us -> 267 us (1.019)
  Pallas kernels: 37 us -> 42 us
  matrix products: 8.76 us -> 4.04 us
  local copies, waits for them, and re-layouts: 36.4 us -> 41.1 us
    pallas_call x1, Pallas kernels: 24.6 us -> 29.6 us  [attend(): pl.pallas_call(attend_kernel, grid_spec=grid_spec, out_shape=jax.ShapeDty...]
    cond x0 -> x1, local copies, waits for them, and re-layouts: none -> 4.75 us
    dot_general x1 -> x0, matrix products: 4.72 us -> none  [body(): jnp.dot(attended, out_weight, preferred_element_type=jnp.float32)]
where the time goes in v9:
time: 267 us
  waiting for transfers between devices  122 us (46%)
  Pallas kernels  42 us (16%)
  local copies, waits for them, and re-layouts  41.1 us (15%)
  other arithmetic  28.2 us (11%)
  between operations  17.7 us (7%)
  starting transfers between devices  11.8 us (4%)
  matrix products  4.04 us (2%)
    all_to_all x1, waiting for transfers between devices, exchange_relay(): lax.all_to_all(outgoing, 'req', split_axis=0, concat_axis=0, tiled=True)  82.3 us
    reduce_scatter x1, waiting for transfers between devices, body(): return lax.psum_scatter(head_term, 'tp', scatter_dimension=0, tiled=True)  39.4 us
    pallas_call x1, Pallas kernels, attend(): pl.pallas_call(attend_kernel, grid_spec=grid_spec, out_shape=jax.ShapeDty...  29.6 us
    pallas_call x1, Pallas kernels, swap_pieces(): pl.pallas_call(swap_kernel, out_shape=jax.ShapeDtypeStruct(pieces.shape,...  12.4 us
    all_to_all x1, starting transfers between devices, exchange_relay(): lax.all_to_all(outgoing, 'req', split_axis=0, concat_axis=0, tiled=True)  11.8 us
    unnamed x25, local copies, waits for them, and re-layouts  8.45 us
    reshape x3, local copies, waits for them, and re-layouts, exchange_relay(): pieces = kv_pool[slot_a].reshape(RELAY_A, 2, req_count, frag, width).tran...  7.13 us
    concatenate x1, other arithmetic, exchange_relay(): outgoing = jnp.concatenate([kv_pool[send_slots], pieces], axis=2)  5.38 us
  transfers between devices with their start and end apart: 2, of which 2 were waited for; matrix products, arithmetic and copies ran while one was open for 13% of the time, Pallas kernels for 0%

profile of v9, /device:TPU:2, one launch (start us, length us, event | category | flops | bytes accessed | tf_op | source)
XLA Modules:
  0.0 266.6 jit_solution(13055662201383083431)
XLA Ops:
  6.5 1.7 convert_reduce_fusion.1
  10.6 1.1 select_reduce_fusion.2
  11.8 1.5 select_reduce_fusion.4
  13.7 3.2 %gather_fusion.2 = bf16[8,2,128,256]{3,2,1,0:T(8,128)(2,1)} fusion(bf16[16,2,128,256]{3,2,1,0:T(8,128)(2,1)} %param.13, s32[1024]{0:T(1024)S(1)} %pad_clamp_fusion.2), kind=kCustom, calls=%fused_computation.2 | custom fusion | bytes 2097184 | tf_op jit(solution)/shard_map/gather | solution.py:280
  16.9 2.2 reshape.419
  19.1 2.8 %copy.65 = bf16[8,2,32,4,256]{4,3,0,1,2:T(4,128)(2,1)} copy(bf16[8,2,32,4,256]{4,3,2,1,0:T(4,128)(2,1)} %reshape.419) | data formatting | bytes 2097152 | tf_op jit(solution)/shard_map/reshape | solution.py:281
  21.9 2.1 reshape.420
  24.1 4.3 %gather_fusion.1 = bf16[32,2,128,256]{3,2,1,0:T(8,128)(2,1)} fusion(bf16[16,2,128,256]{3,2,1,0:T(8,128)(2,1)} %param.13, s32[1024]{0:T(1024)S(1)} %pad_clamp_fusion.3), kind=kCustom, calls=%fused_computation.1 | custom fusion | bytes 8388736 | tf_op jit(solution)/shard_map/gather | solution.py:285
  28.4 5.4 %pad_maximum_fusion = bf16[32,2,160,256]{3,2,1,0:T(8,128)(2,1)} fusion(bf16[32,2,32,256]{3,2,1,0:T(8,128)(2,1)} %reshape.420, bf16[32,2,128,256]{3,2,1,0:T(8,128)(2,1)} %gather_fusion.1), kind=kLoop, calls=%fused_computation.23 | loop fusion | flops 10485760 | bytes 10485760 | tf_op jit(solution)/shard_map/concatenate | solution.py:285
  33.8 11.8 %all-to-all-start.1 = ((bf16[32,2,160,256]{3,2,1,0:T(8,128)(2,1)}), bf16[32,2,160,256]{3,2,1,0:T(8,128)(2,1)}, u32[]{:S(2)}, u32[]{:S(2)}) async-start(bf16[32,2,160,256]{3,2,1,0:T(8,128)(2,1)} %pad_maximum_fusion), calls=%async_computation.1 | async-start | bytes 10485760 | tf_op jit(solution)/shard_map/all_to_all | solution.py:286
  47.1 2.8 %convert_reduce_fusion = f32[1024]{0:T(1024)S(1)} fusion(bf16[1024,2048]{1,0:T(8,128)(2,1)} %param.10), kind=kLoop, calls=%fused_computation.18 | loop fusion | flops 4193280 | bytes 4198400 | tf_op jit(solution)/shard_map/reduce_sum | solution.py:221
  49.9 1.2 fusion.3
  51.2 4.0 %fusion.6 = f32[1024,3,256]{0,2,1:T(8,128)S(1)} fusion(bf16[2048,3,256]{2,0,1:T(8,128)(2,1)S(1)} %copy-done, bf16[1024,2048]{1,0:T(8,128)(2,1)S(1)} %copy-done.3, f32[1024]{0:T(1024)S(1)} %add_rsqrt_fusion, f32[1024]{0:T(1024)S(1)} %broadcast_multiply_fusion.1), kind=kOutput, calls=%fused_computation.25 | convolution fusion | flops 3229614080 | bytes 10493952 | tf_op jit(solution)/shard_map/td,dcf->tcf/dot_general | solution.py:225
  56.4 0.9 fusion.23
  57.8 1.5 copy.53
  59.3 1.1 fusion.22
  60.4 1.4 copy.54
  61.9 2.2 copy.55
  65.4 1.9 multiply_cosine_fusion
  67.3 3.9 %subtract_convert_fusion = (bf16[1024,2,64]{2,1,0:T(2,128)(2,1)S(1)}, bf16[1024,2,64]{2,1,0:T(2,128)(2,1)S(1)}, bf16[1024,2,64]{2,1,0:T(2,128)(2,1)S(1)}, bf16[1024,2,64]{2,1,0:T(2,128)(2,1)S(1)}) fusion(f32[1024,2,64]{2,1,0:T(2,128)} %copy.55, f32[1024,2,64]{2,1,0:T(2,128)S(1)} %copy.54, f32[1024,64]{1,0:T(8,128)S(1)} %get-tuple-element.61, ...), kind=kLoop, calls=%fused_computation.31 | loop fusion | flops 2097152 | bytes 3670016 | tf_op jit(solution)/shard_map/convert.1
  71.2 2.9 %pad_maximum_fusion.1 = (bf16[1024,2,128]{2,1,0:T(2,128)(2,1)S(1)}, bf16[1024,2,128]{2,1,0:T(2,128)(2,1)S(1)}) fusion(bf16[1024,2,64]{2,1,0:T(2,128)(2,1)S(1)} %get-tuple-element.53, bf16[1024,2,64]{2,1,0:T(2,128)(2,1)S(1)} %get-tuple-element.54, bf16[1024,2,64]{2,1,0:T(2,128)(2,1)S(1)} %get-tuple-element.48, bf16[1024,2,64]{2,1,0:T(2,128)(2,1)S(1)} %get-tuple-element.47), kind=kLoop, calls=%fused_computation.40 | loop fusion | flops 2097152 | bytes 2097152 | tf_op jit(solution)/shard_map/concatenate | solution.py:29
  74.1 0.9 copy.66
  78.1 1.0 copy.56
  83.4 82.3 %all-to-all-done.1.mk_ref.mv_ref = bf16[32,2,160,256]{3,2,1,0:T(8,128)(2,1)} async-done(((bf16[32,2,160,256]{3,2,1,0:T(8,128)(2,1)}), bf16[32,2,160,256]{3,2,1,0:T(8,128)(2,1)}, u32[]{:S(2)}, u32[]{:S(2)}) %all-to-all-start.1) | async-done | bytes 5242912 | tf_op jit(solution)/shard_map/all_to_all | solution.py:286
  165.7 2.4 slice.52
  168.0 1.5 reshape.421
  171.9 12.4 %shard_map.82 = bf16[32,8,256]{2,1,0:T(8,128)(2,1)} custom-call(bf16[32,8,256]{2,1,0:T(8,128)(2,1)} %reshape_reshape_transpose.3.send_ref), custom_call_target="tpu_custom_call" | custom-call | tf_op jit(solution)/shard_map/pallas_call | solution.py:204
  184.2 0.9 reshape_reshape.3
  185.9 29.6 %shard_map.83 = bf16[1024,2048]{1,0:T(8,128)(2,1)} custom-call(s32[1]{0:T(128)} %mul.171.live_ref, s32[1,4096]{1,0:T(1,128)} %bitcast.92, s32[1,128]{1,0:T(1,128)} %broadcast_select_fusion.kpe_ref, bf16[1024,256]{1,0:T(8,128)(2,1)} %bitcast.86, bf16[32,2,160,256]{3,2,1,0:T(8,128)(2,1)} %all-to-all-done.1.mk_ref.mv_ref, ...), custom_call_target="tpu_custom_call" | custom-call | flops 6576668672 | bytes 6422528 | tf_op jit(solution)/shard_map/pallas_call | solution.py:129
  215.5 4.8 %conditional.1 = (bf16[1024,2048]{1,0:T(8,128)(2,1)}) conditional(s32[]{:T(128)} %convert_element_type.68, (s32[]{:T(128)}, s32[32,32]{1,0:T(8,128)S(1)}, s32[32,32]{1,0:T(8,128)S(1)}, s32[32,32]{1,0:T(8,128)S(1)}, bf16[16,2,128,256]{3,2,1,0:T(8,128)(2,1)S(1)}, /*index=5*/s32[1]{0:T(128)}, bf16[1024,256]{1,0:T(8,128)(2,1)}, ...), branch_computations={%region_17.21_spmd, %region_21.22_spmd} | conditional | flops 10871702528 | bytes 63384396 | solution.py:360
  215.5 4.7 %copy.70 = bf16[1024,2048]{1,0:T(8,128)(2,1)} copy(bf16[1024,2048]{1,0:T(8,128)(2,1)} %param.1) | data formatting | bytes 8388608 | tf_op jit(solution)/shard_map/cond
  220.3 39.4 %reduce-scatter.2.cloned.1.call-done = bf16[128,2048]{1,0:T(8,128)(2,1)} async-done(((bf16[1024,2048]{1,0:T(8,128)(2,1)}), bf16[128,2048]{1,0:T(8,128)(2,1)}) %reduce-scatter.2.cloned.1.call-update) | async-done | bytes 524304 | tf_op jit(solution)/shard_map/reduce_scatter | solution.py:377
  (67 shorter events, 13.8 us)
Async XLA Ops:
  6.5 44.7 %copy-start = (bf16[2048,3,256]{2,0,1:T(8,128)(2,1)S(1)}, bf16[2048,3,256]{2,0,1:T(8,128)(2,1)}, u32[]{:S(2)}) copy-start(bf16[2048,3,256]{2,0,1:T(8,128)(2,1)} %param.11) | copy-start | bytes 9437188
  33.8 12.0 %copy-start.11 = (s32[32]{0:T(128)S(1)}, s32[32]{0:T(128)}, u32[]{:S(2)}) copy-start(s32[32]{0:T(128)} %param.14) | copy-start | bytes 388
  33.8 12.6 %copy-start.12 = (s32[32]{0:T(128)S(1)}, s32[32]{0:T(128)}, u32[]{:S(2)}) copy-start(s32[32]{0:T(128)} %param.17) | copy-start | bytes 388
  33.8 131.9 %all-to-all-start.1 = ((bf16[32,2,160,256]{3,2,1,0:T(8,128)(2,1)}), bf16[32,2,160,256]{3,2,1,0:T(8,128)(2,1)}, u32[]{:S(2)}, u32[]{:S(2)}) async-start(bf16[32,2,160,256]{3,2,1,0:T(8,128)(2,1)} %pad_maximum_fusion), calls=%async_computation.1 | async-start | bytes 10485760 | tf_op jit(solution)/shard_map/all_to_all | solution.py:286
  45.6 214.1 %reduce-scatter.2.cloned.1.call-start = ((), (), s32[]{:S(2)}) async-start(), calls=%async_computation.3 | async-start | bytes 4718592 | tf_op jit(solution)/shard_map/reduce_scatter | solution.py:377
  45.8 4.1 %copy-start.3 = (bf16[1024,2048]{1,0:T(8,128)(2,1)S(1)}, bf16[1024,2048]{1,0:T(8,128)(2,1)}, u32[]{:S(2)}) copy-start(bf16[1024,2048]{1,0:T(8,128)(2,1)} %param.10) | copy-start | bytes 12582916
  71.2 6.9 %copy-start.4 = (bf16[1024,1,256]{0,2,1:T(8,128)(2,1)S(1)}, bf16[1024,1,256]{0,2,1:T(8,128)(2,1)}, u32[]{:S(2)}) copy-start(bf16[1024,1,256]{0,2,1:T(8,128)(2,1)} %slice.51) | copy-start | bytes 1572868
  71.2 10.6 %copy-start.5 = (s32[32,32,1]{1,2,0:T(1,128)S(1)}, s32[32,32,1]{1,2,0:T(1,128)}, u32[]{:S(2)}) copy-start(s32[32,32,1]{1,2,0:T(1,128)} %param.16) | copy-start | bytes 12292
  168.0 17.9 %copy-start.2 = (bf16[16,2,128,256]{3,2,1,0:T(8,128)(2,1)S(1)}, bf16[16,2,128,256]{3,2,1,0:T(8,128)(2,1)}, u32[]{:S(2)}) copy-start(bf16[16,2,128,256]{3,2,1,0:T(8,128)(2,1)} %param.13) | copy-start | bytes 6291460
  168.0 17.9 %copy-start.9 = (s32[32,32]{1,0:T(8,128)S(1)}, s32[32,32]{1,0:T(8,128)}, u32[]{:S(2)}) copy-start(s32[32,32]{1,0:T(8,128)} %param.15) | copy-start | bytes 12292
  220.3 39.4 %copy-start.1 = (bf16[2048,3,256]{2,0,1:T(8,128)(2,1)S(1)}, bf16[2048,3,256]{2,0,1:T(8,128)(2,1)}, u32[]{:S(2)}) copy-start(bf16[2048,3,256]{2,0,1:T(8,128)(2,1)} %param.11) | copy-start | bytes 9437188
Sparse Core Ops, SparseCore 0:
  220.4 39.2 reduce-scatter.1

commit v10 on v8

--- a/solution.py
+++ b/solution.py
@@ -263,7 +263,8 @@
         .transpose(2, 1, 0, 3, 4)
         .reshape(req_count, 2, RELAY_A * frag, width)
     )
-    outgoing = jnp.concatenate([kv_pool[send_slots], pieces], axis=2)
+    padded = jnp.pad(kv_pool, ((0, 0), (0, 0), (0, RELAY_A * frag), (0, 0)))
+    outgoing = padded[send_slots].at[:, :, PAGE:, :].set(pieces)
     incoming = lax.all_to_all(outgoing, "req", split_axis=0, concat_axis=0, tiled=True)
     relayed = (
         incoming[:, :, PAGE:]

time: 262 us -> 262 us (level)
    concatenate x1 -> x0, other arithmetic: 5.38 us -> none  [exchange_relay(): outgoing = jnp.concatenate([kv_pool[send_slots], pieces], axis=2)]
    scatter x0 -> x1, other arithmetic: none -> 5.38 us  [exchange_relay(): outgoing = padded[send_slots].at[:, :, PAGE:, :].set(pieces)]
    reshape x3 -> x2, local copies, waits for them, and re-layouts: 7.13 us -> 4.99 us  [exchange_relay(): pieces = kv_pool[slot_a].reshape(RELAY_A, 2, req_count, frag, width).tran...]
where the time goes in v10:
time: 262 us; the launch traced here: 261 us
  waiting for transfers between devices  122 us (47%)
  Pallas kernels  37 us (14%)
  local copies, waits for them, and re-layouts  36.4 us (14%)
  other arithmetic  28 us (11%)
  between operations  17.5 us (7%)
  starting transfers between devices  11.8 us (5%)
  matrix products  8.76 us (3%)
    all_to_all x1, waiting for transfers between devices, exchange_relay(): lax.all_to_all(outgoing, 'req', split_axis=0, concat_axis=0, tiled=True)  82.5 us
    reduce_scatter x1, waiting for transfers between devices, body(): lax.psum_scatter(head_term.astype(jnp.bfloat16), 'tp', scatter_dimension=...  39.4 us
    pallas_call x1, Pallas kernels, attend(): pl.pallas_call(attend_kernel, grid_spec=grid_spec, out_shape=jax.ShapeDty...  24.6 us
    pallas_call x1, Pallas kernels, swap_pieces(): pl.pallas_call(swap_kernel, out_shape=jax.ShapeDtypeStruct(pieces.shape,...  12.4 us
    all_to_all x1, starting transfers between devices, exchange_relay(): lax.all_to_all(outgoing, 'req', split_axis=0, concat_axis=0, tiled=True)  11.8 us
    unnamed x25, local copies, waits for them, and re-layouts  8.44 us
    scatter x1, other arithmetic, exchange_relay(): outgoing = padded[send_slots].at[:, :, PAGE:, :].set(pieces)  5.38 us
  transfers between devices with their start and end apart: 2, of which 2 were waited for; matrix products, arithmetic and copies ran while one was open for 13% of the time, Pallas kernels for 0%

profile of v10, /device:TPU:2, one launch (start us, length us, event | category | flops | bytes accessed | tf_op | source)
XLA Modules:
  0.0 261.5 jit_solution(2204549483790056178)
XLA Ops:
  6.5 1.7 convert_reduce_fusion.1
  10.6 1.1 select_reduce_fusion.2
  11.8 1.5 select_reduce_fusion.4
  13.7 3.2 %gather_fusion.2 = bf16[8,2,128,256]{3,2,1,0:T(8,128)(2,1)} fusion(bf16[16,2,128,256]{3,2,1,0:T(8,128)(2,1)} %param.15, s32[1024]{0:T(1024)S(1)} %pad_clamp_fusion.2), kind=kCustom, calls=%fused_computation.2 | custom fusion | bytes 2097184 | tf_op jit(solution)/shard_map/gather | solution.py:261
  16.9 2.2 reshape.458
  19.1 2.8 %copy.63 = bf16[8,2,32,4,256]{4,3,0,1,2:T(4,128)(2,1)} copy(bf16[8,2,32,4,256]{4,3,2,1,0:T(4,128)(2,1)} %reshape.458) | data formatting | bytes 2097152 | tf_op jit(solution)/shard_map/reshape | solution.py:262
  21.9 2.1 reshape.459
  24.1 4.3 %gather_fusion.1 = bf16[32,2,128,256]{3,2,1,0:T(8,128)(2,1)} fusion(bf16[16,2,128,256]{3,2,1,0:T(8,128)(2,1)} %param.15, s32[1024]{0:T(1024)S(1)} %pad_clamp_fusion.3), kind=kCustom, calls=%fused_computation.1 | custom fusion | bytes 8388736 | tf_op jit(solution)/shard_map/gather | solution.py:267
  28.4 5.4 %pad_maximum_fusion = bf16[32,2,160,256]{3,2,1,0:T(8,128)(2,1)} fusion(bf16[32,2,32,256]{3,2,1,0:T(8,128)(2,1)} %reshape.459, bf16[32,2,128,256]{3,2,1,0:T(8,128)(2,1)} %gather_fusion.1), kind=kLoop, calls=%fused_computation.23 | loop fusion | flops 10485760 | bytes 10485760 | tf_op jit(solution)/shard_map/scatter | solution.py:267
  33.8 11.8 %all-to-all-start.1 = ((bf16[32,2,160,256]{3,2,1,0:T(8,128)(2,1)}), bf16[32,2,160,256]{3,2,1,0:T(8,128)(2,1)}, u32[]{:S(2)}, u32[]{:S(2)}) async-start(bf16[32,2,160,256]{3,2,1,0:T(8,128)(2,1)} %pad_maximum_fusion), calls=%async_computation.1 | async-start | bytes 10485760 | tf_op jit(solution)/shard_map/all_to_all | solution.py:268
  47.2 2.8 %convert_reduce_fusion = f32[1024]{0:T(1024)S(1)} fusion(bf16[1024,2048]{1,0:T(8,128)(2,1)} %param.12), kind=kLoop, calls=%fused_computation.18 | loop fusion | flops 4193280 | bytes 4198400 | tf_op jit(solution)/shard_map/reduce_sum | solution.py:202
  50.0 1.2 fusion.3
  51.2 4.0 %fusion.6 = f32[1024,3,256]{0,2,1:T(8,128)S(1)} fusion(bf16[2048,3,256]{2,0,1:T(8,128)(2,1)S(1)} %copy-done, bf16[1024,2048]{1,0:T(8,128)(2,1)S(1)} %copy-done.3, f32[1024]{0:T(1024)S(1)} %add_rsqrt_fusion, f32[1024]{0:T(1024)S(1)} %broadcast_multiply_fusion.1), kind=kOutput, calls=%fused_computation.25 | convolution fusion | flops 3229614080 | bytes 10493952 | tf_op jit(solution)/shard_map/td,dcf->tcf/dot_general | solution.py:206
  56.4 0.9 fusion.23
  57.9 1.5 copy.52
  59.3 1.1 fusion.22
  60.4 1.4 copy.53
  61.9 2.2 copy.54
  65.5 1.9 multiply_cosine_fusion
  67.4 3.9 %subtract_convert_fusion = (bf16[1024,2,64]{2,1,0:T(2,128)(2,1)S(1)}, bf16[1024,2,64]{2,1,0:T(2,128)(2,1)S(1)}, bf16[1024,2,64]{2,1,0:T(2,128)(2,1)S(1)}, bf16[1024,2,64]{2,1,0:T(2,128)(2,1)S(1)}) fusion(f32[1024,2,64]{2,1,0:T(2,128)} %copy.54, f32[1024,2,64]{2,1,0:T(2,128)S(1)} %copy.53, f32[1024,64]{1,0:T(8,128)S(1)} %get-tuple-element.70, ...), kind=kLoop, calls=%fused_computation.32 | loop fusion | flops 2097152 | bytes 3670016 | tf_op jit(solution)/shard_map/convert.1
  71.3 2.9 %pad_maximum_fusion.1 = (bf16[1024,2,128]{2,1,0:T(2,128)(2,1)S(1)}, bf16[1024,2,128]{2,1,0:T(2,128)(2,1)S(1)}) fusion(bf16[1024,2,64]{2,1,0:T(2,128)(2,1)S(1)} %get-tuple-element.62, bf16[1024,2,64]{2,1,0:T(2,128)(2,1)S(1)} %get-tuple-element.63, bf16[1024,2,64]{2,1,0:T(2,128)(2,1)S(1)} %get-tuple-element.57, bf16[1024,2,64]{2,1,0:T(2,128)(2,1)S(1)} %get-tuple-element.56), kind=kLoop, calls=%fused_computation.41 | loop fusion | flops 2097152 | bytes 2097152 | tf_op jit(solution)/shard_map/concatenate | solution.py:29
  75.1 0.9 copy.65
  78.1 1.0 copy.55
  83.2 82.5 %all-to-all-done.1.mk_ref.mv_ref = bf16[32,2,160,256]{3,2,1,0:T(8,128)(2,1)} async-done(((bf16[32,2,160,256]{3,2,1,0:T(8,128)(2,1)}), bf16[32,2,160,256]{3,2,1,0:T(8,128)(2,1)}, u32[]{:S(2)}, u32[]{:S(2)}) %all-to-all-start.1) | async-done | bytes 5242912 | tf_op jit(solution)/shard_map/all_to_all | solution.py:268
  165.7 2.4 slice.79
  168.0 1.5 reshape.460
  170.5 1.3 gather_fusion.3
  171.8 12.4 %shard_map.82 = bf16[32,2,4,256]{3,2,1,0:T(4,128)(2,1)} custom-call(bf16[32,2,4,256]{3,2,1,0:T(4,128)(2,1)} %gather_fusion.3), custom_call_target="tpu_custom_call" | custom-call | tf_op jit(solution)/shard_map/pallas_call | solution.py:185
  184.2 1.0 copy.49
  185.8 24.6 %shard_map.83 = bf16[1024,256]{1,0:T(8,128)(2,1)} custom-call(s32[1]{0:T(128)} %mul.171.live_ref, s32[1,4096]{1,0:T(1,128)} %bitcast.94, s32[1,128]{1,0:T(1,128)} %broadcast_select_fusion.kpe_ref, bf16[1024,256]{1,0:T(8,128)(2,1)} %bitcast.88, bf16[32,2,160,256]{3,2,1,0:T(8,128)(2,1)} %all-to-all-done.1.mk_ref.mv_ref, ...), custom_call_target="tpu_custom_call" | custom-call | flops 5502926848 | bytes 6422528 | tf_op jit(solution)/shard_map/pallas_call | solution.py:111
  210.5 4.7 %convolution_convert_fusion = bf16[1024,2048]{1,0:T(8,128)(2,1)} fusion(bf16[1024,256]{1,0:T(8,128)(2,1)} %get-tuple-element.73, bf16[256,2048]{1,0:T(8,128)(2,1)} %param.14), kind=kOutput, calls=%fused_computation.28 | convolution fusion | flops 1075838976 | bytes 5767168 | tf_op jit(solution)/shard_map/dot_general | solution.py:340
  215.2 39.4 %reduce-scatter.2.cloned.1.call-done = bf16[128,2048]{1,0:T(8,128)(2,1)} async-done(((bf16[1024,2048]{1,0:T(8,128)(2,1)}), bf16[128,2048]{1,0:T(8,128)(2,1)}) %reduce-scatter.2.cloned.1.call-update) | async-done | bytes 524304 | tf_op jit(solution)/shard_map/reduce_scatter | solution.py:341
  (65 shorter events, 12.3 us)
Async XLA Ops:
  6.5 44.7 %copy-start = (bf16[2048,3,256]{2,0,1:T(8,128)(2,1)S(1)}, bf16[2048,3,256]{2,0,1:T(8,128)(2,1)}, u32[]{:S(2)}) copy-start(bf16[2048,3,256]{2,0,1:T(8,128)(2,1)} %param.13) | copy-start | bytes 9437188
  33.8 12.0 %copy-start.10 = (s32[32]{0:T(128)S(1)}, s32[32]{0:T(128)}, u32[]{:S(2)}) copy-start(s32[32]{0:T(128)} %param.16) | copy-start | bytes 388
  33.8 12.7 %copy-start.11 = (s32[32]{0:T(128)S(1)}, s32[32]{0:T(128)}, u32[]{:S(2)}) copy-start(s32[32]{0:T(128)} %param.19) | copy-start | bytes 388
  33.8 131.9 %all-to-all-start.1 = ((bf16[32,2,160,256]{3,2,1,0:T(8,128)(2,1)}), bf16[32,2,160,256]{3,2,1,0:T(8,128)(2,1)}, u32[]{:S(2)}, u32[]{:S(2)}) async-start(bf16[32,2,160,256]{3,2,1,0:T(8,128)(2,1)} %pad_maximum_fusion), calls=%async_computation.1 | async-start | bytes 10485760 | tf_op jit(solution)/shard_map/all_to_all | solution.py:268
  45.6 209.1 %reduce-scatter.2.cloned.1.call-start = ((), (), s32[]{:S(2)}) async-start(), calls=%async_computation.3 | async-start | bytes 4718592 | tf_op jit(solution)/shard_map/reduce_scatter | solution.py:341
  45.8 4.1 %copy-start.3 = (bf16[1024,2048]{1,0:T(8,128)(2,1)S(1)}, bf16[1024,2048]{1,0:T(8,128)(2,1)}, u32[]{:S(2)}) copy-start(bf16[1024,2048]{1,0:T(8,128)(2,1)} %param.12) | copy-start | bytes 12582916
  71.3 6.7 %copy-start.4 = (bf16[1024,1,256]{0,2,1:T(8,128)(2,1)S(1)}, bf16[1024,1,256]{0,2,1:T(8,128)(2,1)}, u32[]{:S(2)}) copy-start(bf16[1024,1,256]{0,2,1:T(8,128)(2,1)} %slice.78) | copy-start | bytes 1572868
  71.3 10.3 %copy-start.5 = (s32[32,32,1]{1,2,0:T(1,128)S(1)}, s32[32,32,1]{1,2,0:T(1,128)}, u32[]{:S(2)}) copy-start(s32[32,32,1]{1,2,0:T(1,128)} %param.18) | copy-start | bytes 12292
  168.0 17.8 %copy-start.2 = (bf16[16,2,128,256]{3,2,1,0:T(8,128)(2,1)S(1)}, bf16[16,2,128,256]{3,2,1,0:T(8,128)(2,1)}, u32[]{:S(2)}) copy-start(bf16[16,2,128,256]{3,2,1,0:T(8,128)(2,1)} %param.15) | copy-start | bytes 6291460
  168.0 17.8 %copy-start.9 = (s32[32,32]{1,0:T(8,128)S(1)}, s32[32,32]{1,0:T(8,128)}, u32[]{:S(2)}) copy-start(s32[32,32]{1,0:T(8,128)} %param.17) | copy-start | bytes 12292
  210.5 44.2 %copy-start.1 = (bf16[2048,3,256]{2,0,1:T(8,128)(2,1)S(1)}, bf16[2048,3,256]{2,0,1:T(8,128)(2,1)}, u32[]{:S(2)}) copy-start(bf16[2048,3,256]{2,0,1:T(8,128)(2,1)} %param.13) | copy-start | bytes 9437188
Sparse Core Ops, SparseCore 0:
  215.3 39.2 reduce-scatter.1

commit v11 on v10

--- a/solution.py
+++ b/solution.py
@@ -38,52 +38,59 @@
 def attend_kernel(
     live_ref, kpm_ref, kpe_ref, q_ref, mk_ref, mv_ref, ek_ref, ev_ref, nk_ref, nv_ref, out_ref
 ):
-    block = pl.program_id(1)
     live = live_ref[0]
     main_span = mk_ref.shape[0] * mk_ref.shape[1]
     extra_span = ek_ref.shape[0] * ek_ref.shape[1]
-    query = q_ref[...]
     contract = (((1,), (1,)), ((), ()))
     scale = HD ** (-0.5)
-
-    def scores(keys):
-        return lax.dot_general(query, keys, contract, preferred_element_type=jnp.float32) * scale
-
-    main_scores = scores(mk_ref[...].reshape(main_span, HD))
-    extra_scores = scores(ek_ref[...].reshape(extra_span, HD))
-    new_scores = scores(nk_ref[...])
     main_ok = kpm_ref[...] < live
     extra_ok = kpe_ref[...] < live
-    query_pos = block * BLOCK_Q + lax.broadcasted_iota(jnp.int32, new_scores.shape, 0)
-    new_ok = lax.broadcasted_iota(jnp.int32, new_scores.shape, 1) <= query_pos
-    main_scores = jnp.where(main_ok, main_scores, -1e30)
-    extra_scores = jnp.where(extra_ok, extra_scores, -1e30)
-    new_scores = jnp.where(new_ok, new_scores, -1e30)
-    row_top = jnp.maximum(
-        jnp.maximum(
-            jnp.max(main_scores, axis=1, keepdims=True),
-            jnp.max(extra_scores, axis=1, keepdims=True),
-        ),
-        jnp.max(new_scores, axis=1, keepdims=True),
-    )
-    main_w = jnp.exp(main_scores - row_top)
-    extra_w = jnp.exp(extra_scores - row_top)
-    new_w = jnp.exp(new_scores - row_top)
-    row_total = (
-        jnp.sum(main_w, axis=1, keepdims=True)
-        + jnp.sum(extra_w, axis=1, keepdims=True)
-        + jnp.sum(new_w, axis=1, keepdims=True)
-    )
-
-    def weighted(weights, values):
-        return jnp.dot(weights.astype(jnp.bfloat16), values, preferred_element_type=jnp.float32)
-
-    summed = (
-        weighted(main_w, mv_ref[...].reshape(main_span, HD))
-        + weighted(extra_w, ev_ref[...].reshape(extra_span, HD))
-        + weighted(new_w, nv_ref[...])
-    )
-    out_ref[...] = (summed / row_total).astype(out_ref.dtype)
+
+    for block in range(q_ref.shape[0] // BLOCK_Q):
+        rows = pl.ds(block * BLOCK_Q, BLOCK_Q)
+        seen = pl.ds(0, (block + 1) * BLOCK_Q)
+        query = q_ref[rows, :]
+
+        def scores(keys):
+            return (
+                lax.dot_general(query, keys, contract, preferred_element_type=jnp.float32) * scale
+            )
+
+        main_scores = scores(mk_ref[...].reshape(main_span, HD))
+        extra_scores = scores(ek_ref[...].reshape(extra_span, HD))
+        new_scores = scores(nk_ref[seen, :])
+        query_pos = block * BLOCK_Q + lax.broadcasted_iota(jnp.int32, new_scores.shape, 0)
+        new_ok = lax.broadcasted_iota(jnp.int32, new_scores.shape, 1) <= query_pos
+        main_scores = jnp.where(main_ok, main_scores, -1e30)
+        extra_scores = jnp.where(extra_ok, extra_scores, -1e30)
+        new_scores = jnp.where(new_ok, new_scores, -1e30)
+        row_top = jnp.maximum(
+            jnp.maximum(
+                jnp.max(main_scores, axis=1, keepdims=True),
+                jnp.max(extra_scores, axis=1, keepdims=True),
+            ),
+            jnp.max(new_scores, axis=1, keepdims=True),
+        )
+        main_w = jnp.exp(main_scores - row_top)
+        extra_w = jnp.exp(extra_scores - row_top)
+        new_w = jnp.exp(new_scores - row_top)
+        row_total = (
+            jnp.sum(main_w, axis=1, keepdims=True)
+            + jnp.sum(extra_w, axis=1, keepdims=True)
+            + jnp.sum(new_w, axis=1, keepdims=True)
+        )
+
+        def weighted(weights, values):
+            return jnp.dot(
+                weights.astype(jnp.bfloat16), values, preferred_element_type=jnp.float32
+            )
+
+        summed = (
+            weighted(main_w, mv_ref[...].reshape(main_span, HD))
+            + weighted(extra_w, ev_ref[...].reshape(extra_span, HD))
+            + weighted(new_w, nv_ref[seen, :])
+        )
+        out_ref[rows, :] = (summed / row_total).astype(out_ref.dtype)
 
 
 def attend(live, query, main_pages, main_pos, extra_pages, extra_pos, new_key, new_value):
@@ -93,21 +100,21 @@
     extra_n = extra_pages.shape[0]
     grid_spec = pltpu.PrefetchScalarGridSpec(
         num_scalar_prefetch=1,
-        grid=(heads, rows // BLOCK_Q),
+        grid=(heads,),
         in_specs=[
-            pl.BlockSpec((1, main_n * PAGE), lambda h, b, live: (0, 0)),
-            pl.BlockSpec((1, extra_n * PAGE), lambda h, b, live: (0, 0)),
-            pl.BlockSpec((BLOCK_Q, HD), lambda h, b, live: (b, h)),
-            pl.BlockSpec((main_n, None, PAGE, HD), lambda h, b, live: (0, 0, 0, h)),
-            pl.BlockSpec((main_n, None, PAGE, HD), lambda h, b, live: (0, 1, 0, h)),
-            pl.BlockSpec((extra_n, None, PAGE, HD), lambda h, b, live: (0, 0, 0, h)),
-            pl.BlockSpec((extra_n, None, PAGE, HD), lambda h, b, live: (0, 1, 0, h)),
-            pl.BlockSpec((rows, HD), lambda h, b, live: (0, h)),
-            pl.BlockSpec((rows, HD), lambda h, b, live: (0, h)),
+            pl.BlockSpec((1, main_n * PAGE), lambda h, live: (0, 0)),
+            pl.BlockSpec((1, extra_n * PAGE), lambda h, live: (0, 0)),
+            pl.BlockSpec((rows, HD), lambda h, live: (0, h)),
+            pl.BlockSpec((main_n, None, PAGE, HD), lambda h, live: (0, 0, 0, h)),
+            pl.BlockSpec((main_n, None, PAGE, HD), lambda h, live: (0, 1, 0, h)),
+            pl.BlockSpec((extra_n, None, PAGE, HD), lambda h, live: (0, 0, 0, h)),
+            pl.BlockSpec((extra_n, None, PAGE, HD), lambda h, live: (0, 1, 0, h)),
+            pl.BlockSpec((rows, HD), lambda h, live: (0, h)),
+            pl.BlockSpec((rows, HD), lambda h, live: (0, h)),
         ],
-        out_specs=pl.BlockSpec((BLOCK_Q, HD), lambda h, b, live: (b, h)),
-    )
-    keys_n = (main_n + extra_n) * PAGE + rows
+        out_specs=pl.BlockSpec((rows, HD), lambda h, live: (0, h)),
+    )
+    keys_n = (main_n + extra_n) * PAGE + rows // 2
     return pl.pallas_call(
         attend_kernel,
         grid_spec=grid_spec,
@@ -132,6 +139,103 @@
     )
 
 
+def grid_attend_kernel(
+    live_ref, kpm_ref, kpe_ref, q_ref, mk_ref, mv_ref, ek_ref, ev_ref, nk_ref, nv_ref, out_ref
+):
+    block = pl.program_id(1)
+    live = live_ref[0]
+    main_span = mk_ref.shape[0] * mk_ref.shape[1]
+    extra_span = ek_ref.shape[0] * ek_ref.shape[1]
+    query = q_ref[...]
+    contract = (((1,), (1,)), ((), ()))
+    scale = HD ** (-0.5)
+
+    def scores(keys):
+        return lax.dot_general(query, keys, contract, preferred_element_type=jnp.float32) * scale
+
+    main_scores = scores(mk_ref[...].reshape(main_span, HD))
+    extra_scores = scores(ek_ref[...].reshape(extra_span, HD))
+    new_scores = scores(nk_ref[...])
+    main_ok = kpm_ref[...] < live
+    extra_ok = kpe_ref[...] < live
+    query_pos = block * BLOCK_Q + lax.broadcasted_iota(jnp.int32, new_scores.shape, 0)
+    new_ok = lax.broadcasted_iota(jnp.int32, new_scores.shape, 1) <= query_pos
+    main_scores = jnp.where(main_ok, main_scores, -1e30)
+    extra_scores = jnp.where(extra_ok, extra_scores, -1e30)
+    new_scores = jnp.where(new_ok, new_scores, -1e30)
+    row_top = jnp.maximum(
+        jnp.maximum(
+            jnp.max(main_scores, axis=1, keepdims=True),
+            jnp.max(extra_scores, axis=1, keepdims=True),
+        ),
+        jnp.max(new_scores, axis=1, keepdims=True),
+    )
+    main_w = jnp.exp(main_scores - row_top)
+    extra_w = jnp.exp(extra_scores - row_top)
+    new_w = jnp.exp(new_scores - row_top)
+    row_total = (
+        jnp.sum(main_w, axis=1, keepdims=True)
+        + jnp.sum(extra_w, axis=1, keepdims=True)
+        + jnp.sum(new_w, axis=1, keepdims=True)
+    )
+
+    def weighted(weights, values):
+        return jnp.dot(weights.astype(jnp.bfloat16), values, preferred_element_type=jnp.float32)
+
+    summed = (
+        weighted(main_w, mv_ref[...].reshape(main_span, HD))
+        + weighted(extra_w, ev_ref[...].reshape(extra_span, HD))
+        + weighted(new_w, nv_ref[...])
+    )
+    out_ref[...] = (summed / row_total).astype(out_ref.dtype)
+
+
+def grid_attend(live, query, main_pages, main_pos, extra_pages, extra_pos, new_key, new_value):
+    rows, width = query.shape
+    heads = width // HD
+    main_n = main_pages.shape[0]
+    extra_n = extra_pages.shape[0]
+    grid_spec = pltpu.PrefetchScalarGridSpec(
+        num_scalar_prefetch=1,
+        grid=(heads, rows // BLOCK_Q),
+        in_specs=[
+            pl.BlockSpec((1, main_n * PAGE), lambda h, b, live: (0, 0)),
+            pl.BlockSpec((1, extra_n * PAGE), lambda h, b, live: (0, 0)),
+            pl.BlockSpec((BLOCK_Q, HD), lambda h, b, live: (b, h)),
+            pl.BlockSpec((main_n, None, PAGE, HD), lambda h, b, live: (0, 0, 0, h)),
+            pl.BlockSpec((main_n, None, PAGE, HD), lambda h, b, live: (0, 1, 0, h)),
+            pl.BlockSpec((extra_n, None, PAGE, HD), lambda h, b, live: (0, 0, 0, h)),
+            pl.BlockSpec((extra_n, None, PAGE, HD), lambda h, b, live: (0, 1, 0, h)),
+            pl.BlockSpec((rows, HD), lambda h, b, live: (0, h)),
+            pl.BlockSpec((rows, HD), lambda h, b, live: (0, h)),
+        ],
+        out_specs=pl.BlockSpec((BLOCK_Q, HD), lambda h, b, live: (b, h)),
+    )
+    keys_n = (main_n + extra_n) * PAGE + rows
+    return pl.pallas_call(
+        grid_attend_kernel,
+        grid_spec=grid_spec,
+        out_shape=jax.ShapeDtypeStruct((rows, width), jnp.bfloat16),
+        compiler_params=pltpu.CompilerParams(vmem_limit_bytes=56 * 1024 * 1024),
+        cost_estimate=pl.CostEstimate(
+            flops=4 * rows * keys_n * width,
+            transcendentals=rows * keys_n * heads,
+            bytes_accessed=2 * (2 * keys_n * width + 2 * rows * width),
+        ),
+    )(
+        live,
+        main_pos.reshape(1, -1),
+        extra_pos.reshape(1, -1),
+        query,
+        main_pages,
+        main_pages,
+        extra_pages,
+        extra_pages,
+        new_key,
+        new_value,
+    )
+
+
 def swap_kernel(send_ref, recv_ref, send_sems, recv_sems):
     count = send_ref.shape[0]
     me = lax.axis_index("req")
@@ -329,7 +433,7 @@
     def redo(ops):
         _, query, key, value, pool, slots, holders, ranks, live = ops
         pages, pos, extra, extra_at = exchange_wide(pool, slots, holders, ranks, req_index, req_count)
-        return attend(live, query, pages, pos, extra, extra_at, key, value)
+        return grid_attend(live, query, pages, pos, extra, extra_at, key, value)
 
     attended = lax.cond(
         relay_fits,

time: 262 us -> 259 us (0.989)
  Pallas kernels: 37 us -> 33.9 us
    pallas_call x1, Pallas kernels: 24.6 us -> 21.6 us  [attend(): pl.pallas_call(attend_kernel, grid_spec=grid_spec, out_shape=jax.ShapeDty...]
where the time goes in v11:
time: 259 us; the launch traced here: 258 us
  waiting for transfers between devices  122 us (47%)
  local copies, waits for them, and re-layouts  36.4 us (14%)
  Pallas kernels  33.9 us (13%)
  other arithmetic  28 us (11%)
  between operations  17.5 us (7%)
  starting transfers between devices  11.8 us (5%)
  matrix products  8.76 us (3%)
    all_to_all x1, waiting for transfers between devices, exchange_relay(): lax.all_to_all(outgoing, 'req', split_axis=0, concat_axis=0, tiled=True)  82.5 us
    reduce_scatter x1, waiting for transfers between devices, body(): lax.psum_scatter(head_term.astype(jnp.bfloat16), 'tp', scatter_dimension=...  39.4 us
    pallas_call x1, Pallas kernels, attend(): pl.pallas_call(attend_kernel, grid_spec=grid_spec, out_shape=jax.ShapeDty...  21.6 us
    pallas_call x1, Pallas kernels, swap_pieces(): pl.pallas_call(swap_kernel, out_shape=jax.ShapeDtypeStruct(pieces.shape,...  12.4 us
    all_to_all x1, starting transfers between devices, exchange_relay(): lax.all_to_all(outgoing, 'req', split_axis=0, concat_axis=0, tiled=True)  11.8 us
    unnamed x25, local copies, waits for them, and re-layouts  8.44 us
    scatter x1, other arithmetic, exchange_relay(): outgoing = padded[send_slots].at[:, :, PAGE:, :].set(pieces)  5.38 us
  transfers between devices with their start and end apart: 2, of which 2 were waited for; matrix products, arithmetic and copies ran while one was open for 13% of the time, Pallas kernels for 0%

profile of v11, /device:TPU:2, one launch (start us, length us, event | category | flops | bytes accessed | tf_op | source)
XLA Modules:
  0.0 258.4 jit_solution(9667247530033533131)
XLA Ops:
  6.5 1.7 convert_reduce_fusion.1
  10.6 1.1 select_reduce_fusion.2
  11.8 1.5 select_reduce_fusion.4
  13.7 3.2 %gather_fusion.2 = bf16[8,2,128,256]{3,2,1,0:T(8,128)(2,1)} fusion(bf16[16,2,128,256]{3,2,1,0:T(8,128)(2,1)} %param.15, s32[1024]{0:T(1024)S(1)} %pad_clamp_fusion.2), kind=kCustom, calls=%fused_computation.2 | custom fusion | bytes 2097184 | tf_op jit(solution)/shard_map/gather | solution.py:365
  16.9 2.2 reshape.458
  19.1 2.8 %copy.63 = bf16[8,2,32,4,256]{4,3,0,1,2:T(4,128)(2,1)} copy(bf16[8,2,32,4,256]{4,3,2,1,0:T(4,128)(2,1)} %reshape.458) | data formatting | bytes 2097152 | tf_op jit(solution)/shard_map/reshape | solution.py:366
  21.9 2.1 reshape.459
  24.1 4.3 %gather_fusion.1 = bf16[32,2,128,256]{3,2,1,0:T(8,128)(2,1)} fusion(bf16[16,2,128,256]{3,2,1,0:T(8,128)(2,1)} %param.15, s32[1024]{0:T(1024)S(1)} %pad_clamp_fusion.3), kind=kCustom, calls=%fused_computation.1 | custom fusion | bytes 8388736 | tf_op jit(solution)/shard_map/gather | solution.py:371
  28.4 5.4 %pad_maximum_fusion = bf16[32,2,160,256]{3,2,1,0:T(8,128)(2,1)} fusion(bf16[32,2,32,256]{3,2,1,0:T(8,128)(2,1)} %reshape.459, bf16[32,2,128,256]{3,2,1,0:T(8,128)(2,1)} %gather_fusion.1), kind=kLoop, calls=%fused_computation.23 | loop fusion | flops 10485760 | bytes 10485760 | tf_op jit(solution)/shard_map/scatter | solution.py:371
  33.8 11.8 %all-to-all-start.1 = ((bf16[32,2,160,256]{3,2,1,0:T(8,128)(2,1)}), bf16[32,2,160,256]{3,2,1,0:T(8,128)(2,1)}, u32[]{:S(2)}, u32[]{:S(2)}) async-start(bf16[32,2,160,256]{3,2,1,0:T(8,128)(2,1)} %pad_maximum_fusion), calls=%async_computation.1 | async-start | bytes 10485760 | tf_op jit(solution)/shard_map/all_to_all | solution.py:372
  47.2 2.8 %convert_reduce_fusion = f32[1024]{0:T(1024)S(1)} fusion(bf16[1024,2048]{1,0:T(8,128)(2,1)} %param.12), kind=kLoop, calls=%fused_computation.18 | loop fusion | flops 4193280 | bytes 4198400 | tf_op jit(solution)/shard_map/reduce_sum | solution.py:306
  50.0 1.2 fusion.3
  51.2 4.0 %fusion.6 = f32[1024,3,256]{0,2,1:T(8,128)S(1)} fusion(bf16[2048,3,256]{2,0,1:T(8,128)(2,1)S(1)} %copy-done, bf16[1024,2048]{1,0:T(8,128)(2,1)S(1)} %copy-done.3, f32[1024]{0:T(1024)S(1)} %add_rsqrt_fusion, f32[1024]{0:T(1024)S(1)} %broadcast_multiply_fusion.1), kind=kOutput, calls=%fused_computation.25 | convolution fusion | flops 3229614080 | bytes 10493952 | tf_op jit(solution)/shard_map/td,dcf->tcf/dot_general | solution.py:310
  56.4 0.9 fusion.23
  57.9 1.5 copy.52
  59.3 1.1 fusion.22
  60.4 1.4 copy.53
  61.9 2.2 copy.54
  65.5 1.9 multiply_cosine_fusion
  67.4 3.9 %subtract_convert_fusion = (bf16[1024,2,64]{2,1,0:T(2,128)(2,1)S(1)}, bf16[1024,2,64]{2,1,0:T(2,128)(2,1)S(1)}, bf16[1024,2,64]{2,1,0:T(2,128)(2,1)S(1)}, bf16[1024,2,64]{2,1,0:T(2,128)(2,1)S(1)}) fusion(f32[1024,2,64]{2,1,0:T(2,128)} %copy.54, f32[1024,2,64]{2,1,0:T(2,128)S(1)} %copy.53, f32[1024,64]{1,0:T(8,128)S(1)} %get-tuple-element.70, ...), kind=kLoop, calls=%fused_computation.32 | loop fusion | flops 2097152 | bytes 3670016 | tf_op jit(solution)/shard_map/convert.1
  71.3 2.9 %pad_maximum_fusion.1 = (bf16[1024,2,128]{2,1,0:T(2,128)(2,1)S(1)}, bf16[1024,2,128]{2,1,0:T(2,128)(2,1)S(1)}) fusion(bf16[1024,2,64]{2,1,0:T(2,128)(2,1)S(1)} %get-tuple-element.62, bf16[1024,2,64]{2,1,0:T(2,128)(2,1)S(1)} %get-tuple-element.63, bf16[1024,2,64]{2,1,0:T(2,128)(2,1)S(1)} %get-tuple-element.57, bf16[1024,2,64]{2,1,0:T(2,128)(2,1)S(1)} %get-tuple-element.56), kind=kLoop, calls=%fused_computation.41 | loop fusion | flops 2097152 | bytes 2097152 | tf_op jit(solution)/shard_map/concatenate | solution.py:29
  75.1 0.9 copy.65
  78.1 1.0 copy.55
  83.2 82.5 %all-to-all-done.1.mk_ref.mv_ref = bf16[32,2,160,256]{3,2,1,0:T(8,128)(2,1)} async-done(((bf16[32,2,160,256]{3,2,1,0:T(8,128)(2,1)}), bf16[32,2,160,256]{3,2,1,0:T(8,128)(2,1)}, u32[]{:S(2)}, u32[]{:S(2)}) %all-to-all-start.1) | async-done | bytes 5242912 | tf_op jit(solution)/shard_map/all_to_all | solution.py:372
  165.7 2.4 slice.79
  168.0 1.5 reshape.460
  170.5 1.3 gather_fusion.3
  171.8 12.4 %shard_map.82 = bf16[32,2,4,256]{3,2,1,0:T(4,128)(2,1)} custom-call(bf16[32,2,4,256]{3,2,1,0:T(4,128)(2,1)} %gather_fusion.3), custom_call_target="tpu_custom_call" | custom-call | tf_op jit(solution)/shard_map/pallas_call | solution.py:289
  184.2 1.0 copy.49
  185.8 21.6 %shard_map.83 = bf16[1024,256]{1,0:T(8,128)(2,1)} custom-call(s32[1]{0:T(128)} %mul.171.live_ref, s32[1,4096]{1,0:T(1,128)} %bitcast.94, s32[1,128]{1,0:T(1,128)} %broadcast_select_fusion.kpe_ref, bf16[1024,256]{1,0:T(8,128)(2,1)} %bitcast.88, bf16[32,2,160,256]{3,2,1,0:T(8,128)(2,1)} %all-to-all-done.1.mk_ref.mv_ref, ...), custom_call_target="tpu_custom_call" | custom-call | flops 4966055936 | bytes 5898240 | tf_op jit(solution)/shard_map/pallas_call | solution.py:118
  207.4 4.7 %convolution_convert_fusion = bf16[1024,2048]{1,0:T(8,128)(2,1)} fusion(bf16[1024,256]{1,0:T(8,128)(2,1)} %get-tuple-element.73, bf16[256,2048]{1,0:T(8,128)(2,1)} %param.14), kind=kOutput, calls=%fused_computation.28 | convolution fusion | flops 1075838976 | bytes 5767168 | tf_op jit(solution)/shard_map/dot_general | solution.py:444
  212.1 39.4 %reduce-scatter.2.cloned.1.call-done = bf16[128,2048]{1,0:T(8,128)(2,1)} async-done(((bf16[1024,2048]{1,0:T(8,128)(2,1)}), bf16[128,2048]{1,0:T(8,128)(2,1)}) %reduce-scatter.2.cloned.1.call-update) | async-done | bytes 524304 | tf_op jit(solution)/shard_map/reduce_scatter | solution.py:445
  (65 shorter events, 12.3 us)
Async XLA Ops:
  6.5 44.7 %copy-start = (bf16[2048,3,256]{2,0,1:T(8,128)(2,1)S(1)}, bf16[2048,3,256]{2,0,1:T(8,128)(2,1)}, u32[]{:S(2)}) copy-start(bf16[2048,3,256]{2,0,1:T(8,128)(2,1)} %param.13) | copy-start | bytes 9437188
  33.8 12.0 %copy-start.10 = (s32[32]{0:T(128)S(1)}, s32[32]{0:T(128)}, u32[]{:S(2)}) copy-start(s32[32]{0:T(128)} %param.16) | copy-start | bytes 388
  33.8 12.7 %copy-start.11 = (s32[32]{0:T(128)S(1)}, s32[32]{0:T(128)}, u32[]{:S(2)}) copy-start(s32[32]{0:T(128)} %param.19) | copy-start | bytes 388
  33.8 131.9 %all-to-all-start.1 = ((bf16[32,2,160,256]{3,2,1,0:T(8,128)(2,1)}), bf16[32,2,160,256]{3,2,1,0:T(8,128)(2,1)}, u32[]{:S(2)}, u32[]{:S(2)}) async-start(bf16[32,2,160,256]{3,2,1,0:T(8,128)(2,1)} %pad_maximum_fusion), calls=%async_computation.1 | async-start | bytes 10485760 | tf_op jit(solution)/shard_map/all_to_all | solution.py:372
  45.6 206.0 %reduce-scatter.2.cloned.1.call-start = ((), (), s32[]{:S(2)}) async-start(), calls=%async_computation.3 | async-start | bytes 4718592 | tf_op jit(solution)/shard_map/reduce_scatter | solution.py:445
  45.8 4.1 %copy-start.3 = (bf16[1024,2048]{1,0:T(8,128)(2,1)S(1)}, bf16[1024,2048]{1,0:T(8,128)(2,1)}, u32[]{:S(2)}) copy-start(bf16[1024,2048]{1,0:T(8,128)(2,1)} %param.12) | copy-start | bytes 12582916
  71.3 6.7 %copy-start.4 = (bf16[1024,1,256]{0,2,1:T(8,128)(2,1)S(1)}, bf16[1024,1,256]{0,2,1:T(8,128)(2,1)}, u32[]{:S(2)}) copy-start(bf16[1024,1,256]{0,2,1:T(8,128)(2,1)} %slice.78) | copy-start | bytes 1572868
  71.3 10.3 %copy-start.5 = (s32[32,32,1]{1,2,0:T(1,128)S(1)}, s32[32,32,1]{1,2,0:T(1,128)}, u32[]{:S(2)}) copy-start(s32[32,32,1]{1,2,0:T(1,128)} %param.18) | copy-start | bytes 12292
  168.0 17.8 %copy-start.2 = (bf16[16,2,128,256]{3,2,1,0:T(8,128)(2,1)S(1)}, bf16[16,2,128,256]{3,2,1,0:T(8,128)(2,1)}, u32[]{:S(2)}) copy-start(bf16[16,2,128,256]{3,2,1,0:T(8,128)(2,1)} %param.15) | copy-start | bytes 6291460
  168.0 17.8 %copy-start.9 = (s32[32,32]{1,0:T(8,128)S(1)}, s32[32,32]{1,0:T(8,128)}, u32[]{:S(2)}) copy-start(s32[32,32]{1,0:T(8,128)} %param.17) | copy-start | bytes 12292
  207.4 44.2 %copy-start.1 = (bf16[2048,3,256]{2,0,1:T(8,128)(2,1)S(1)}, bf16[2048,3,256]{2,0,1:T(8,128)(2,1)}, u32[]{:S(2)}) copy-start(bf16[2048,3,256]{2,0,1:T(8,128)(2,1)} %param.13) | copy-start | bytes 9437188
Sparse Core Ops, SparseCore 0:
  212.3 39.2 reduce-scatter.1

commit v12 on v11

--- a/solution.py
+++ b/solution.py
@@ -45,52 +45,69 @@
     scale = HD ** (-0.5)
     main_ok = kpm_ref[...] < live
     extra_ok = kpe_ref[...] < live
-
-    for block in range(q_ref.shape[0] // BLOCK_Q):
-        rows = pl.ds(block * BLOCK_Q, BLOCK_Q)
-        seen = pl.ds(0, (block + 1) * BLOCK_Q)
-        query = q_ref[rows, :]
+    diag_ok = lax.broadcasted_iota(jnp.int32, (BLOCK_Q, BLOCK_Q), 1) <= lax.broadcasted_iota(
+        jnp.int32, (BLOCK_Q, BLOCK_Q), 0
+    )
+
+    def weighted(weights, values):
+        return jnp.dot(weights.astype(jnp.bfloat16), values, preferred_element_type=jnp.float32)
+
+    def block_body(block, carry):
+        start = pl.multiple_of(block * BLOCK_Q, BLOCK_Q)
+        query = q_ref[pl.ds(start, BLOCK_Q), :]
 
         def scores(keys):
             return (
                 lax.dot_general(query, keys, contract, preferred_element_type=jnp.float32) * scale
             )
 
-        main_scores = scores(mk_ref[...].reshape(main_span, HD))
-        extra_scores = scores(ek_ref[...].reshape(extra_span, HD))
-        new_scores = scores(nk_ref[seen, :])
-        query_pos = block * BLOCK_Q + lax.broadcasted_iota(jnp.int32, new_scores.shape, 0)
-        new_ok = lax.broadcasted_iota(jnp.int32, new_scores.shape, 1) <= query_pos
-        main_scores = jnp.where(main_ok, main_scores, -1e30)
-        extra_scores = jnp.where(extra_ok, extra_scores, -1e30)
-        new_scores = jnp.where(new_ok, new_scores, -1e30)
+        def chunk(index):
+            return pl.ds(pl.multiple_of(index * BLOCK_Q, BLOCK_Q), BLOCK_Q)
+
+        main_scores = jnp.where(main_ok, scores(mk_ref[...].reshape(main_span, HD)), -1e30)
+        extra_scores = jnp.where(extra_ok, scores(ek_ref[...].reshape(extra_span, HD)), -1e30)
+        diag_scores = jnp.where(diag_ok, scores(nk_ref[chunk(block), :]), -1e30)
         row_top = jnp.maximum(
             jnp.maximum(
                 jnp.max(main_scores, axis=1, keepdims=True),
                 jnp.max(extra_scores, axis=1, keepdims=True),
             ),
-            jnp.max(new_scores, axis=1, keepdims=True),
+            jnp.max(diag_scores, axis=1, keepdims=True),
         )
+
+        def past_top(index, top):
+            return jnp.maximum(
+                top, jnp.max(scores(nk_ref[chunk(index), :]), axis=1, keepdims=True)
+            )
+
+        row_top = lax.fori_loop(0, block, past_top, row_top)
         main_w = jnp.exp(main_scores - row_top)
         extra_w = jnp.exp(extra_scores - row_top)
-        new_w = jnp.exp(new_scores - row_top)
+        diag_w = jnp.exp(diag_scores - row_top)
         row_total = (
             jnp.sum(main_w, axis=1, keepdims=True)
             + jnp.sum(extra_w, axis=1, keepdims=True)
-            + jnp.sum(new_w, axis=1, keepdims=True)
+            + jnp.sum(diag_w, axis=1, keepdims=True)
         )
-
-        def weighted(weights, values):
-            return jnp.dot(
-                weights.astype(jnp.bfloat16), values, preferred_element_type=jnp.float32
-            )
-
         summed = (
             weighted(main_w, mv_ref[...].reshape(main_span, HD))
             + weighted(extra_w, ev_ref[...].reshape(extra_span, HD))
-            + weighted(new_w, nv_ref[seen, :])
+            + weighted(diag_w, nv_ref[chunk(block), :])
         )
-        out_ref[rows, :] = (summed / row_total).astype(out_ref.dtype)
+
+        def past_sum(index, sums):
+            total, acc = sums
+            past_w = jnp.exp(scores(nk_ref[chunk(index), :]) - row_top)
+            return (
+                total + jnp.sum(past_w, axis=1, keepdims=True),
+                acc + weighted(past_w, nv_ref[chunk(index), :]),
+            )
+
+        row_total, summed = lax.fori_loop(0, block, past_sum, (row_total, summed))
+        out_ref[pl.ds(start, BLOCK_Q), :] = (summed / row_total).astype(out_ref.dtype)
+        return carry
+
+    lax.fori_loop(0, q_ref.shape[0] // BLOCK_Q, block_body, 0)
 
 
 def attend(live, query, main_pages, main_pos, extra_pages, extra_pos, new_key, new_value):

time: 259 us -> 263 us (1.015)
  Pallas kernels: 33.9 us -> 37.9 us
    pallas_call x1, Pallas kernels: 21.6 us -> 25.5 us  [attend(): pl.pallas_call(attend_kernel, grid_spec=grid_spec, out_shape=jax.ShapeDty...]
where the time goes in v12:
time: 263 us; the launch traced here: 262 us
  waiting for transfers between devices  122 us (46%)
  Pallas kernels  37.9 us (14%)
  local copies, waits for them, and re-layouts  36.4 us (14%)
  other arithmetic  28 us (11%)
  between operations  17.5 us (7%)
  starting transfers between devices  11.8 us (4%)
  matrix products  8.76 us (3%)
    all_to_all x1, waiting for transfers between devices, exchange_relay(): lax.all_to_all(outgoing, 'req', split_axis=0, concat_axis=0, tiled=True)  82.5 us
    reduce_scatter x1, waiting for transfers between devices, body(): lax.psum_scatter(head_term.astype(jnp.bfloat16), 'tp', scatter_dimension=...  39.4 us
    pallas_call x1, Pallas kernels, attend(): pl.pallas_call(attend_kernel, grid_spec=grid_spec, out_shape=jax.ShapeDty...  25.5 us
    pallas_call x1, Pallas kernels, swap_pieces(): pl.pallas_call(swap_kernel, out_shape=jax.ShapeDtypeStruct(pieces.shape,...  12.4 us
    all_to_all x1, starting transfers between devices, exchange_relay(): lax.all_to_all(outgoing, 'req', split_axis=0, concat_axis=0, tiled=True)  11.8 us
    unnamed x25, local copies, waits for them, and re-layouts  8.44 us
    scatter x1, other arithmetic, exchange_relay(): outgoing = padded[send_slots].at[:, :, PAGE:, :].set(pieces)  5.38 us
  transfers between devices with their start and end apart: 2, of which 2 were waited for; matrix products, arithmetic and copies ran while one was open for 13% of the time, Pallas kernels for 0%

profile of v12, /device:TPU:2, one launch (start us, length us, event | category | flops | bytes accessed | tf_op | source)
XLA Modules:
  0.0 262.4 jit_solution(8686829960606319111)
XLA Ops:
  6.5 1.7 convert_reduce_fusion.1
  10.6 1.1 select_reduce_fusion.2
  11.8 1.5 select_reduce_fusion.4
  13.7 3.2 %gather_fusion.2 = bf16[8,2,128,256]{3,2,1,0:T(8,128)(2,1)} fusion(bf16[16,2,128,256]{3,2,1,0:T(8,128)(2,1)} %param.15, s32[1024]{0:T(1024)S(1)} %pad_clamp_fusion.2), kind=kCustom, calls=%fused_computation.2 | custom fusion | bytes 2097184 | tf_op jit(solution)/shard_map/gather | solution.py:382
  16.9 2.2 reshape.458
  19.1 2.8 %copy.63 = bf16[8,2,32,4,256]{4,3,0,1,2:T(4,128)(2,1)} copy(bf16[8,2,32,4,256]{4,3,2,1,0:T(4,128)(2,1)} %reshape.458) | data formatting | bytes 2097152 | tf_op jit(solution)/shard_map/reshape | solution.py:383
  21.9 2.1 reshape.459
  24.1 4.3 %gather_fusion.1 = bf16[32,2,128,256]{3,2,1,0:T(8,128)(2,1)} fusion(bf16[16,2,128,256]{3,2,1,0:T(8,128)(2,1)} %param.15, s32[1024]{0:T(1024)S(1)} %pad_clamp_fusion.3), kind=kCustom, calls=%fused_computation.1 | custom fusion | bytes 8388736 | tf_op jit(solution)/shard_map/gather | solution.py:388
  28.4 5.4 %pad_maximum_fusion = bf16[32,2,160,256]{3,2,1,0:T(8,128)(2,1)} fusion(bf16[32,2,32,256]{3,2,1,0:T(8,128)(2,1)} %reshape.459, bf16[32,2,128,256]{3,2,1,0:T(8,128)(2,1)} %gather_fusion.1), kind=kLoop, calls=%fused_computation.23 | loop fusion | flops 10485760 | bytes 10485760 | tf_op jit(solution)/shard_map/scatter | solution.py:388
  33.8 11.8 %all-to-all-start.1 = ((bf16[32,2,160,256]{3,2,1,0:T(8,128)(2,1)}), bf16[32,2,160,256]{3,2,1,0:T(8,128)(2,1)}, u32[]{:S(2)}, u32[]{:S(2)}) async-start(bf16[32,2,160,256]{3,2,1,0:T(8,128)(2,1)} %pad_maximum_fusion), calls=%async_computation.1 | async-start | bytes 10485760 | tf_op jit(solution)/shard_map/all_to_all | solution.py:389
  47.2 2.8 %convert_reduce_fusion = f32[1024]{0:T(1024)S(1)} fusion(bf16[1024,2048]{1,0:T(8,128)(2,1)} %param.12), kind=kLoop, calls=%fused_computation.18 | loop fusion | flops 4193280 | bytes 4198400 | tf_op jit(solution)/shard_map/reduce_sum | solution.py:323
  50.0 1.2 fusion.3
  51.2 4.0 %fusion.6 = f32[1024,3,256]{0,2,1:T(8,128)S(1)} fusion(bf16[2048,3,256]{2,0,1:T(8,128)(2,1)S(1)} %copy-done, bf16[1024,2048]{1,0:T(8,128)(2,1)S(1)} %copy-done.3, f32[1024]{0:T(1024)S(1)} %add_rsqrt_fusion, f32[1024]{0:T(1024)S(1)} %broadcast_multiply_fusion.1), kind=kOutput, calls=%fused_computation.25 | convolution fusion | flops 3229614080 | bytes 10493952 | tf_op jit(solution)/shard_map/td,dcf->tcf/dot_general | solution.py:327
  56.4 0.9 fusion.23
  57.9 1.5 copy.52
  59.3 1.1 fusion.22
  60.4 1.4 copy.53
  61.9 2.2 copy.54
  65.5 1.9 multiply_cosine_fusion
  67.4 3.9 %subtract_convert_fusion = (bf16[1024,2,64]{2,1,0:T(2,128)(2,1)S(1)}, bf16[1024,2,64]{2,1,0:T(2,128)(2,1)S(1)}, bf16[1024,2,64]{2,1,0:T(2,128)(2,1)S(1)}, bf16[1024,2,64]{2,1,0:T(2,128)(2,1)S(1)}) fusion(f32[1024,2,64]{2,1,0:T(2,128)} %copy.54, f32[1024,2,64]{2,1,0:T(2,128)S(1)} %copy.53, f32[1024,64]{1,0:T(8,128)S(1)} %get-tuple-element.70, ...), kind=kLoop, calls=%fused_computation.32 | loop fusion | flops 2097152 | bytes 3670016 | tf_op jit(solution)/shard_map/convert.1
  71.3 2.9 %pad_maximum_fusion.1 = (bf16[1024,2,128]{2,1,0:T(2,128)(2,1)S(1)}, bf16[1024,2,128]{2,1,0:T(2,128)(2,1)S(1)}) fusion(bf16[1024,2,64]{2,1,0:T(2,128)(2,1)S(1)} %get-tuple-element.62, bf16[1024,2,64]{2,1,0:T(2,128)(2,1)S(1)} %get-tuple-element.63, bf16[1024,2,64]{2,1,0:T(2,128)(2,1)S(1)} %get-tuple-element.57, bf16[1024,2,64]{2,1,0:T(2,128)(2,1)S(1)} %get-tuple-element.56), kind=kLoop, calls=%fused_computation.41 | loop fusion | flops 2097152 | bytes 2097152 | tf_op jit(solution)/shard_map/concatenate | solution.py:29
  75.1 0.9 copy.65
  78.1 1.0 copy.55
  83.2 82.5 %all-to-all-done.1.mk_ref.mv_ref = bf16[32,2,160,256]{3,2,1,0:T(8,128)(2,1)} async-done(((bf16[32,2,160,256]{3,2,1,0:T(8,128)(2,1)}), bf16[32,2,160,256]{3,2,1,0:T(8,128)(2,1)}, u32[]{:S(2)}, u32[]{:S(2)}) %all-to-all-start.1) | async-done | bytes 5242912 | tf_op jit(solution)/shard_map/all_to_all | solution.py:389
  165.7 2.4 slice.79
  168.0 1.5 reshape.460
  170.5 1.3 gather_fusion.3
  171.8 12.4 %shard_map.82 = bf16[32,2,4,256]{3,2,1,0:T(4,128)(2,1)} custom-call(bf16[32,2,4,256]{3,2,1,0:T(4,128)(2,1)} %gather_fusion.3), custom_call_target="tpu_custom_call" | custom-call | tf_op jit(solution)/shard_map/pallas_call | solution.py:306
  184.2 1.0 copy.49
  185.8 25.5 %shard_map.83 = bf16[1024,256]{1,0:T(8,128)(2,1)} custom-call(s32[1]{0:T(128)} %mul.171.live_ref, s32[1,4096]{1,0:T(1,128)} %bitcast.94, s32[1,128]{1,0:T(1,128)} %broadcast_select_fusion.kpe_ref, bf16[1024,256]{1,0:T(8,128)(2,1)} %bitcast.88, bf16[32,2,160,256]{3,2,1,0:T(8,128)(2,1)} %all-to-all-done.1.mk_ref.mv_ref, ...), custom_call_target="tpu_custom_call" | custom-call | flops 4966055936 | bytes 5898240 | tf_op jit(solution)/shard_map/pallas_call | solution.py:135
  211.4 4.7 %convolution_convert_fusion = bf16[1024,2048]{1,0:T(8,128)(2,1)} fusion(bf16[1024,256]{1,0:T(8,128)(2,1)} %get-tuple-element.73, bf16[256,2048]{1,0:T(8,128)(2,1)} %param.14), kind=kOutput, calls=%fused_computation.28 | convolution fusion | flops 1075838976 | bytes 5767168 | tf_op jit(solution)/shard_map/dot_general | solution.py:461
  216.1 39.4 %reduce-scatter.2.cloned.1.call-done = bf16[128,2048]{1,0:T(8,128)(2,1)} async-done(((bf16[1024,2048]{1,0:T(8,128)(2,1)}), bf16[128,2048]{1,0:T(8,128)(2,1)}) %reduce-scatter.2.cloned.1.call-update) | async-done | bytes 524304 | tf_op jit(solution)/shard_map/reduce_scatter | solution.py:462
  (65 shorter events, 12.3 us)
Async XLA Ops:
  6.5 44.7 %copy-start = (bf16[2048,3,256]{2,0,1:T(8,128)(2,1)S(1)}, bf16[2048,3,256]{2,0,1:T(8,128)(2,1)}, u32[]{:S(2)}) copy-start(bf16[2048,3,256]{2,0,1:T(8,128)(2,1)} %param.13) | copy-start | bytes 9437188
  33.8 12.0 %copy-start.10 = (s32[32]{0:T(128)S(1)}, s32[32]{0:T(128)}, u32[]{:S(2)}) copy-start(s32[32]{0:T(128)} %param.16) | copy-start | bytes 388
  33.8 12.7 %copy-start.11 = (s32[32]{0:T(128)S(1)}, s32[32]{0:T(128)}, u32[]{:S(2)}) copy-start(s32[32]{0:T(128)} %param.19) | copy-start | bytes 388
  33.8 131.9 %all-to-all-start.1 = ((bf16[32,2,160,256]{3,2,1,0:T(8,128)(2,1)}), bf16[32,2,160,256]{3,2,1,0:T(8,128)(2,1)}, u32[]{:S(2)}, u32[]{:S(2)}) async-start(bf16[32,2,160,256]{3,2,1,0:T(8,128)(2,1)} %pad_maximum_fusion), calls=%async_computation.1 | async-start | bytes 10485760 | tf_op jit(solution)/shard_map/all_to_all | solution.py:389
  45.6 210.0 %reduce-scatter.2.cloned.1.call-start = ((), (), s32[]{:S(2)}) async-start(), calls=%async_computation.3 | async-start | bytes 4718592 | tf_op jit(solution)/shard_map/reduce_scatter | solution.py:462
  45.8 4.1 %copy-start.3 = (bf16[1024,2048]{1,0:T(8,128)(2,1)S(1)}, bf16[1024,2048]{1,0:T(8,128)(2,1)}, u32[]{:S(2)}) copy-start(bf16[1024,2048]{1,0:T(8,128)(2,1)} %param.12) | copy-start | bytes 12582916
  71.3 6.7 %copy-start.4 = (bf16[1024,1,256]{0,2,1:T(8,128)(2,1)S(1)}, bf16[1024,1,256]{0,2,1:T(8,128)(2,1)}, u32[]{:S(2)}) copy-start(bf16[1024,1,256]{0,2,1:T(8,128)(2,1)} %slice.78) | copy-start | bytes 1572868
  71.3 10.3 %copy-start.5 = (s32[32,32,1]{1,2,0:T(1,128)S(1)}, s32[32,32,1]{1,2,0:T(1,128)}, u32[]{:S(2)}) copy-start(s32[32,32,1]{1,2,0:T(1,128)} %param.18) | copy-start | bytes 12292
  168.0 17.8 %copy-start.2 = (bf16[16,2,128,256]{3,2,1,0:T(8,128)(2,1)S(1)}, bf16[16,2,128,256]{3,2,1,0:T(8,128)(2,1)}, u32[]{:S(2)}) copy-start(bf16[16,2,128,256]{3,2,1,0:T(8,128)(2,1)} %param.15) | copy-start | bytes 6291460
  168.0 17.8 %copy-start.9 = (s32[32,32]{1,0:T(8,128)S(1)}, s32[32,32]{1,0:T(8,128)}, u32[]{:S(2)}) copy-start(s32[32,32]{1,0:T(8,128)} %param.17) | copy-start | bytes 12292
  211.4 44.2 %copy-start.1 = (bf16[2048,3,256]{2,0,1:T(8,128)(2,1)S(1)}, bf16[2048,3,256]{2,0,1:T(8,128)(2,1)}, u32[]{:S(2)}) copy-start(bf16[2048,3,256]{2,0,1:T(8,128)(2,1)} %param.13) | copy-start | bytes 9437188
Sparse Core Ops, SparseCore 0:
  216.2 39.2 reduce-scatter.1

commit v13 on v11

--- a/solution.py
+++ b/solution.py
@@ -370,18 +370,20 @@
     padded = jnp.pad(kv_pool, ((0, 0), (0, 0), (0, RELAY_A * frag), (0, 0)))
     outgoing = padded[send_slots].at[:, :, PAGE:, :].set(pieces)
     incoming = lax.all_to_all(outgoing, "req", split_axis=0, concat_axis=0, tiled=True)
-    relayed = (
-        incoming[:, :, PAGE:]
-        .reshape(req_count, 2, RELAY_A, frag, width)
-        .transpose(0, 2, 1, 3, 4)
-        .reshape(req_count * RELAY_A, 2, frag, width)
-    )
     match_b = spill[:, None, :] & (req_order[:, None, :] == jnp.arange(RELAY_B)[None, :, None])
     src_holder = jnp.sum(jnp.where(match_b, holder_rows[:, None, :], 0), axis=2)
     src_index = jnp.sum(
         jnp.where(match_b, holder_order.reshape(rows, entries)[:, None, :], 0), axis=2
     )
-    extra = relayed[src_holder * RELAY_A + jnp.clip(src_index, 0, RELAY_A - 1)]
+    zero = jnp.zeros_like(src_holder)
+    starts = jnp.stack(
+        [src_holder, zero, PAGE + jnp.clip(src_index, 0, RELAY_A - 1) * frag, zero], axis=-1
+    )
+
+    def window(start):
+        return lax.dynamic_slice(incoming, tuple(start), (1, 2, frag, width))[0]
+
+    extra = jax.vmap(jax.vmap(window))(starts)
     extra = extra.transpose(0, 2, 1, 3, 4).reshape(rows, 2, RELAY_B * frag, width)
     returned = swap_pieces(extra)
     extra_pages = (

time: 259 us -> 271 us (1.046); the launches traced: 258 us -> 267 us
  local copies, waits for them, and re-layouts: 36.4 us -> 43.7 us
    all_to_all x0 -> x1, local copies, waits for them, and re-layouts: none -> 10.2 us  [exchange_relay(): lax.all_to_all(outgoing, 'req', split_axis=0, concat_axis=0, tiled=True)]
    gather x1 -> x2, local copies, waits for them, and re-layouts: 1.3 us -> 4.06 us  [window(): return lax.dynamic_slice(incoming, tuple(start), (1, 2, frag, width))[0]]
  transfers between devices with their start and end apart: 2 -> 2, of which waited for: 2 -> 2; matrix products, arithmetic and copies ran while one was open for 13% -> 12% of each run, Pallas kernels for 0% -> 0%
where the time goes in v13:
time: 271 us; the launch traced here: 267 us
  waiting for transfers between devices  122 us (45%)
  local copies, waits for them, and re-layouts  43.7 us (16%)
  Pallas kernels  33.8 us (12%)
  other arithmetic  28.1 us (10%)
  between operations  17.7 us (7%)
  starting transfers between devices  12.3 us (5%)
  matrix products  8.76 us (3%)
    all_to_all x1, waiting for transfers between devices, exchange_relay(): lax.all_to_all(outgoing, 'req', split_axis=0, concat_axis=0, tiled=True)  82.7 us
    reduce_scatter x1, waiting for transfers between devices, body(): lax.psum_scatter(head_term.astype(jnp.bfloat16), 'tp', scatter_dimension=...  39.4 us
    pallas_call x1, Pallas kernels, attend(): pl.pallas_call(attend_kernel, grid_spec=grid_spec, out_shape=jax.ShapeDty...  21.5 us
    pallas_call x1, Pallas kernels, swap_pieces(): pl.pallas_call(swap_kernel, out_shape=jax.ShapeDtypeStruct(pieces.shape,...  12.4 us
    all_to_all x1, starting transfers between devices, exchange_relay(): lax.all_to_all(outgoing, 'req', split_axis=0, concat_axis=0, tiled=True)  11.8 us
    all_to_all x1, local copies, waits for them, and re-layouts, exchange_relay(): lax.all_to_all(outgoing, 'req', split_axis=0, concat_axis=0, tiled=True)  10.2 us
    unnamed x25, local copies, waits for them, and re-layouts  7.63 us
  transfers between devices with their start and end apart: 2, of which 2 were waited for; matrix products, arithmetic and copies ran while one was open for 12% of the time, Pallas kernels for 0%

profile of v13, /device:TPU:2, one launch (start us, length us, event | category | flops | bytes accessed | tf_op | source)
XLA Modules:
  0.0 266.7 jit_solution(16414076801563985927)
XLA Ops:
  6.5 1.7 convert_reduce_fusion.1
  10.6 1.1 select_reduce_fusion.2
  11.8 1.5 select_reduce_fusion.4
  13.7 3.2 %gather_fusion.2 = bf16[8,2,128,256]{3,2,1,0:T(8,128)(2,1)} fusion(bf16[16,2,128,256]{3,2,1,0:T(8,128)(2,1)} %param.15, s32[1024]{0:T(1024)S(1)} %pad_clamp_fusion.1), kind=kCustom, calls=%fused_computation.2 | custom fusion | bytes 2097184 | tf_op jit(solution)/shard_map/gather | solution.py:365
  16.9 2.2 reshape.469
  19.1 2.8 %copy.53 = bf16[8,2,32,4,256]{4,3,0,1,2:T(4,128)(2,1)} copy(bf16[8,2,32,4,256]{4,3,2,1,0:T(4,128)(2,1)} %reshape.469) | data formatting | bytes 2097152 | tf_op jit(solution)/shard_map/reshape | solution.py:366
  21.9 2.1 reshape.470
  24.1 4.3 %gather_fusion.1 = bf16[32,2,128,256]{3,2,1,0:T(8,128)(2,1)} fusion(bf16[16,2,128,256]{3,2,1,0:T(8,128)(2,1)} %param.15, s32[1024]{0:T(1024)S(1)} %pad_clamp_fusion.2), kind=kCustom, calls=%fused_computation.1 | custom fusion | bytes 8388736 | tf_op jit(solution)/shard_map/gather | solution.py:371
  28.4 5.4 %pad_maximum_fusion = bf16[32,2,160,256]{3,2,1,0:T(8,128)(2,1)} fusion(bf16[32,2,32,256]{3,2,1,0:T(8,128)(2,1)} %reshape.470, bf16[32,2,128,256]{3,2,1,0:T(8,128)(2,1)} %gather_fusion.1), kind=kLoop, calls=%fused_computation.23 | loop fusion | flops 10485760 | bytes 10485760 | tf_op jit(solution)/shard_map/scatter | solution.py:371
  33.8 11.8 %all-to-all-start.1 = ((bf16[32,2,160,256]{3,2,1,0:T(8,128)(2,1)}), bf16[32,2,160,256]{3,2,1,0:T(8,128)(2,1)}, u32[]{:S(2)}, u32[]{:S(2)}) async-start(bf16[32,2,160,256]{3,2,1,0:T(8,128)(2,1)} %pad_maximum_fusion), calls=%async_computation.1 | async-start | bytes 10485760 | tf_op jit(solution)/shard_map/all_to_all | solution.py:372
  47.6 2.8 %convert_reduce_fusion = f32[1024]{0:T(1024)S(1)} fusion(bf16[1024,2048]{1,0:T(8,128)(2,1)} %param.12), kind=kLoop, calls=%fused_computation.18 | loop fusion | flops 4193280 | bytes 4198400 | tf_op jit(solution)/shard_map/reduce_sum | solution.py:306
  50.4 1.2 fusion.3
  51.7 4.0 %fusion.6 = f32[1024,3,256]{0,2,1:T(8,128)S(1)} fusion(bf16[2048,3,256]{2,0,1:T(8,128)(2,1)S(1)} %copy-done, bf16[1024,2048]{1,0:T(8,128)(2,1)S(1)} %copy-done.3, f32[1024]{0:T(1024)S(1)} %add_rsqrt_fusion, f32[1024]{0:T(1024)S(1)} %broadcast_multiply_fusion.1), kind=kOutput, calls=%fused_computation.25 | convolution fusion | flops 3229614080 | bytes 10493952 | tf_op jit(solution)/shard_map/td,dcf->tcf/dot_general | solution.py:310
  55.7 0.9 slice.76
  56.8 0.9 fusion.22
  58.3 1.5 copy.44
  59.8 1.1 fusion.21
  60.9 1.4 copy.45
  62.4 2.2 copy.46
  65.9 1.9 multiply_cosine_fusion
  67.8 3.9 %subtract_convert_fusion = (bf16[1024,2,64]{2,1,0:T(2,128)(2,1)S(1)}, bf16[1024,2,64]{2,1,0:T(2,128)(2,1)S(1)}, bf16[1024,2,64]{2,1,0:T(2,128)(2,1)S(1)}, bf16[1024,2,64]{2,1,0:T(2,128)(2,1)S(1)}) fusion(f32[1024,2,64]{2,1,0:T(2,128)} %copy.46, f32[1024,2,64]{2,1,0:T(2,128)S(1)} %copy.45, f32[1024,64]{1,0:T(8,128)S(1)} %get-tuple-element.70, ...), kind=kLoop, calls=%fused_computation.31 | loop fusion | flops 2097152 | bytes 3670016 | tf_op jit(solution)/shard_map/convert.1
  71.8 3.1 %pad_maximum_fusion.1 = (bf16[1024,2,128]{2,1,0:T(2,128)(2,1)S(1)}, bf16[1024,2,128]{2,1,0:T(2,128)(2,1)S(1)}) fusion(bf16[1024,2,64]{2,1,0:T(2,128)(2,1)S(1)} %get-tuple-element.62, bf16[1024,2,64]{2,1,0:T(2,128)(2,1)S(1)} %get-tuple-element.63, bf16[1024,2,64]{2,1,0:T(2,128)(2,1)S(1)} %get-tuple-element.57, bf16[1024,2,64]{2,1,0:T(2,128)(2,1)S(1)} %get-tuple-element.56), kind=kLoop, calls=%fused_computation.40 | loop fusion | flops 2097152 | bytes 2097152 | tf_op jit(solution)/shard_map/concatenate | solution.py:29
  74.9 0.9 copy.55
  77.9 1.0 copy.47
  82.9 82.7 %all-to-all-done.1.mk_ref.mv_ref = bf16[32,2,160,256]{3,2,1,0:T(8,128)(2,1)} async-done(((bf16[32,2,160,256]{3,2,1,0:T(8,128)(2,1)}), bf16[32,2,160,256]{3,2,1,0:T(8,128)(2,1)}, u32[]{:S(2)}, u32[]{:S(2)}) %all-to-all-start.1) | async-done | bytes 5242912 | tf_op jit(solution)/shard_map/all_to_all | solution.py:372
  165.7 10.2 %copy.39 = bf16[32,2,160,256]{3,1,0,2:T(2,128)(2,1)} copy(bf16[32,2,160,256]{3,2,1,0:T(8,128)(2,1)} %all-to-all-done.1.mk_ref.mv_ref) | data formatting | bytes 10485760 | tf_op jit(solution)/shard_map/all_to_all | solution.py:372
  175.9 3.4 %gather_fusion.3 = bf16[32,2,4,256]{3,1,2,0:T(2,128)(2,1)S(1)} fusion(bf16[32,2,160,256]{3,1,0,2:T(2,128)(2,1)} %copy.39, s32[32]{0:T(128)S(1)} %or_bitcast_fusion), kind=kCustom, calls=%fused_computation.3 | custom fusion | bytes 262656 | tf_op jit(solution)/shard_map/vmap(vmap())/gather | solution.py:384
  180.0 12.4 %shard_map.82 = bf16[32,2,4,256]{3,2,1,0:T(4,128)(2,1)} custom-call(bf16[32,2,4,256]{3,2,1,0:T(4,128)(2,1)} %copy.40.send_ref), custom_call_target="tpu_custom_call" | custom-call | tf_op jit(solution)/shard_map/pallas_call | solution.py:289
  192.4 1.0 copy.41
  194.0 21.5 %shard_map.83 = bf16[1024,256]{1,0:T(8,128)(2,1)} custom-call(s32[1]{0:T(128)} %mul.168.live_ref, s32[1,4096]{1,0:T(1,128)} %bitcast.92, s32[1,128]{1,0:T(1,128)} %broadcast_select_fusion.kpe_ref, bf16[1024,256]{1,0:T(8,128)(2,1)} %bitcast.86, bf16[32,2,160,256]{3,2,1,0:T(8,128)(2,1)} %all-to-all-done.1.mk_ref.mv_ref, ...), custom_call_target="tpu_custom_call" | custom-call | flops 4966055936 | bytes 5898240 | tf_op jit(solution)/shard_map/pallas_call | solution.py:118
  215.5 4.7 %convolution_convert_fusion = bf16[1024,2048]{1,0:T(8,128)(2,1)} fusion(bf16[1024,256]{1,0:T(8,128)(2,1)} %get-tuple-element.75, bf16[256,2048]{1,0:T(8,128)(2,1)} %param.14), kind=kOutput, calls=%fused_computation.28 | convolution fusion | flops 1075838976 | bytes 5767168 | tf_op jit(solution)/shard_map/dot_general | solution.py:446
  220.2 39.4 %reduce-scatter.2.cloned.1.call-done = bf16[128,2048]{1,0:T(8,128)(2,1)} async-done(((bf16[1024,2048]{1,0:T(8,128)(2,1)}), bf16[128,2048]{1,0:T(8,128)(2,1)}) %reduce-scatter.2.cloned.1.call-update) | async-done | bytes 524304 | tf_op jit(solution)/shard_map/reduce_scatter | solution.py:447
  (65 shorter events, 10.8 us)
Async XLA Ops:
  6.5 45.1 %copy-start = (bf16[2048,3,256]{2,0,1:T(8,128)(2,1)S(1)}, bf16[2048,3,256]{2,0,1:T(8,128)(2,1)}, u32[]{:S(2)}) copy-start(bf16[2048,3,256]{2,0,1:T(8,128)(2,1)} %param.13) | copy-start | bytes 9437188
  33.8 12.5 %copy-start.9 = (s32[32]{0:T(128)S(1)}, s32[32]{0:T(128)}, u32[]{:S(2)}) copy-start(s32[32]{0:T(128)} %param.16) | copy-start | bytes 388
  33.8 13.2 %copy-start.10 = (s32[32]{0:T(128)S(1)}, s32[32]{0:T(128)}, u32[]{:S(2)}) copy-start(s32[32]{0:T(128)} %param.19) | copy-start | bytes 388
  33.8 131.9 %all-to-all-start.1 = ((bf16[32,2,160,256]{3,2,1,0:T(8,128)(2,1)}), bf16[32,2,160,256]{3,2,1,0:T(8,128)(2,1)}, u32[]{:S(2)}, u32[]{:S(2)}) async-start(bf16[32,2,160,256]{3,2,1,0:T(8,128)(2,1)} %pad_maximum_fusion), calls=%async_computation.1 | async-start | bytes 10485760 | tf_op jit(solution)/shard_map/all_to_all | solution.py:372
  45.6 214.0 %reduce-scatter.2.cloned.1.call-start = ((), (), s32[]{:S(2)}) async-start(), calls=%async_computation.3 | async-start | bytes 4718592 | tf_op jit(solution)/shard_map/reduce_scatter | solution.py:447
  46.3 4.1 %copy-start.3 = (bf16[1024,2048]{1,0:T(8,128)(2,1)S(1)}, bf16[1024,2048]{1,0:T(8,128)(2,1)}, u32[]{:S(2)}) copy-start(bf16[1024,2048]{1,0:T(8,128)(2,1)} %param.12) | copy-start | bytes 12582916
  67.8 13.6 %copy-start.5 = (s32[32,32,1]{1,2,0:T(1,128)S(1)}, s32[32,32,1]{1,2,0:T(1,128)}, u32[]{:S(2)}) copy-start(s32[32,32,1]{1,2,0:T(1,128)} %param.18) | copy-start | bytes 12292
  71.8 6.1 %copy-start.4 = (bf16[1024,1,256]{0,2,1:T(8,128)(2,1)S(1)}, bf16[1024,1,256]{0,2,1:T(8,128)(2,1)}, u32[]{:S(2)}) copy-start(bf16[1024,1,256]{0,2,1:T(8,128)(2,1)} %slice.76) | copy-start | bytes 1572868
  82.9 111.1 %copy-start.2 = (bf16[16,2,128,256]{3,2,1,0:T(8,128)(2,1)S(1)}, bf16[16,2,128,256]{3,2,1,0:T(8,128)(2,1)}, u32[]{:S(2)}) copy-start(bf16[16,2,128,256]{3,2,1,0:T(8,128)(2,1)} %param.15) | copy-start | bytes 6291460
  82.9 111.1 %copy-start.8 = (s32[32,32]{1,0:T(8,128)S(1)}, s32[32,32]{1,0:T(8,128)}, u32[]{:S(2)}) copy-start(s32[32,32]{1,0:T(8,128)} %param.17) | copy-start | bytes 12292
  215.5 44.2 %copy-start.1 = (bf16[2048,3,256]{2,0,1:T(8,128)(2,1)S(1)}, bf16[2048,3,256]{2,0,1:T(8,128)(2,1)}, u32[]{:S(2)}) copy-start(bf16[2048,3,256]{2,0,1:T(8,128)(2,1)} %param.13) | copy-start | bytes 9437188
Sparse Core Ops, SparseCore 0:
  220.3 39.2 reduce-scatter.1

commit v14 on v13

--- a/solution.py
+++ b/solution.py
@@ -377,11 +377,13 @@
     )
     zero = jnp.zeros_like(src_holder)
     starts = jnp.stack(
-        [src_holder, zero, PAGE + jnp.clip(src_index, 0, RELAY_A - 1) * frag, zero], axis=-1
-    )
+        [src_holder, zero, jnp.clip(src_index, 0, RELAY_A - 1) * frag, zero], axis=-1
+    )
+
+    relayed = incoming[:, :, PAGE:]
 
     def window(start):
-        return lax.dynamic_slice(incoming, tuple(start), (1, 2, frag, width))[0]
+        return lax.dynamic_slice(relayed, tuple(start), (1, 2, frag, width))[0]
 
     extra = jax.vmap(jax.vmap(window))(starts)
     extra = extra.transpose(0, 2, 1, 3, 4).reshape(rows, 2, RELAY_B * frag, width)

time: 271 us -> 273 us (level)
  Pallas kernels: 33.8 us -> 46.2 us
  local copies, waits for them, and re-layouts: 43.7 us -> 36.8 us
    pallas_call x1, Pallas kernels: 21.5 us -> 33.8 us  [attend(): pl.pallas_call(attend_kernel, grid_spec=grid_spec, out_shape=jax.ShapeDty...]
    all_to_all x1 -> x0, local copies, waits for them, and re-layouts: 10.2 us -> none  [exchange_relay(): lax.all_to_all(outgoing, 'req', split_axis=0, concat_axis=0, tiled=True)]
    slice x0 -> x2, local copies, waits for them, and re-layouts: none -> 3.43 us  [exchange_relay(): relayed = incoming[:, :, PAGE:]]
where the time goes in v14:
time: 273 us; the launch traced here: 271 us
  waiting for transfers between devices  122 us (45%)
  Pallas kernels  46.2 us (17%)
  local copies, waits for them, and re-layouts  36.8 us (13%)
  other arithmetic  28.1 us (10%)
  between operations  17.7 us (6%)
  starting transfers between devices  11.8 us (4%)
  matrix products  8.76 us (3%)
    all_to_all x1, waiting for transfers between devices, exchange_relay(): lax.all_to_all(outgoing, 'req', split_axis=0, concat_axis=0, tiled=True)  82.2 us
    reduce_scatter x1, waiting for transfers between devices, body(): lax.psum_scatter(head_term.astype(jnp.bfloat16), 'tp', scatter_dimension=...  39.4 us
    pallas_call x1, Pallas kernels, attend(): pl.pallas_call(attend_kernel, grid_spec=grid_spec, out_shape=jax.ShapeDty...  33.8 us
    pallas_call x1, Pallas kernels, swap_pieces(): pl.pallas_call(swap_kernel, out_shape=jax.ShapeDtypeStruct(pieces.shape,...  12.4 us
    all_to_all x1, starting transfers between devices, exchange_relay(): lax.all_to_all(outgoing, 'req', split_axis=0, concat_axis=0, tiled=True)  11.8 us
    unnamed x25, local copies, waits for them, and re-layouts  8.68 us
  transfers between devices with their start and end apart: 2, of which 2 were waited for; matrix products, arithmetic and copies ran while one was open for 12% of the time, Pallas kernels for 0%

profile of v14, /device:TPU:2, one launch (start us, length us, event | category | flops | bytes accessed | tf_op | source)
XLA Modules:
  0.0 271.0 jit_solution(11865021314917736685)
XLA Ops:
  6.5 1.7 convert_reduce_fusion.1
  10.6 1.1 select_reduce_fusion.2
  11.8 1.5 select_reduce_fusion.4
  13.7 3.2 %gather_fusion.2 = bf16[8,2,128,256]{3,2,1,0:T(8,128)(2,1)} fusion(bf16[16,2,128,256]{3,2,1,0:T(8,128)(2,1)} %param.15, s32[1024]{0:T(1024)S(1)} %pad_clamp_fusion.1), kind=kCustom, calls=%fused_computation.2 | custom fusion | bytes 2097184 | tf_op jit(solution)/shard_map/gather | solution.py:365
  16.9 2.2 reshape.461
  19.1 2.8 %copy.53 = bf16[8,2,32,4,256]{4,3,0,1,2:T(4,128)(2,1)} copy(bf16[8,2,32,4,256]{4,3,2,1,0:T(4,128)(2,1)} %reshape.461) | data formatting | bytes 2097152 | tf_op jit(solution)/shard_map/reshape | solution.py:366
  21.9 2.1 reshape.462
  24.1 4.3 %gather_fusion.1 = bf16[32,2,128,256]{3,2,1,0:T(8,128)(2,1)} fusion(bf16[16,2,128,256]{3,2,1,0:T(8,128)(2,1)} %param.15, s32[1024]{0:T(1024)S(1)} %pad_clamp_fusion.2), kind=kCustom, calls=%fused_computation.1 | custom fusion | bytes 8388736 | tf_op jit(solution)/shard_map/gather | solution.py:371
  28.4 5.4 %pad_maximum_fusion = bf16[32,2,160,256]{3,2,1,0:T(8,128)(2,1)} fusion(bf16[32,2,32,256]{3,2,1,0:T(8,128)(2,1)} %reshape.462, bf16[32,2,128,256]{3,2,1,0:T(8,128)(2,1)} %gather_fusion.1), kind=kLoop, calls=%fused_computation.23 | loop fusion | flops 10485760 | bytes 10485760 | tf_op jit(solution)/shard_map/scatter | solution.py:371
  33.8 11.8 %all-to-all-start.1 = ((bf16[32,2,160,256]{3,2,1,0:T(8,128)(2,1)}), bf16[32,2,160,256]{3,2,1,0:T(8,128)(2,1)}, u32[]{:S(2)}, u32[]{:S(2)}) async-start(bf16[32,2,160,256]{3,2,1,0:T(8,128)(2,1)} %pad_maximum_fusion), calls=%async_computation.1 | async-start | bytes 10485760 | tf_op jit(solution)/shard_map/all_to_all | solution.py:372
  47.2 2.8 %convert_reduce_fusion = f32[1024]{0:T(1024)S(1)} fusion(bf16[1024,2048]{1,0:T(8,128)(2,1)} %param.12), kind=kLoop, calls=%fused_computation.18 | loop fusion | flops 4193280 | bytes 4198400 | tf_op jit(solution)/shard_map/reduce_sum | solution.py:306
  50.0 1.2 fusion.3
  51.3 4.0 %fusion.6 = f32[1024,3,256]{0,2,1:T(8,128)S(1)} fusion(bf16[2048,3,256]{2,0,1:T(8,128)(2,1)S(1)} %copy-done, bf16[1024,2048]{1,0:T(8,128)(2,1)S(1)} %copy-done.3, f32[1024]{0:T(1024)S(1)} %add_rsqrt_fusion, f32[1024]{0:T(1024)S(1)} %broadcast_multiply_fusion.1), kind=kOutput, calls=%fused_computation.25 | convolution fusion | flops 3229614080 | bytes 10493952 | tf_op jit(solution)/shard_map/td,dcf->tcf/dot_general | solution.py:310
  56.4 0.9 fusion.22
  58.1 1.5 copy.44
  59.6 1.1 fusion.21
  60.7 1.4 copy.45
  62.2 2.2 copy.46
  65.7 1.9 multiply_cosine_fusion
  67.6 3.9 %subtract_convert_fusion = (bf16[1024,2,64]{2,1,0:T(2,128)(2,1)S(1)}, bf16[1024,2,64]{2,1,0:T(2,128)(2,1)S(1)}, bf16[1024,2,64]{2,1,0:T(2,128)(2,1)S(1)}, bf16[1024,2,64]{2,1,0:T(2,128)(2,1)S(1)}) fusion(f32[1024,2,64]{2,1,0:T(2,128)} %copy.46, f32[1024,2,64]{2,1,0:T(2,128)S(1)} %copy.45, f32[1024,64]{1,0:T(8,128)S(1)} %get-tuple-element.70, ...), kind=kLoop, calls=%fused_computation.31 | loop fusion | flops 2097152 | bytes 3670016 | tf_op jit(solution)/shard_map/convert.1
  71.6 2.9 %pad_maximum_fusion.1 = (bf16[1024,2,128]{2,1,0:T(2,128)(2,1)S(1)}, bf16[1024,2,128]{2,1,0:T(2,128)(2,1)S(1)}) fusion(bf16[1024,2,64]{2,1,0:T(2,128)(2,1)S(1)} %get-tuple-element.62, bf16[1024,2,64]{2,1,0:T(2,128)(2,1)S(1)} %get-tuple-element.63, bf16[1024,2,64]{2,1,0:T(2,128)(2,1)S(1)} %get-tuple-element.57, bf16[1024,2,64]{2,1,0:T(2,128)(2,1)S(1)} %get-tuple-element.56), kind=kLoop, calls=%fused_computation.40 | loop fusion | flops 2097152 | bytes 2097152 | tf_op jit(solution)/shard_map/concatenate | solution.py:29
  75.4 0.9 copy.55
  78.3 1.0 copy.47
  83.5 82.2 %all-to-all-done.1.mk_ref.mv_ref = bf16[32,2,160,256]{3,2,1,0:T(8,128)(2,1)} async-done(((bf16[32,2,160,256]{3,2,1,0:T(8,128)(2,1)}), bf16[32,2,160,256]{3,2,1,0:T(8,128)(2,1)}, u32[]{:S(2)}, u32[]{:S(2)}) %all-to-all-start.1) | async-done | bytes 5242912 | tf_op jit(solution)/shard_map/all_to_all | solution.py:372
  165.7 1.3 slice.81
  167.0 2.1 copy.39
  169.1 2.1 gather_fusion.3
  171.9 12.4 %shard_map.82 = bf16[32,2,4,256]{3,2,1,0:T(4,128)(2,1)} custom-call(bf16[32,2,4,256]{3,2,1,0:T(4,128)(2,1)} %copy.40.send_ref), custom_call_target="tpu_custom_call" | custom-call | tf_op jit(solution)/shard_map/pallas_call | solution.py:289
  184.3 1.0 copy.41
  186.0 33.8 %shard_map.83 = bf16[1024,256]{1,0:T(8,128)(2,1)} custom-call(s32[1]{0:T(128)} %mul.173.live_ref, s32[1,4096]{1,0:T(1,128)} %bitcast.90, s32[1,128]{1,0:T(1,128)} %broadcast_select_fusion.kpe_ref, bf16[1024,256]{1,0:T(8,128)(2,1)} %bitcast.84, bf16[32,2,160,256]{3,2,1,0:T(8,128)(2,1)} %all-to-all-done.1.mk_ref.mv_ref, ...), custom_call_target="tpu_custom_call" | custom-call | flops 4966055936 | bytes 5898240 | tf_op jit(solution)/shard_map/pallas_call | solution.py:118
  219.8 4.7 %convolution_convert_fusion = bf16[1024,2048]{1,0:T(8,128)(2,1)} fusion(bf16[1024,256]{1,0:T(8,128)(2,1)} %get-tuple-element.75, bf16[256,2048]{1,0:T(8,128)(2,1)} %param.14), kind=kOutput, calls=%fused_computation.28 | convolution fusion | flops 1075838976 | bytes 5767168 | tf_op jit(solution)/shard_map/dot_general | solution.py:448
  224.5 39.4 %reduce-scatter.2.cloned.1.call-done = bf16[128,2048]{1,0:T(8,128)(2,1)} async-done(((bf16[1024,2048]{1,0:T(8,128)(2,1)}), bf16[128,2048]{1,0:T(8,128)(2,1)}) %reduce-scatter.2.cloned.1.call-update) | async-done | bytes 524304 | tf_op jit(solution)/shard_map/reduce_scatter | solution.py:449
  (66 shorter events, 12.3 us)
Async XLA Ops:
  6.5 44.7 %copy-start = (bf16[2048,3,256]{2,0,1:T(8,128)(2,1)S(1)}, bf16[2048,3,256]{2,0,1:T(8,128)(2,1)}, u32[]{:S(2)}) copy-start(bf16[2048,3,256]{2,0,1:T(8,128)(2,1)} %param.13) | copy-start | bytes 9437188
  33.8 12.0 %copy-start.10 = (s32[32]{0:T(128)S(1)}, s32[32]{0:T(128)}, u32[]{:S(2)}) copy-start(s32[32]{0:T(128)} %param.16) | copy-start | bytes 388
  33.8 12.7 %copy-start.11 = (s32[32]{0:T(128)S(1)}, s32[32]{0:T(128)}, u32[]{:S(2)}) copy-start(s32[32]{0:T(128)} %param.19) | copy-start | bytes 388
  33.8 131.9 %all-to-all-start.1 = ((bf16[32,2,160,256]{3,2,1,0:T(8,128)(2,1)}), bf16[32,2,160,256]{3,2,1,0:T(8,128)(2,1)}, u32[]{:S(2)}, u32[]{:S(2)}) async-start(bf16[32,2,160,256]{3,2,1,0:T(8,128)(2,1)} %pad_maximum_fusion), calls=%async_computation.1 | async-start | bytes 10485760 | tf_op jit(solution)/shard_map/all_to_all | solution.py:372
  45.6 218.4 %reduce-scatter.2.cloned.1.call-start = ((), (), s32[]{:S(2)}) async-start(), calls=%async_computation.3 | async-start | bytes 4718592 | tf_op jit(solution)/shard_map/reduce_scatter | solution.py:449
  45.8 4.1 %copy-start.3 = (bf16[1024,2048]{1,0:T(8,128)(2,1)S(1)}, bf16[1024,2048]{1,0:T(8,128)(2,1)}, u32[]{:S(2)}) copy-start(bf16[1024,2048]{1,0:T(8,128)(2,1)} %param.12) | copy-start | bytes 12582916
  71.6 6.8 %copy-start.4 = (bf16[1024,1,256]{0,2,1:T(8,128)(2,1)S(1)}, bf16[1024,1,256]{0,2,1:T(8,128)(2,1)}, u32[]{:S(2)}) copy-start(bf16[1024,1,256]{0,2,1:T(8,128)(2,1)} %slice.80) | copy-start | bytes 1572868
  71.6 10.3 %copy-start.5 = (s32[32,32,1]{1,2,0:T(1,128)S(1)}, s32[32,32,1]{1,2,0:T(1,128)}, u32[]{:S(2)}) copy-start(s32[32,32,1]{1,2,0:T(1,128)} %param.18) | copy-start | bytes 12292
  74.5 111.5 %copy-start.2 = (bf16[16,2,128,256]{3,2,1,0:T(8,128)(2,1)S(1)}, bf16[16,2,128,256]{3,2,1,0:T(8,128)(2,1)}, u32[]{:S(2)}) copy-start(bf16[16,2,128,256]{3,2,1,0:T(8,128)(2,1)} %param.15) | copy-start | bytes 6291460
  74.5 111.5 %copy-start.9 = (s32[32,32]{1,0:T(8,128)S(1)}, s32[32,32]{1,0:T(8,128)}, u32[]{:S(2)}) copy-start(s32[32,32]{1,0:T(8,128)} %param.17) | copy-start | bytes 12292
  219.8 44.2 %copy-start.1 = (bf16[2048,3,256]{2,0,1:T(8,128)(2,1)S(1)}, bf16[2048,3,256]{2,0,1:T(8,128)(2,1)}, u32[]{:S(2)}) copy-start(bf16[2048,3,256]{2,0,1:T(8,128)(2,1)} %param.13) | copy-start | bytes 9437188
Sparse Core Ops, SparseCore 0:
  224.7 39.2 reduce-scatter.1
